TPU v7x, 32 devices: a whole 2x2x4 slice. The times are simulated.
32 devices in a mesh: fsdp: 16 (over z, y, core), tp: 2 (over x).
Axes of the slice: x: 2, y: 2, z: 4, core: 2. Of those that a mesh axis runs over, the one named last changes fastest.
Arguments:
- frames: bfloat16 [16, 1504, 1280], P('fsdp', 'tp'), may hold values from -6 to 6
- out_grad: bfloat16 [16, 1504, 1280], P('fsdp', 'tp'), may hold values from -6 to 6
- clip_lengths: int32 [16], replicated, may hold values from 1 to 1504, 18048 in all
- clip_order: int32 [16], replicated, may hold values from 0 to 15, each once
- w_query: bfloat16 [1280, 1280], P('fsdp', 'tp'), may hold values from -0.25 to 0.25
- w_key: bfloat16 [1280, 1280], P('fsdp', 'tp'), may hold values from -0.25 to 0.25
- w_value: bfloat16 [1280, 1280], P('fsdp', 'tp'), may hold values from -0.15625 to 0.15625
- b_query: bfloat16 [1280], P(('tp', 'fsdp')), may hold values from -3 to 3
- b_value: bfloat16 [1280], P(('tp', 'fsdp')), may hold values from -0.1796875 to 0.1796875
- w_out: bfloat16 [1280, 1280], P('tp', 'fsdp'), may hold values from -1.75 to 1.75
- b_out: bfloat16 [1280], P(('fsdp', 'tp')), may hold values from -3 to 3
- w_expand: bfloat16 [1280, 5120], P('fsdp', 'tp'), may hold values from -0.15625 to 0.15625
- b_expand: bfloat16 [5120], P(('tp', 'fsdp')), may hold values from -3 to 3
- w_reduce: bfloat16 [5120, 1280], P('tp', 'fsdp'), may hold values from -0.078125 to 0.078125
- b_reduce: bfloat16 [1280], P(('fsdp', 'tp')), may hold values from -3 to 3
- first_gain: bfloat16 [1280], P(('fsdp', 'tp')), may hold values from 0.099609375 to 1.8984375
- first_shift: bfloat16 [1280], P(('fsdp', 'tp')), may hold values from -2 to 2
- second_gain: bfloat16 [1280], P(('fsdp', 'tp')), may hold values from 0.099609375 to 1.8984375
- second_shift: bfloat16 [1280], P(('fsdp', 'tp')), may hold values from -2 to 2
Outputs:
- out_frames: bfloat16 [16, 1504, 1280], P('fsdp', 'tp')
- frames_grad: bfloat16 [16, 1504, 1280], P('fsdp', 'tp')
- w_query_grad: float32 [1280, 1280], P('fsdp', 'tp')
- w_key_grad: float32 [1280, 1280], P('fsdp', 'tp')
- w_value_grad: float32 [1280, 1280], P('fsdp', 'tp')
- b_query_grad: float32 [1280], P(('tp', 'fsdp'))
- b_value_grad: float32 [1280], P(('tp', 'fsdp'))
- w_out_grad: float32 [1280, 1280], P('tp', 'fsdp')
- b_out_grad: float32 [1280], P(('fsdp', 'tp'))
- w_expand_grad: float32 [1280, 5120], P('fsdp', 'tp')
- b_expand_grad: float32 [5120], P(('tp', 'fsdp'))
- w_reduce_grad: float32 [5120, 1280], P('tp', 'fsdp')
- b_reduce_grad: float32 [1280], P(('fsdp', 'tp'))
- first_gain_grad: float32 [1280], P(('fsdp', 'tp'))
- first_shift_grad: float32 [1280], P(('fsdp', 'tp'))
- second_gain_grad: float32 [1280], P(('fsdp', 'tp'))
- second_shift_grad: float32 [1280], P(('fsdp', 'tp'))
Inputs may be any that keep to these rules, and one draw needn't show every extreme that they name: `clip_lengths`: frames of each clip that keys may come from; they sum to 18048. `clip_order`: each clip stands in exactly one slot.
All inputs are finite; a program needn't handle non-finite values.
Results may differ from a plain program's by a relative error of at most 0.02.
Values may be sent and summed in bfloat16 or wider, within the bound.
No kernel may reach another device: no remote copies, remote signals or barrier semaphores. Data moves between devices by JAX's collectives and lax.ppermute only.
A program may use at most 448 MiB of HBM per device.

v0:
```python
import jax
import jax.numpy as jnp
from jax import lax
from jax.sharding import PartitionSpec as P

HD = 80


EPSILON = 1e-05
MASKED = -1000000000.0


def layer_norm(features, norm_gain, norm_shift):
    row_mean = jnp.mean(features, axis=-1, keepdims=True)
    centred = features - row_mean
    row_var = jnp.mean(centred * centred, axis=-1, keepdims=True)
    inverse = lax.rsqrt(row_var + EPSILON)
    normed = centred * inverse
    return (normed * norm_gain + norm_shift, normed, inverse)


def norm_back(upstream, normed, inverse, norm_gain):
    tilted = upstream * norm_gain
    return inverse * (
        tilted
        - jnp.mean(tilted, axis=-1, keepdims=True)
        - normed * jnp.mean(tilted * normed, axis=-1, keepdims=True)
    )


def gelu_exact(inputs):
    return jax.nn.gelu(inputs, approximate=False)


def masked_scores(queries, key_rows, length):
    scores = jnp.einsum("qhe,khe->hqk", queries, key_rows, preferred_element_type=jnp.float32)
    allowed = jnp.arange(scores.shape[-1]) < length
    return jnp.where(allowed[None, None, :], scores, MASKED)


def attend(inputs):
    queries, key_rows, value_rows, length = inputs
    scores = masked_scores(queries, key_rows, length)
    row_top = jnp.max(scores, axis=-1, keepdims=True)
    raised = jnp.exp(scores - row_top)
    row_sum = jnp.sum(raised, axis=-1, keepdims=True)
    weights = (raised / row_sum).astype(jnp.bfloat16)
    context = jnp.einsum("hqk,khe->qhe", weights, value_rows, preferred_element_type=jnp.float32)
    return (context.astype(jnp.bfloat16), row_top[..., 0] + jnp.log(row_sum[..., 0]))


def attend_back(inputs):
    queries, key_rows, value_rows, length, log_total, context_grad = inputs
    scores = masked_scores(queries, key_rows, length)
    probs = jnp.exp(scores - log_total[..., None])
    weights = probs.astype(jnp.bfloat16)
    value_grad = jnp.einsum(
        "hqk,qhe->khe", weights, context_grad, preferred_element_type=jnp.float32
    )
    weight_grad = jnp.einsum(
        "qhe,khe->hqk", context_grad, value_rows, preferred_element_type=jnp.float32
    )
    row_inner = jnp.sum(weight_grad * probs, axis=-1, keepdims=True)
    score_grad = (probs * (weight_grad - row_inner)).astype(jnp.bfloat16)
    query_grad = jnp.einsum(
        "hqk,khe->qhe", score_grad, key_rows, preferred_element_type=jnp.float32
    )
    key_grad = jnp.einsum("hqk,qhe->khe", score_grad, queries, preferred_element_type=jnp.float32)
    return (
        query_grad.astype(jnp.bfloat16),
        key_grad.astype(jnp.bfloat16),
        value_grad.astype(jnp.bfloat16),
    )


def gather_inward(w_query, w_key, w_value, b_query, b_value, w_expand, b_expand):
    return (
        lax.all_gather(w_query, "fsdp", axis=0, tiled=True),
        lax.all_gather(w_key, "fsdp", axis=0, tiled=True),
        lax.all_gather(w_value, "fsdp", axis=0, tiled=True),
        lax.all_gather(b_query, "fsdp", axis=0, tiled=True),
        lax.all_gather(b_value, "fsdp", axis=0, tiled=True),
        lax.all_gather(w_expand, "fsdp", axis=0, tiled=True),
        lax.all_gather(b_expand, "fsdp", axis=0, tiled=True),
    )


def gather_outward(w_out, w_reduce):
    return (
        lax.all_gather(w_out, "fsdp", axis=1, tiled=True),
        lax.all_gather(w_reduce, "fsdp", axis=1, tiled=True),
    )


def per_device(
    frames,
    out_grad,
    clip_lengths,
    clip_order,
    w_query,
    w_key,
    w_value,
    b_query,
    b_value,
    w_out,
    b_out,
    w_expand,
    b_expand,
    w_reduce,
    b_reduce,
    first_gain,
    first_shift,
    second_gain,
    second_shift,
):
    per_group = frames.shape[0]
    clip_count = clip_order.shape[0]
    slot_ids = lax.axis_index("fsdp") * per_group + jnp.arange(per_group, dtype=jnp.int32)
    every_clip = jnp.arange(clip_count, dtype=jnp.int32)
    clip_ids = jnp.sum(
        jnp.where(every_clip[None, :] == slot_ids[:, None], clip_order[None, :], 0), axis=1
    )
    lengths = jnp.sum(
        jnp.where(every_clip[None, :] == clip_ids[:, None], clip_lengths[None, :], 0), axis=1
    )
    norm_params = (
        lax.all_gather(first_gain, ("fsdp", "tp"), axis=0, tiled=True),
        lax.all_gather(first_shift, ("fsdp", "tp"), axis=0, tiled=True),
        lax.all_gather(second_gain, ("fsdp", "tp"), axis=0, tiled=True),
        lax.all_gather(second_shift, ("fsdp", "tp"), axis=0, tiled=True),
        lax.all_gather(b_out, ("fsdp", "tp"), axis=0, tiled=True),
        lax.all_gather(b_reduce, ("fsdp", "tp"), axis=0, tiled=True),
    )
    gain_one, shift_one, gain_two, shift_two, out_bias, reduce_bias = [
        tensor.astype(jnp.float32) for tensor in norm_params
    ]
    wq_all, wk_all, wv_all, bq_all, bv_all, we_all, be_all = gather_inward(
        w_query, w_key, w_value, b_query, b_value, w_expand, b_expand
    )
    wo_all, wr_all = gather_outward(w_out, w_reduce)
    q_factor = HD ** (-0.5)
    frames_wide = frames.astype(jnp.float32)
    norm_one, normed_one, inverse_one = layer_norm(frames_wide, gain_one, shift_one)
    first_rows = lax.all_gather(norm_one.astype(jnp.bfloat16), "tp", axis=1, tiled=True)
    seq_len = first_rows.shape[1]
    queries = (
        (
            jnp.einsum("csd,de->cse", first_rows, wq_all, preferred_element_type=jnp.float32)
            + bq_all.astype(jnp.float32)
        )
        * q_factor
    ).astype(jnp.bfloat16)
    keys = jnp.einsum("csd,de->cse", first_rows, wk_all, preferred_element_type=jnp.float32).astype(
        jnp.bfloat16
    )
    values = (
        jnp.einsum("csd,de->cse", first_rows, wv_all, preferred_element_type=jnp.float32)
        + bv_all.astype(jnp.float32)
    ).astype(jnp.bfloat16)
    head_shape = (per_group, seq_len, -1, HD)
    query_heads = queries.reshape(head_shape)
    key_heads = keys.reshape(head_shape)
    value_heads = values.reshape(head_shape)
    context, log_total = lax.map(attend, (query_heads, key_heads, value_heads, lengths))
    context_flat = context.reshape(per_group, seq_len, -1)
    attn_terms = jnp.einsum("cse,ed->csd", context_flat, wo_all, preferred_element_type=jnp.float32)
    attn_part = lax.psum_scatter(
        attn_terms.astype(jnp.bfloat16), "tp", scatter_dimension=1, tiled=True
    ).astype(jnp.float32)
    middle = frames_wide + attn_part + out_bias
    norm_two, normed_two, inverse_two = layer_norm(middle, gain_two, shift_two)
    second_rows = lax.all_gather(norm_two.astype(jnp.bfloat16), "tp", axis=1, tiled=True)
    expanded = jnp.einsum(
        "csd,df->csf", second_rows, we_all, preferred_element_type=jnp.float32
    ) + be_all.astype(jnp.float32)
    activated, gelu_pull = jax.vjp(gelu_exact, expanded)
    hidden = activated.astype(jnp.bfloat16)
    mlp_terms = jnp.einsum("csf,fd->csd", hidden, wr_all, preferred_element_type=jnp.float32)
    out_frames = (
        middle
        + lax.psum_scatter(
            mlp_terms.astype(jnp.bfloat16), "tp", scatter_dimension=1, tiled=True
        ).astype(jnp.float32)
        + reduce_bias
    ).astype(jnp.bfloat16)
    wq_all, wk_all, wv_all, bq_all, bv_all, we_all, be_all = gather_inward(
        w_query, w_key, w_value, b_query, b_value, w_expand, b_expand
    )
    wo_all, wr_all = gather_outward(w_out, w_reduce)
    grad_wide = out_grad.astype(jnp.float32)
    grad_rows = lax.all_gather(out_grad, "tp", axis=1, tiled=True)
    w_reduce_grad = jnp.einsum("csf,csd->fd", hidden, grad_rows, preferred_element_type=jnp.float32)
    hidden_grad = jnp.einsum("csd,fd->csf", grad_rows, wr_all, preferred_element_type=jnp.float32)
    expanded_grad = gelu_pull(hidden_grad)[0].astype(jnp.bfloat16)
    b_expand_grad = jnp.sum(expanded_grad.astype(jnp.float32), axis=(0, 1))
    w_expand_grad = jnp.einsum(
        "csd,csf->df", second_rows, expanded_grad, preferred_element_type=jnp.float32
    )
    second_terms = jnp.einsum(
        "csf,df->csd", expanded_grad, we_all, preferred_element_type=jnp.float32
    )
    second_grad = lax.psum_scatter(
        second_terms.astype(jnp.bfloat16), "tp", scatter_dimension=1, tiled=True
    ).astype(jnp.float32)
    second_gain_grad = jnp.sum(second_grad * normed_two, axis=(0, 1))
    second_shift_grad = jnp.sum(second_grad, axis=(0, 1))
    middle_grad = grad_wide + norm_back(second_grad, normed_two, inverse_two, gain_two)
    branch_grad = middle_grad.astype(jnp.bfloat16)
    b_out_grad = jnp.sum(branch_grad.astype(jnp.float32), axis=(0, 1))
    b_reduce_grad = jnp.sum(grad_wide, axis=(0, 1))
    branch_rows = lax.all_gather(branch_grad, "tp", axis=1, tiled=True)
    w_out_grad = jnp.einsum(
        "cse,csd->ed", context_flat, branch_rows, preferred_element_type=jnp.float32
    )
    context_grad = jnp.einsum(
        "csd,ed->cse", branch_rows, wo_all, preferred_element_type=jnp.float32
    ).astype(jnp.bfloat16)
    query_grad, key_grad, value_grad = lax.map(
        attend_back,
        (query_heads, key_heads, value_heads, lengths, log_total, context_grad.reshape(head_shape)),
    )
    query_grad = query_grad.reshape(per_group, seq_len, -1)
    key_grad = key_grad.reshape(per_group, seq_len, -1)
    value_grad = value_grad.reshape(per_group, seq_len, -1)
    w_query_grad = (
        jnp.einsum("csd,cse->de", first_rows, query_grad, preferred_element_type=jnp.float32)
        * q_factor
    )
    b_query_grad = jnp.sum(query_grad.astype(jnp.float32), axis=(0, 1)) * q_factor
    w_key_grad = jnp.einsum("csd,cse->de", first_rows, key_grad, preferred_element_type=jnp.float32)
    w_value_grad = jnp.einsum(
        "csd,cse->de", first_rows, value_grad, preferred_element_type=jnp.float32
    )
    b_value_grad = jnp.sum(value_grad.astype(jnp.float32), axis=(0, 1))
    first_terms = (
        jnp.einsum("cse,de->csd", query_grad, wq_all, preferred_element_type=jnp.float32) * q_factor
        + jnp.einsum("cse,de->csd", key_grad, wk_all, preferred_element_type=jnp.float32)
        + jnp.einsum("cse,de->csd", value_grad, wv_all, preferred_element_type=jnp.float32)
    )
    first_grad = lax.psum_scatter(
        first_terms.astype(jnp.bfloat16), "tp", scatter_dimension=1, tiled=True
    ).astype(jnp.float32)
    first_gain_grad = jnp.sum(first_grad * normed_one, axis=(0, 1))
    first_shift_grad = jnp.sum(first_grad, axis=(0, 1))
    frames_grad = (middle_grad + norm_back(first_grad, normed_one, inverse_one, gain_one)).astype(
        jnp.bfloat16
    )
    inward_grads = (
        lax.psum_scatter(
            w_query_grad.astype(jnp.bfloat16), "fsdp", scatter_dimension=0, tiled=True
        ).astype(jnp.float32),
        lax.psum_scatter(
            w_key_grad.astype(jnp.bfloat16), "fsdp", scatter_dimension=0, tiled=True
        ).astype(jnp.float32),
        lax.psum_scatter(
            w_value_grad.astype(jnp.bfloat16), "fsdp", scatter_dimension=0, tiled=True
        ).astype(jnp.float32),
        lax.psum_scatter(
            b_query_grad.astype(jnp.bfloat16), "fsdp", scatter_dimension=0, tiled=True
        ).astype(jnp.float32),
        lax.psum_scatter(
            b_value_grad.astype(jnp.bfloat16), "fsdp", scatter_dimension=0, tiled=True
        ).astype(jnp.float32),
        lax.psum_scatter(
            w_expand_grad.astype(jnp.bfloat16), "fsdp", scatter_dimension=0, tiled=True
        ).astype(jnp.float32),
        lax.psum_scatter(
            b_expand_grad.astype(jnp.bfloat16), "fsdp", scatter_dimension=0, tiled=True
        ).astype(jnp.float32),
    )
    outward_grads = (
        lax.psum_scatter(
            w_out_grad.astype(jnp.bfloat16), "fsdp", scatter_dimension=1, tiled=True
        ).astype(jnp.float32),
        lax.psum_scatter(
            w_reduce_grad.astype(jnp.bfloat16), "fsdp", scatter_dimension=1, tiled=True
        ).astype(jnp.float32),
    )
    small_grads = (
        lax.psum_scatter(first_gain_grad, ("fsdp", "tp"), scatter_dimension=0, tiled=True),
        lax.psum_scatter(first_shift_grad, ("fsdp", "tp"), scatter_dimension=0, tiled=True),
        lax.psum_scatter(second_gain_grad, ("fsdp", "tp"), scatter_dimension=0, tiled=True),
        lax.psum_scatter(second_shift_grad, ("fsdp", "tp"), scatter_dimension=0, tiled=True),
        lax.psum_scatter(b_out_grad, ("fsdp", "tp"), scatter_dimension=0, tiled=True),
        lax.psum_scatter(b_reduce_grad, ("fsdp", "tp"), scatter_dimension=0, tiled=True),
    )
    return (
        out_frames,
        frames_grad,
        inward_grads[0],
        inward_grads[1],
        inward_grads[2],
        inward_grads[3],
        inward_grads[4],
        outward_grads[0],
        small_grads[4],
        inward_grads[5],
        inward_grads[6],
        outward_grads[1],
        small_grads[5],
        small_grads[0],
        small_grads[1],
        small_grads[2],
        small_grads[3],
    )


def solution(mesh):
    return jax.shard_map(
        per_device,
        mesh=mesh,
        in_specs=(
            P("fsdp", "tp", None),
            P("fsdp", "tp", None),
            P(),
            P(),
            P("fsdp", "tp"),
            P("fsdp", "tp"),
            P("fsdp", "tp"),
            P(("tp", "fsdp")),
            P(("tp", "fsdp")),
            P("tp", "fsdp"),
            P(("fsdp", "tp")),
            P("fsdp", "tp"),
            P(("tp", "fsdp")),
            P("tp", "fsdp"),
            P(("fsdp", "tp")),
            P(("fsdp", "tp")),
            P(("fsdp", "tp")),
            P(("fsdp", "tp")),
            P(("fsdp", "tp")),
        ),
        out_specs=(
            P("fsdp", "tp", None),
            P("fsdp", "tp", None),
            P("fsdp", "tp"),
            P("fsdp", "tp"),
            P("fsdp", "tp"),
            P(("tp", "fsdp")),
            P(("tp", "fsdp")),
            P("tp", "fsdp"),
            P(("fsdp", "tp")),
            P("fsdp", "tp"),
            P(("tp", "fsdp")),
            P("tp", "fsdp"),
            P(("fsdp", "tp")),
            P(("fsdp", "tp")),
            P(("fsdp", "tp")),
            P(("fsdp", "tp")),
            P(("fsdp", "tp")),
        ),
        check_vma=False,
    )
```

profile of v0, /device:TPU:0, one launch (start us, length us, event | category | flops | bytes accessed | tf_op | source)
XLA Modules:
  0.0 1336.5 jit_solution(3240912666753867138)
XLA Ops:
  13.1 43.0 %all-reduce.19 = (bf16[1280]{0:T(1024)(128)(2,1)}, bf16[1280]{0:T(1024)(128)(2,1)}, bf16[1280]{0:T(1024)(128)(2,1)}, bf16[1280]{0:T(1024)(128)(2,1)S(1)}, bf16[1...) all-reduce(bf16[1280]{0:T(1024)(128)(2,1)S(1)} %dynamic-update-slice, ...), channel_id=1, replica_groups=mesh['fsdp'=16,'tp'=2] {'fsdp','tp'}, use_global_device_ids=true, to_apply=%add.6 | all-reduce | flops 7680 | bytes 30720
  70.1 59.8 %all-reduce.21 = (bf16[640]{0:T(1024)(128)(2,1)S(1)}, bf16[640]{0:T(1024)(128)(2,1)S(1)}, bf16[2560]{0:T(1024)(128)(2,1)}) all-reduce(bf16[640]{0:T(1024)(128)(2,1)S(1)} %dynamic-update-slice.2, bf16[640]{0:T(1024)(128)(2,1)S(1)} %dynamic-update-slice.3, ...), channel_id=1, replica_groups=mesh['fsdp'=16,'tp'=2] {'fsdp'}, use_global_device_ids=true, to_apply=%add.2 | all-reduce | flops 3840 | bytes 15360
  139.6 18.5 %all-gather.13.cloned.1.call-done = bf16[1280,640]{1,0:T(8,128)(2,1)} async-done(((bf16[80,640]{1,0:T(8,128)(2,1)}), bf16[1280,640]{1,0:T(8,128)(2,1)}) %all-gather.13.cloned.1.call-update) | async-done | bytes 1638416 | tf_op jit(solution)/shard_map/all_gather | solution.py:80
  169.1 29.9 %all-gather.17.cloned.1.call-done = bf16[1280,640]{1,0:T(8,128)(2,1)} async-done(((bf16[80,640]{1,0:T(8,128)(2,1)}), bf16[1280,640]{1,0:T(8,128)(2,1)}) %all-gather.17.cloned.1.call-update) | async-done | bytes 1638416 | tf_op jit(solution)/shard_map/all_gather | solution.py:79
  210.0 28.9 %fusion.101 = (f32[8,1504]{1,0:T(8,128)S(1)}, f32[8,1504,1504]{1,2,0:T(8,128)}) fusion(bf16[1504,8,80]{0,2,1:T(8,128)(2,1)S(1)} %bitcast.117, bf16[1504,8,80]{0,2,1:T(8,128)(2,1)} %bitcast.119, pred[1504]{0:T(1024)(128)(4,1)S(1)} %iota_compare_fusion), kind=kOutput, calls=%fused_computation.138 | convolution fusion | flops 2931560704 | bytes 76284384 | tf_op jit(solution)/shard_map/while/body/eval_jaxpr/qhe,khe->hqk/dot_general | solution.py:36
  238.8 23.5 %fusion = f32[8,1504]{1,0:T(8,128)S(1)} fusion(f32[8,1504,1504]{1,2,0:T(8,128)} %get-tuple-element.104, f32[8,1504]{1,0:T(8,128)S(1)} %get-tuple-element.103), kind=kLoop, calls=%fused_computation.5 | loop fusion | flops 36180224 | bytes 72480768 | tf_op jit(solution)/shard_map/while/body/eval_jaxpr/reduce_sum | solution.py:46
  262.4 27.5 %fusion.95 = bf16[8,80,1504]{2,1,0:T(8,128)(2,1)} fusion(bf16[1504,8,80]{0,2,1:T(8,128)(2,1)S(1)} %bitcast.122, f32[8,1504,1504]{1,2,0:T(8,128)} %get-tuple-element.104, f32[8,1504]{1,0:T(8,128)S(1)} %fusion, f32[8,1504]{1,0:T(8,128)S(1)} %get-tuple-element.103), kind=kOutput, calls=%fused_computation.116 | convolution fusion | flops 2950631424 | bytes 76331008 | tf_op jit(solution)/shard_map/while/body/eval_jaxpr/hqk,khe->qhe/dot_general | solution.py:48
  298.3 48.8 %reduce-scatter.11.cloned.1.call-done = bf16[1,752,1280]{2,1,0:T(8,128)(2,1)} async-done(((bf16[1,1504,1280]{2,1,0:T(8,128)(2,1)}), bf16[1,752,1280]{2,1,0:T(8,128)(2,1)}) %reduce-scatter.11.cloned.1.call-update) | async-done | bytes 1925136 | tf_op jit(solution)/shard_map/reduce_scatter | solution.py:167
  355.0 58.2 %all-gather.23.cloned.1.call-done = bf16[1280,2560]{1,0:T(8,128)(2,1)} async-done(((bf16[80,2560]{1,0:T(8,128)(2,1)}), bf16[1280,2560]{1,0:T(8,128)(2,1)}) %all-gather.23.cloned.1.call-update) | async-done | bytes 6553616 | tf_op jit(solution)/shard_map/all_gather | solution.py:83
  413.2 53.7 %all-gather.21.cloned.1.call-done = bf16[1,1504,1280]{2,1,0:T(8,128)(2,1)} async-done(((bf16[1,752,1280]{2,1,0:T(8,128)(2,1)}), bf16[1,1504,1280]{2,1,0:T(8,128)(2,1)}) %all-gather.21.cloned.1.call-update) | async-done | bytes 3850256 | tf_op jit(solution)/shard_map/all_gather | solution.py:172
  466.8 46.3 %multiply_convert_fusion.1 = (bf16[1504,2560]{1,0:T(8,128)(2,1)}, f32[1504,2560]{1,0:T(8,128)}, f32[1504,2560]{1,0:T(8,128)}) fusion(f32[2560]{0:T(1024)S(1)} %convert_element_type.231, bf16[1280,2560]{1,0:T(8,128)(2,1)} %all-gather.23.cloned.1.call-done, bf16[1,1504,1280]{2,1,0:T(8,128)(2,1)} %all-gather.21.cloned.1.call-done), kind=kOutput, calls=%fused_computation.14 | convolution fusion | flops 10110730240 | bytes 48916480 | tf_op jit(solution)/shard_map/csd,df->csf/dot_general | solution.py:173
  513.2 8.2 all-gather.27.cloned.1.call-done
  521.3 65.8 %all-gather.25.cloned.1.call-done = bf16[2560,1280]{0,1:T(8,128)(2,1)} async-done(((bf16[2560,80]{0,1:T(8,128)(2,1)}), bf16[2560,1280]{0,1:T(8,128)(2,1)}) %all-gather.25.cloned.1.call-update) | async-done | bytes 6553616 | tf_op jit(solution)/shard_map/all_gather | solution.py:91
  587.2 27.5 %fusion.102 = (bf16[2560]{0:T(1024)(128)(2,1)}, bf16[1504,2560]{1,0:T(8,128)(2,1)}) fusion(f32[1504,2560]{1,0:T(8,128)} %get-tuple-element.98, bf16[2560,1280]{0,1:T(8,128)(2,1)} %all-gather.25.cloned.1.call-done, bf16[1,1504,1280]{2,1,0:T(8,128)(2,1)} %all-gather.27.cloned.1.call-done, f32[1504,2560]{1,0:T(8,128)} %get-tuple-element.105, ...), kind=kOutput, calls=%fused_computation.139 | convolution fusion | flops 9918216192 | bytes 48921600 | tf_op jit(solution)/shard_map/csd,fd->csf/dot_general | solution.py:193
  614.7 15.8 %fusion.16 = bf16[1,1504,1280]{2,1,0:T(8,128)(2,1)} fusion(bf16[1504,2560]{1,0:T(8,128)(2,1)} %get-tuple-element.113, bf16[1280,2560]{1,0:T(8,128)(2,1)} %all-gather.23.cloned.1.call-done), kind=kOutput, calls=%fused_computation.38 | convolution fusion | flops 9858539520 | bytes 18104320 | tf_op jit(solution)/shard_map/csf,df->csd/dot_general | solution.py:199
  630.5 15.6 %fusion.15 = bf16[1,1504,1280]{2,1,0:T(8,128)(2,1)} fusion(bf16[1504,2560]{1,0:T(8,128)(2,1)} %get-tuple-element.97, bf16[2560,1280]{0,1:T(8,128)(2,1)} %all-gather.25.cloned.1.call-done), kind=kOutput, calls=%fused_computation.37 | convolution fusion | flops 9858539520 | bytes 18104320 | tf_op jit(solution)/shard_map/csf,fd->csd/dot_general | solution.py:178
  646.8 33.4 %reduce-scatter.15.cloned.1.call-done = bf16[1,752,1280]{2,1,0:T(8,128)(2,1)} async-done(((bf16[1,1504,1280]{2,1,0:T(8,128)(2,1)}), bf16[1,752,1280]{2,1,0:T(8,128)(2,1)}) %reduce-scatter.15.cloned.1.call-update) | async-done | bytes 1925136 | tf_op jit(solution)/shard_map/reduce_scatter | solution.py:202
  685.1 48.4 %reduce-scatter.13.cloned.1.call-done = bf16[1,752,1280]{2,1,0:T(8,128)(2,1)} async-done(((bf16[1,1504,1280]{2,1,0:T(8,128)(2,1)}), bf16[1,752,1280]{2,1,0:T(8,128)(2,1)}) %reduce-scatter.13.cloned.1.call-update) | async-done | bytes 1925136 | tf_op jit(solution)/shard_map/reduce_scatter | solution.py:181
  741.2 15.9 %convolution_convert_fusion = bf16[2560,1280]{0,1:T(8,128)(2,1)} fusion(bf16[1504,2560]{1,0:T(8,128)(2,1)} %get-tuple-element.97, bf16[1,1504,1280]{2,1,0:T(8,128)(2,1)} %all-gather.27.cloned.1.call-done), kind=kOutput, calls=%fused_computation.28 | convolution fusion | flops 9859891200 | bytes 18104320 | tf_op jit(solution)/shard_map/csf,csd->fd/dot_general | solution.py:192
  757.1 15.7 %convolution_convert_fusion.1 = bf16[1280,2560]{1,0:T(8,128)(2,1)} fusion(bf16[1504,2560]{1,0:T(8,128)(2,1)} %get-tuple-element.113, bf16[1,1504,1280]{2,1,0:T(8,128)(2,1)} %all-gather.21.cloned.1.call-done), kind=kOutput, calls=%fused_computation.29 | convolution fusion | flops 9859891200 | bytes 18104320 | tf_op jit(solution)/shard_map/csd,csf->df/dot_general | solution.py:196
  773.7 20.5 %all-gather.29.cloned.1.call-done = bf16[1,1504,1280]{2,1,0:T(8,128)(2,1)} async-done(((bf16[1,752,1280]{2,1,0:T(8,128)(2,1)}), bf16[1,1504,1280]{2,1,0:T(8,128)(2,1)}) %all-gather.29.cloned.1.call-update) | async-done | bytes 3850256 | tf_op jit(solution)/shard_map/all_gather | solution.py:211
  811.3 50.4 %multiply_reduce_fusion = (f32[8,1504]{1,0:T(8,128)S(1)}, f32[8,1504,1504]{1,2,0:T(8,128)}) fusion(f32[8,1504,1504]{1,2,0:T(8,128)} %get-tuple-element.104, f32[8,1504]{1,0:T(8,128)S(1)} %log_add_fusion, bf16[1504,8,80]{0,2,1:T(8,128)(2,1)S(1)} %bitcast.115, bf16[1504,8,80]{0,2,1:T(8,128)(2,1)} %bitcast.121), kind=kOutput, calls=%fused_computation.1 | convolution fusion | flops 2949656832 | bytes 148715520 | tf_op jit(solution)/shard_map/while/body/eval_jaxpr/qhe,khe->hqk/dot_general | solution.py:60
  861.6 27.5 %bitcast_reduce_fusion = (bf16[8,80]{1,0:T(8,128)(2,1)S(1)}, bf16[8,80,1504]{2,1,0:T(8,128)(2,1)}) fusion(bf16[1504,8,80]{0,2,1:T(8,128)(2,1)S(1)} %bitcast.116, f32[8,1504,1504]{1,2,0:T(8,128)} %get-tuple-element.104, f32[8,1504]{1,0:T(8,128)S(1)} %log_add_fusion), kind=kOutput, calls=%fused_computation.117 | convolution fusion | flops 2933497344 | bytes 76284160 | tf_op jit(solution)/shard_map/while/body/eval_jaxpr/hqk,qhe->khe/dot_general | solution.py:57
  896.7 62.4 %multiply_convert_fusion = bf16[8,1504,1504]{1,2,0:T(8,128)(2,1)} fusion(f32[8,1504,1504]{1,2,0:T(8,128)} %get-tuple-element.107, f32[8,1504,1504]{1,2,0:T(8,128)} %get-tuple-element.104, f32[8,1504]{1,0:T(8,128)S(1)} %get-tuple-element.106, f32[8,1504]{1,0:T(8,128)S(1)} %log_add_fusion), kind=kLoop, calls=%fused_computation | loop fusion | flops 72384512 | bytes 181057536 | tf_op jit(solution)/shard_map/while/body/eval_jaxpr/convert_element_type | solution.py:64
  959.1 15.1 %convert_reduce_fusion.4 = (f32[8,80]{1,0:T(8,128)S(1)}, bf16[8,80,1504]{2,1,0:T(8,128)(2,1)S(1)}) fusion(bf16[1504,8,80]{0,2,1:T(8,128)(2,1)S(1)} %bitcast.120, bf16[8,1504,1504]{1,2,0:T(8,128)(2,1)} %multiply_convert_fusion), kind=kOutput, calls=%fused_computation.62 | convolution fusion | flops 2898267648 | bytes 40045056 | tf_op jit(solution)/shard_map/while/body/eval_jaxpr/hqk,khe->qhe/dot_general | solution.py:65
  982.2 18.4 %convolution_convert_fusion.5 = bf16[8,80,1504]{2,1,0:T(8,128)(2,1)} fusion(bf16[1504,8,80]{0,2,1:T(8,128)(2,1)S(1)} %bitcast.118, bf16[8,1504,1504]{1,2,0:T(8,128)(2,1)} %multiply_convert_fusion), kind=kOutput, calls=%fused_computation.108 | convolution fusion | flops 2896343040 | bytes 40042496 | tf_op jit(solution)/shard_map/while/body/eval_jaxpr/hqk,qhe->khe/dot_general | solution.py:68
  1027.1 61.4 %all-reduce.20 = (bf16[640]{0:T(1024)(128)(2,1)S(1)}, bf16[640]{0:T(1024)(128)(2,1)S(1)}, bf16[2560]{0:T(1024)(128)(2,1)S(1)}) all-reduce(bf16[640]{0:T(1024)(128)(2,1)S(1)} %convert_element_type.265, bf16[640]{0:T(1024)(128)(2,1)S(1)} %reduce_sum.213, ...), channel_id=9, replica_groups=mesh['fsdp'=16,'tp'=2] {'fsdp'}, use_global_device_ids=true, to_apply=%region_21.22.clone | all-reduce | flops 3840 | bytes 15360
  1091.9 8.4 reduce-scatter.23.cloned.1.call-done
  1101.9 61.5 %reduce-scatter.19.cloned.1.call-done = bf16[80,640]{1,0:T(8,128)(2,1)} async-done(((bf16[1280,640]{1,0:T(8,128)(2,1)}), bf16[80,640]{1,0:T(8,128)(2,1)}) %reduce-scatter.19.cloned.1.call-update) | async-done | bytes 102416 | tf_op jit(solution)/shard_map/reduce_scatter | solution.py:249
  1165.0 60.6 %reduce-scatter.21.cloned.1.call-done = bf16[80,640]{1,0:T(8,128)(2,1)} async-done(((bf16[1280,640]{1,0:T(8,128)(2,1)}), bf16[80,640]{1,0:T(8,128)(2,1)}) %reduce-scatter.21.cloned.1.call-update) | async-done | bytes 102416 | tf_op jit(solution)/shard_map/reduce_scatter | solution.py:252
  1227.1 50.8 %reduce-scatter.17.cloned.1.call-done = bf16[1,752,1280]{2,1,0:T(8,128)(2,1)} async-done(((bf16[1,1504,1280]{2,1,0:T(8,128)(2,1)}), bf16[1,752,1280]{2,1,0:T(8,128)(2,1)}) %reduce-scatter.17.cloned.1.call-update) | async-done | bytes 1925136 | tf_op jit(solution)/shard_map/reduce_scatter | solution.py:240
  1281.5 40.1 %all-reduce.18 = (f32[1280]{0:T(1024)S(1)}, f32[1280]{0:T(1024)S(1)}, f32[1280]{0:T(1024)S(1)}, f32[1280]{0:T(1024)S(1)}, f32[1280]{0:T(1024)S(1)}, /*index=5*/f32[1280]{0:T(1024)S(1)}) all-reduce(f32[1280]{0:T(1024)S(1)} %copy-done.32, f32[1280]{0:T(1024)S(1)} %copy-done.33, ...), channel_id=12, replica_groups=mesh['fsdp'=16,'tp'=2] {'fsdp','tp'}, use_global_device_ids=true, to_apply=%region_26.27.clone | all-reduce | flops 7680 | bytes 61440
  (229 shorter events, 157.1 us)
Async XLA Ops:
  7.2 53.7 %copy-start = (bf16[1,752,1280]{2,1,0:T(8,128)(2,1)S(1)}, bf16[1,752,1280]{2,1,0:T(8,128)(2,1)}, u32[]{:S(2)}) copy-start(bf16[1,752,1280]{2,1,0:T(8,128)(2,1)} %param.19) | copy-start | bytes 5775364
  7.2 122.7 %all-gather.15.cloned.1.call-start = ((), (), s32[]{:S(2)}) async-start(), calls=%async_computation.12 | async-start | bytes 1740800 | tf_op jit(solution)/shard_map/all_gather | solution.py:78
  7.9 121.9 %all-gather.11.cloned.1.call-start = ((), (), s32[]{:S(2)}) async-start(), calls=%async_computation.10 | async-start | bytes 5775360 | tf_op jit(solution)/shard_map/all_gather | solution.py:144
  62.9 95.2 %all-gather.13.cloned.1.call-start = ((), (), s32[]{:S(2)}) async-start(), calls=%async_computation.11 | async-start | bytes 1740800 | tf_op jit(solution)/shard_map/all_gather | solution.py:80
  63.6 135.3 %all-gather.17.cloned.1.call-start = ((), (), s32[]{:S(2)}) async-start(), calls=%async_computation.13 | async-start | bytes 1740800 | tf_op jit(solution)/shard_map/all_gather | solution.py:79
  64.2 225.7 %all-gather.19.cloned.1.call-start = ((), (), s32[]{:S(2)}) async-start(), calls=%async_computation.14 | async-start | bytes 1740800 | tf_op jit(solution)/shard_map/all_gather | solution.py:90
  64.8 282.4 %reduce-scatter.11.cloned.1.call-start = ((), (), s32[]{:S(2)}) async-start(), calls=%async_computation.15 | async-start | bytes 5775360 | tf_op jit(solution)/shard_map/reduce_scatter | solution.py:167
  139.6 70.4 %copy-start.5 = (bf16[1504,640]{0,1:T(8,128)(2,1)}, bf16[1504,640]{0,1:T(8,128)(2,1)S(1)}, u32[]{:S(2)}) copy-start(bf16[1504,640]{0,1:T(8,128)(2,1)S(1)} %copy.57) | copy-start | bytes 5775364
  297.0 116.1 %all-gather.23.cloned.1.call-start = ((), (), s32[]{:S(2)}) async-start(), calls=%async_computation.17 | async-start | bytes 6963200 | tf_op jit(solution)/shard_map/all_gather | solution.py:83
  297.8 169.0 %all-gather.21.cloned.1.call-start = ((), (), s32[]{:S(2)}) async-start(), calls=%async_computation.16 | async-start | bytes 5775360 | tf_op jit(solution)/shard_map/all_gather | solution.py:172
  298.3 52.3 %copy-start.16 = (f32[1280]{0:T(1024)}, f32[1280]{0:T(1024)S(1)}, u32[]{:S(2)}) copy-start(f32[1280]{0:T(1024)S(1)} %convert_element_type.227) | copy-start | bytes 15364
  353.6 167.8 %all-gather.27.cloned.1.call-start = ((), (), s32[]{:S(2)}) async-start(), calls=%async_computation.20 | async-start | bytes 5775360 | tf_op jit(solution)/shard_map/all_gather | solution.py:191
  354.3 232.8 %all-gather.25.cloned.1.call-start = ((), (), s32[]{:S(2)}) async-start(), calls=%async_computation.18 | async-start | bytes 6963200 | tf_op jit(solution)/shard_map/all_gather | solution.py:91
  354.9 325.3 %reduce-scatter.15.cloned.1.call-start = ((), (), s32[]{:S(2)}) async-start(), calls=%async_computation.21 | async-start | bytes 5775360 | tf_op jit(solution)/shard_map/reduce_scatter | solution.py:202
  630.5 103.0 %reduce-scatter.13.cloned.1.call-start = ((), (), s32[]{:S(2)}) async-start(), calls=%async_computation.19 | async-start | bytes 5775360 | tf_op jit(solution)/shard_map/reduce_scatter | solution.py:181
  646.2 148.0 %all-gather.29.cloned.1.call-start = ((), (), s32[]{:S(2)}) async-start(), calls=%async_computation.22 | async-start | bytes 5775360 | tf_op jit(solution)/shard_map/all_gather | solution.py:211
  741.2 281.8 %reduce-scatter.29.cloned.1.call-start = ((), (), s32[]{:S(2)}) async-start(), calls=%async_computation.29 | async-start | bytes 6963200 | tf_op jit(solution)/shard_map/reduce_scatter | solution.py:275
  757.1 267.8 %reduce-scatter.27.cloned.1.call-start = ((), (), s32[]{:S(2)}) async-start(), calls=%async_computation.28 | async-start | bytes 6963200 | tf_op jit(solution)/shard_map/reduce_scatter | solution.py:264
  772.9 317.4 %reduce-scatter.25.cloned.1.call-start = ((), (), s32[]{:S(2)}) async-start(), calls=%async_computation.27 | async-start | bytes 1740800 | tf_op jit(solution)/shard_map/reduce_scatter | solution.py:272
  810.8 289.5 %reduce-scatter.23.cloned.1.call-start = ((), (), s32[]{:S(2)}) async-start(), calls=%async_computation.26 | async-start | bytes 1740800 | tf_op jit(solution)/shard_map/reduce_scatter | solution.py:255
  896.5 267.0 %reduce-scatter.19.cloned.1.call-start = ((), (), s32[]{:S(2)}) async-start(), calls=%async_computation.24 | async-start | bytes 1740800 | tf_op jit(solution)/shard_map/reduce_scatter | solution.py:249
  896.7 62.4 %copy-start.7 = (bf16[1504,640]{0,1:T(8,128)(2,1)S(1)}, bf16[1504,640]{0,1:T(8,128)(2,1)}, u32[]{:S(2)}) copy-start(bf16[1504,640]{0,1:T(8,128)(2,1)} %copy.58) | copy-start | bytes 5775364
  982.2 243.4 %reduce-scatter.21.cloned.1.call-start = ((), (), s32[]{:S(2)}) async-start(), calls=%async_computation.25 | async-start | bytes 1740800 | tf_op jit(solution)/shard_map/reduce_scatter | solution.py:252
  1008.0 269.9 %reduce-scatter.17.cloned.1.call-start = ((), (), s32[]{:S(2)}) async-start(), calls=%async_computation.23 | async-start | bytes 5775360 | tf_op jit(solution)/shard_map/reduce_scatter | solution.py:240
  1021.4 256.6 %copy-start.3 = (bf16[1,752,1280]{2,1,0:T(8,128)(2,1)S(1)}, bf16[1,752,1280]{2,1,0:T(8,128)(2,1)}, u32[]{:S(2)}) copy-start(bf16[1,752,1280]{2,1,0:T(8,128)(2,1)} %param.19) | copy-start | bytes 5775364
  1021.4 256.6 %copy-start.23 = (f32[1280]{0:T(1024)S(1)}, f32[1280]{0:T(1024)}, u32[]{:S(2)}) copy-start(f32[1280]{0:T(1024)} %copy-done.22) | copy-start | bytes 15364
  1021.4 256.6 %copy-start.25 = (f32[752]{0:T(1024)S(1)}, f32[752]{0:T(1024)}, u32[]{:S(2)}) copy-start(f32[752]{0:T(1024)} %copy-done.24) | copy-start | bytes 9028
  1021.4 256.6 %copy-start.29 = (f32[752]{0:T(1024)S(1)}, f32[752]{0:T(1024)}, u32[]{:S(2)}) copy-start(f32[752]{0:T(1024)} %copy-done.28) | copy-start | bytes 9028
  1021.4 260.0 %copy-start.32 = (f32[1280]{0:T(1024)S(1)}, f32[1280]{0:T(1024)}, u32[]{:S(2)}) copy-start(f32[1280]{0:T(1024)} %get-tuple-element.94) | copy-start | bytes 15364
  1021.4 260.0 %copy-start.33 = (f32[1280]{0:T(1024)S(1)}, f32[1280]{0:T(1024)}, u32[]{:S(2)}) copy-start(f32[1280]{0:T(1024)} %get-tuple-element.100) | copy-start | bytes 15364
  1021.5 260.0 %copy-start.34 = (f32[1280]{0:T(1024)S(1)}, f32[1280]{0:T(1024)}, u32[]{:S(2)}) copy-start(f32[1280]{0:T(1024)} %get-tuple-element.68) | copy-start | bytes 15364
  1021.5 260.0 %copy-start.35 = (f32[1280]{0:T(1024)S(1)}, f32[1280]{0:T(1024)}, u32[]{:S(2)}) copy-start(f32[1280]{0:T(1024)} %get-tuple-element.74) | copy-start | bytes 15364
  (38 other events, 487.2 us)
Sparse Core Ops, SparseCore 0:
  10.2 42.8 all-gather.14
  63.0 52.8 all-gather.10
  118.1 39.9 all-gather.12
  160.1 38.8 all-gather.16
  201.0 38.8 all-gather.18
  297.2 49.9 reduce-scatter.10
  349.7 63.3 all-gather.22
  415.3 51.4 all-gather.20
  468.4 52.8 all-gather.26
  523.7 63.3 all-gather.24
  630.6 49.6 reduce-scatter.14
  682.4 51.0 reduce-scatter.12
  741.3 52.8 all-gather.28
  798.5 86.9 reduce-scatter.28
  889.3 85.9 reduce-scatter.26
  979.3 58.4 reduce-scatter.24
  1041.4 58.8 reduce-scatter.22
  1104.9 58.4 reduce-scatter.18
  1167.1 58.3 reduce-scatter.20
  1227.8 50.1 reduce-scatter.16
where the time goes:
time: 1340 us
  waiting for transfers between devices  571 us (43%)
  matrix products  381 us (28%)
  blocking collectives  204 us (15%)
  other arithmetic  133 us (10%)
  local copies, waits for them, and re-layouts  27.1 us (2%)
  between operations  18 us (1%)
    unnamed x4, blocking collectives  204 us
    all_gather x1, waiting for transfers between devices, gather_outward(): lax.all_gather(w_reduce, 'fsdp', axis=1, tiled=True)  65.8 us
    convert_element_type x1, other arithmetic, attend_back(): score_grad = (probs * (weight_grad - row_inner)).astype(jnp.bfloat16)  62.4 us
    reduce_scatter x1, waiting for transfers between devices, per_device(): lax.psum_scatter(w_query_grad.astype(jnp.bfloat16), 'fsdp', scatter_dimen...  61.5 us
    reduce_scatter x1, waiting for transfers between devices, per_device(): lax.psum_scatter(w_key_grad.astype(jnp.bfloat16), 'fsdp', scatter_dimensi...  60.6 us
    all_gather x1, waiting for transfers between devices, gather_inward(): lax.all_gather(w_expand, 'fsdp', axis=0, tiled=True)  58.2 us
    all_gather x1, waiting for transfers between devices, per_device(): lax.all_gather(norm_two.astype(jnp.bfloat16), 'tp', axis=1, tiled=True)  53.7 us
    reduce_scatter x1, waiting for transfers between devices, per_device(): lax.psum_scatter(first_terms.astype(jnp.bfloat16), 'tp', scatter_dimensio...  50.8 us
  transfers between devices with their start and end apart: 20, of which 14 were waited for; matrix products, arithmetic and copies ran while one was open for 35% of the time, Pallas kernels for 0%

commit v1 on v0

--- a/solution.py
+++ b/solution.py
@@ -1,6 +1,10 @@
+import functools
+
 import jax
 import jax.numpy as jnp
 from jax import lax
+from jax.experimental import pallas as pl
+from jax.experimental.pallas import tpu as pltpu
 from jax.sharding import PartitionSpec as P
 
 HD = 80
@@ -8,6 +12,7 @@
 
 EPSILON = 1e-05
 MASKED = -1000000000.0
+HIDDEN = -1e30
 
 
 def layer_norm(features, norm_gain, norm_shift):
@@ -305,9 +310,740 @@
     )
 
 
+VMEM_LIMIT = 60 << 20
+PAD = 128
+
+
+def kernel_params():
+    return pltpu.CompilerParams(vmem_limit_bytes=VMEM_LIMIT)
+
+
+def cost(flops, moved):
+    return pl.CostEstimate(flops=int(flops), bytes_accessed=int(moved), transcendentals=0)
+
+
+def row_pieces(rows, size):
+    return [(start, min(size, rows - start)) for start in range(0, rows, size)]
+
+
+def whole(shape, fixed=None):
+    index = fixed if fixed is not None else (0,) * len(shape)
+    return pl.BlockSpec(shape, lambda *_: index)
+
+
+def normalise(rows):
+    row_mean = jnp.mean(rows, axis=-1, keepdims=True)
+    centred = rows - row_mean
+    inverse = lax.rsqrt(jnp.mean(centred * centred, axis=-1, keepdims=True) + EPSILON)
+    return centred * inverse, inverse
+
+
+def dot_nn(left, right):
+    return jnp.dot(left, right, preferred_element_type=jnp.float32)
+
+
+def dot_nt(left, right):
+    return lax.dot_general(left, right, (((1,), (1,)), ((), ())), preferred_element_type=jnp.float32)
+
+
+def dot_tn(left, right):
+    return lax.dot_general(left, right, (((0,), (0,)), ((), ())), preferred_element_type=jnp.float32)
+
+
+def project_kernel(
+    heads, scal_ref, frames_ref, gain_ref, shift_ref, weight_ref, bq_ref, bv_ref,
+    first_ref, q_ref, k_ref, v_ref,
+):
+    rows, width = frames_ref.shape
+    cols = heads * HD
+    length, start = scal_ref[0], scal_ref[1]
+    q_factor = HD ** (-0.5)
+    pieces = row_pieces(rows, 256)
+
+    def norm(piece):
+        normed, _ = normalise(frames_ref[piece[0] : piece[0] + piece[1], :].astype(jnp.float32))
+        first = (normed * gain_ref[...] + shift_ref[...]).astype(jnp.bfloat16)
+        first_ref[piece[0] : piece[0] + piece[1], :] = first
+        return first
+
+    def split(block, offset, filler, lane):
+        if offset + PAD <= block.shape[1]:
+            part = block[:, offset : offset + PAD]
+        else:
+            back = block.shape[1] - PAD
+            part = pltpu.roll(block[:, back:], PAD - (offset - back), 1)
+        return jnp.where(lane < HD, part, filler).astype(jnp.bfloat16)
+
+    def finish(piece, out):
+        lane = lax.broadcasted_iota(jnp.int32, (piece[1], PAD), 1)
+        position = lax.broadcasted_iota(jnp.int32, (piece[1], PAD), 0) + (start + piece[0])
+        one = jnp.where(lane == HD, 1.0, 0.0)
+        hide = jnp.where((lane == HD) & (position >= length), HIDDEN, 0.0)
+        queries = (out[:, :cols] + bq_ref[...]) * q_factor
+        keys = out[:, cols : 2 * cols]
+        values = out[:, 2 * cols :] + bv_ref[...]
+        for head in range(heads):
+            where = (head, slice(piece[0], piece[0] + piece[1]), slice(None))
+            q_ref[where] = split(queries, head * HD, one, lane)
+            k_ref[where] = split(keys, head * HD, hide, lane)
+            v_ref[where] = split(values, head * HD, 0.0, lane)
+
+    first = norm(pieces[0])
+    for number, piece in enumerate(pieces):
+        out = dot_nn(first, weight_ref[...])
+        if number + 1 < len(pieces):
+            first = norm(pieces[number + 1])
+        finish(piece, out)
+
+
+def project(scalars, frames, gain, shift, weights, bias_q, bias_v, heads):
+    rows, width = frames.shape
+    cols = heads * HD
+    head_out = jax.ShapeDtypeStruct((heads, rows, PAD), jnp.bfloat16)
+    return pl.pallas_call(
+        functools.partial(project_kernel, heads),
+        out_shape=(jax.ShapeDtypeStruct((rows, width), jnp.bfloat16), head_out, head_out, head_out),
+        grid_spec=pltpu.PrefetchScalarGridSpec(
+            num_scalar_prefetch=1,
+            grid=(1,),
+            in_specs=[
+                whole((rows, width)), whole((1, width)), whole((1, width)),
+                whole((width, 3 * cols)), whole((1, cols)), whole((1, cols)),
+            ],
+            out_specs=(whole((rows, width)),) + (whole((heads, rows, PAD)),) * 3,
+        ),
+        compiler_params=kernel_params(),
+        cost_estimate=cost(2 * rows * width * 3 * cols, 4 * rows * width + 6 * width * cols),
+        name="project",
+    )(scalars, frames, gain, shift, weights, bias_q, bias_v)
+
+
+def attend_kernel(q_ref, ko_ref, kt_ref, vo_ref, vt_ref, out_ref, log_ref):
+    per_step, rows, _ = q_ref.shape
+    half = -(-rows // 256) * 128
+    pieces = [(head, start, size) for head in range(per_step) for start, size in row_pieces(rows, half)]
+    keys = [jnp.concatenate([ko_ref[h], kt_ref[h]], axis=0) for h in range(per_step)]
+    values = [jnp.concatenate([vo_ref[h], vt_ref[h]], axis=0).T[:HD] for h in range(per_step)]
+
+    def scores(piece):
+        head, start, size = piece
+        return dot_nt(keys[head], q_ref[head, start : start + size, :])
+
+    def finish(piece, score):
+        head, start, size = piece
+        top = jnp.max(score, axis=0, keepdims=True)
+        raised = jnp.exp(score - top)
+        total = jnp.sum(raised, axis=0, keepdims=True)
+        context = dot_nn(values[head], raised.astype(jnp.bfloat16)) / total
+        out_ref[head, :, start : start + size] = context.astype(jnp.bfloat16)
+        log_ref[head, :, start : start + size] = top + jnp.log(total)
+
+    current = scores(pieces[0])
+    for number, piece in enumerate(pieces):
+        coming = scores(pieces[number + 1]) if number + 1 < len(pieces) else None
+        finish(piece, current)
+        current = coming
+
+
+def attend_rows(queries, keys_own, keys_far, values_own, values_far):
+    heads, rows, _ = queries.shape
+    per_step = 2 if heads % 2 == 0 else 1
+    spec = pl.BlockSpec((per_step, rows, PAD), lambda h: (h, 0, 0))
+    return pl.pallas_call(
+        attend_kernel,
+        out_shape=(
+            jax.ShapeDtypeStruct((heads, HD, rows), jnp.bfloat16),
+            jax.ShapeDtypeStruct((heads, 1, rows), jnp.float32),
+        ),
+        grid=(heads // per_step,),
+        in_specs=[spec] * 5,
+        out_specs=(
+            pl.BlockSpec((per_step, HD, rows), lambda h: (h, 0, 0)),
+            pl.BlockSpec((per_step, 1, rows), lambda h: (h, 0, 0)),
+        ),
+        compiler_params=kernel_params(),
+        cost_estimate=cost(heads * 2 * rows * 2 * rows * 2 * 400, heads * rows * PAD * 12),
+        name="attend",
+    )(queries, keys_own, keys_far, values_own, values_far)
+
+
+def attend_back_kernel(
+    qo_ref, qt_ref, ko_ref, kt_ref, vo_ref, vt_ref, go_ref, gt_ref, lo_ref, lt_ref,
+    dqo_ref, dqt_ref, dko_ref, dkt_ref, dvo_ref, dvt_ref,
+):
+    rows = qo_ref.shape[1]
+    keys = jnp.concatenate([ko_ref[0], kt_ref[0]], axis=0)
+    values = jnp.concatenate([vo_ref[0], vt_ref[0]], axis=0)
+    keys_turned = keys.T[:HD]
+    pieces = [(side, start, size) for side in range(2) for start, size in row_pieces(rows, 256)]
+    sides = ((qo_ref, go_ref, lo_ref, dqo_ref), (qt_ref, gt_ref, lt_ref, dqt_ref))
+
+    def query(piece):
+        side, start, size = piece
+        return sides[side][0][0, start : start + size, :]
+
+    def upstream(piece):
+        side, start, size = piece
+        return sides[side][1][0, :, start : start + size]
+
+    def begin(piece):
+        score = dot_nt(keys, query(piece))
+        padded = jnp.concatenate(
+            [upstream(piece), jnp.zeros((PAD - HD, piece[2]), jnp.bfloat16)], axis=0
+        )
+        return score, dot_nn(values, padded)
+
+    def middle(piece, score, weight_grad):
+        side, start, size = piece
+        probs = jnp.exp(score - sides[side][2][0, :, start : start + size])
+        tilted = probs * weight_grad
+        inner = jnp.sum(tilted, axis=0, keepdims=True)
+        return probs.astype(jnp.bfloat16), (tilted - probs * inner).astype(jnp.bfloat16)
+
+    total_k = total_v = None
+    current = begin(pieces[0])
+    for number, piece in enumerate(pieces):
+        coming = begin(pieces[number + 1]) if number + 1 < len(pieces) else None
+        weights, score_grad = middle(piece, *current)
+        value_part = dot_nt(weights, upstream(piece))
+        key_part = dot_nn(score_grad, query(piece))
+        query_grad = dot_nn(keys_turned, score_grad)
+        side, start, size = piece
+        sides[side][3][0, start : start + size, :HD] = query_grad.T.astype(jnp.bfloat16)
+        total_v = value_part if total_v is None else total_v + value_part
+        total_k = key_part if total_k is None else total_k + key_part
+        current = coming
+    dko_ref[0] = total_k[:rows].astype(jnp.bfloat16)
+    dkt_ref[0] = total_k[rows:].astype(jnp.bfloat16)
+    dvo_ref[0, :, :HD] = total_v[:rows].astype(jnp.bfloat16)
+    dvt_ref[0, :, :HD] = total_v[rows:].astype(jnp.bfloat16)
+
+
+def attend_back_rows(queries, keys, values, upstream, logs):
+    heads, rows, _ = queries[0].shape
+    spec = pl.BlockSpec((1, rows, PAD), lambda h: (h, 0, 0))
+    turned = pl.BlockSpec((1, HD, rows), lambda h: (h, 0, 0))
+    line = pl.BlockSpec((1, 1, rows), lambda h: (h, 0, 0))
+    return pl.pallas_call(
+        attend_back_kernel,
+        out_shape=(jax.ShapeDtypeStruct((heads, rows, PAD), jnp.bfloat16),) * 6,
+        grid=(heads,),
+        in_specs=[spec] * 6 + [turned] * 2 + [line] * 2,
+        out_specs=(spec,) * 6,
+        compiler_params=kernel_params(),
+        cost_estimate=cost(heads * 4 * rows * rows * 2 * 900, heads * rows * PAD * 24),
+        name="attend_back",
+    )(*queries, *keys, *values, *upstream, *logs)
+
+
+def merge_kernel(
+    co_ref, ct_ref, weight_ref, frames_ref, bias_ref, gain_ref, shift_ref, middle_ref, second_ref
+):
+    rows = frames_ref.shape[0]
+    cols = co_ref.shape[0]
+    own, far = co_ref[...].T, ct_ref[...].T
+    pieces = row_pieces(rows, 256)
+
+    def branch(piece):
+        take = slice(piece[0], piece[0] + piece[1])
+        return dot_nt(own[take], weight_ref[:, :cols]) + dot_nt(far[take], weight_ref[:, cols:])
+
+    def finish(piece, part):
+        take = slice(piece[0], piece[0] + piece[1])
+        middle = frames_ref[take, :].astype(jnp.float32) + part + bias_ref[...]
+        middle_ref[take, :] = middle
+        normed, _ = normalise(middle)
+        second_ref[take, :] = (normed * gain_ref[...] + shift_ref[...]).astype(jnp.bfloat16)
+
+    current = branch(pieces[0])
+    for number, piece in enumerate(pieces):
+        coming = branch(pieces[number + 1]) if number + 1 < len(pieces) else None
+        finish(piece, current)
+        current = coming
+
+
+def merge_heads(context_own, context_far, pack, slot, frames, bias, gain, shift):
+    rows, width = frames.shape
+    cols = context_own.shape[0]
+    return pl.pallas_call(
+        merge_kernel,
+        out_shape=(
+            jax.ShapeDtypeStruct((rows, width), jnp.float32),
+            jax.ShapeDtypeStruct((rows, width), jnp.bfloat16),
+        ),
+        grid=(1,),
+        in_specs=[
+            whole((cols, rows)), whole((cols, rows)), whole((width, 2 * cols), (0, slot)),
+            whole((rows, width)), whole((1, width)), whole((1, width)), whole((1, width)),
+        ],
+        out_specs=(whole((rows, width)),) * 2,
+        compiler_params=kernel_params(),
+        cost_estimate=cost(4 * rows * width * cols, 10 * rows * width + 4 * width * cols),
+        name="merge_heads",
+    )(context_own, context_far, pack, frames, bias, gain, shift)
+
+
+def feed_kernel(
+    second_ref, grad_ref, expand_ref, reduce_ref, bias_ref,
+    hidden_ref, back_ref, bsum_ref, out_ref, terms_ref, out_acc, terms_acc,
+):
+    step = pl.program_id(0)
+    rows = second_ref.shape[0]
+    pieces = row_pieces(rows, 376 if rows % 376 == 0 else 256)
+    expand, reduce = expand_ref[...], reduce_ref[...]
+
+    def begin(piece):
+        take = slice(piece[0], piece[0] + piece[1])
+        return dot_nn(second_ref[take, :], expand), dot_nn(grad_ref[take, :], reduce)
+
+    @pl.when(step == 0)
+    def _():
+        out_acc[...] = jnp.zeros_like(out_acc)
+        terms_acc[...] = jnp.zeros_like(terms_acc)
+
+    sums = None
+    current = begin(pieces[0])
+    for number, piece in enumerate(pieces):
+        coming = begin(pieces[number + 1]) if number + 1 < len(pieces) else None
+        take = slice(piece[0], piece[0] + piece[1])
+        raw, upstream = current
+        raw = raw + bias_ref[...]
+        below = 0.5 + 0.5 * lax.erf(raw * 0.7071067811865476)
+        density = jnp.exp(raw * raw * -0.5) * 0.3989422804014327
+        hidden = (raw * below).astype(jnp.bfloat16)
+        back = (upstream * (below + raw * density)).astype(jnp.bfloat16)
+        hidden_ref[take, :] = hidden
+        back_ref[take, :] = back
+        part = jnp.sum(back.astype(jnp.float32), axis=0, keepdims=True)
+        sums = part if sums is None else sums + part
+        terms_acc[take, :] += dot_nt(back, expand)
+        out_acc[take, :] += dot_nt(hidden, reduce)
+        current = coming
+    bsum_ref[...] = sums
+
+    @pl.when(step == pl.num_programs(0) - 1)
+    def _():
+        out_ref[...] = out_acc[...].astype(jnp.bfloat16)
+        terms_ref[...] = terms_acc[...].astype(jnp.bfloat16)
+
+
+def feed(second, grads, expand_pack, reduce_pack, bias, units):
+    rows, width = second.shape
+    block = 512 if units % 512 == 0 else units
+    wide = pl.BlockSpec((rows, block), lambda j: (0, j))
+    weight = pl.BlockSpec((width, block), lambda j: (0, j))
+    line = pl.BlockSpec((1, block), lambda j: (0, j))
+    return pl.pallas_call(
+        feed_kernel,
+        out_shape=(
+            jax.ShapeDtypeStruct((rows, units), jnp.bfloat16),
+            jax.ShapeDtypeStruct((rows, units), jnp.bfloat16),
+            jax.ShapeDtypeStruct((1, units), jnp.float32),
+            jax.ShapeDtypeStruct((rows, width), jnp.bfloat16),
+            jax.ShapeDtypeStruct((rows, width), jnp.bfloat16),
+        ),
+        grid=(units // block,),
+        in_specs=[whole((rows, width)), whole((rows, width)), weight, weight, line],
+        out_specs=(wide, wide, line, whole((rows, width)), whole((rows, width))),
+        scratch_shapes=[pltpu.VMEM((rows, width), jnp.float32)] * 2,
+        compiler_params=kernel_params(),
+        cost_estimate=cost(8 * rows * width * units, 8 * rows * (units + width) + 4 * width * units),
+        name="feed",
+    )(second, grads, expand_pack, reduce_pack, bias)
+
+
+def weight_grad_kernel(count, scale_cols, scale, *refs):
+    lefts, rights, out_ref = refs[:count], refs[count : 2 * count], refs[2 * count]
+    total = None
+    for left, right in zip(lefts, rights):
+        part = dot_tn(left[...], right[...])
+        total = part if total is None else total + part
+    if scale_cols:
+        block = out_ref.shape[1]
+        total = total * jnp.where(pl.program_id(0) * block < scale_cols, scale, 1.0)
+    out_ref[...] = total.astype(jnp.bfloat16)
+
+
+def weight_grad(lefts, rights, block, scale_cols=0, scale=1.0):
+    width, units = lefts[0].shape[1], rights[0].shape[1]
+    rows = sum(left.shape[0] for left in lefts)
+    return pl.pallas_call(
+        functools.partial(weight_grad_kernel, len(lefts), scale_cols, scale),
+        out_shape=jax.ShapeDtypeStruct((width, units), jnp.bfloat16),
+        grid=(units // block,),
+        in_specs=[whole(left.shape) for left in lefts]
+        + [pl.BlockSpec((right.shape[0], block), lambda j: (0, j)) for right in rights],
+        out_specs=pl.BlockSpec((width, block), lambda j: (0, j)),
+        compiler_params=kernel_params(),
+        cost_estimate=cost(2 * rows * width * units, 2 * (rows * (width + units) + width * units)),
+        name="weight_grad",
+    )(*lefts, *rights)
+
+
+def branch_kernel(
+    own_ref, far_ref, middle_ref, grad_ref, gain_ref, weight_ref,
+    mgrad_ref, branch_ref, go_ref, gt_ref, sums_ref,
+):
+    rows, width = middle_ref.shape
+    cols = go_ref.shape[0]
+    pieces = row_pieces(rows, 256)
+
+    def step_back(piece):
+        take = slice(piece[0], piece[0] + piece[1])
+        second_grad = own_ref[take, :].astype(jnp.float32) + far_ref[take, :].astype(jnp.float32)
+        normed, inverse = normalise(middle_ref[take, :])
+        wide = grad_ref[take, :].astype(jnp.float32)
+        moved = second_grad * normed
+        tilted = second_grad * gain_ref[...]
+        mgrad = wide + inverse * (
+            tilted
+            - jnp.mean(tilted, axis=-1, keepdims=True)
+            - normed * jnp.mean(tilted * normed, axis=-1, keepdims=True)
+        )
+        branch = mgrad.astype(jnp.bfloat16)
+        mgrad_ref[take, :] = mgrad
+        branch_ref[take, :] = branch
+        sums = [
+            jnp.sum(moved, axis=0, keepdims=True),
+            jnp.sum(second_grad, axis=0, keepdims=True),
+            jnp.sum(branch.astype(jnp.float32), axis=0, keepdims=True),
+            jnp.sum(wide, axis=0, keepdims=True),
+        ]
+        return branch, sums
+
+    def finish(piece, branch):
+        take = slice(piece[0], piece[0] + piece[1])
+        out = dot_nn(branch, weight_ref[...]).astype(jnp.bfloat16).T
+        go_ref[:, take] = out[:cols]
+        gt_ref[:, take] = out[cols:]
+
+    totals = None
+    branch, sums = step_back(pieces[0])
+    totals = sums
+    for number, piece in enumerate(pieces):
+        now = branch
+        if number + 1 < len(pieces):
+            branch, sums = step_back(pieces[number + 1])
+            totals = [a + b for a, b in zip(totals, sums)]
+        finish(piece, now)
+    for index, line in enumerate(totals):
+        sums_ref[index : index + 1, :] = line
+
+
+def branch_back(own, far, middle, grads, gain, pack, slot, cols):
+    rows, width = middle.shape
+    full = whole((rows, width))
+    return pl.pallas_call(
+        branch_kernel,
+        out_shape=(
+            jax.ShapeDtypeStruct((rows, width), jnp.float32),
+            jax.ShapeDtypeStruct((rows, width), jnp.bfloat16),
+            jax.ShapeDtypeStruct((cols, rows), jnp.bfloat16),
+            jax.ShapeDtypeStruct((cols, rows), jnp.bfloat16),
+            jax.ShapeDtypeStruct((4, width), jnp.float32),
+        ),
+        grid=(1,),
+        in_specs=[full, full, full, full, whole((1, width)), whole((width, 2 * cols), (0, slot))],
+        out_specs=(full, full, whole((cols, rows)), whole((cols, rows)), whole((4, width))),
+        compiler_params=kernel_params(),
+        cost_estimate=cost(4 * rows * width * cols, 18 * rows * width),
+        name="branch_back",
+    )(own, far, middle, grads, gain, pack)
+
+
+def out_grad_kernel(branch_ref, co_ref, ct_ref, out_ref):
+    cols = co_ref.shape[0]
+    branch = branch_ref[...]
+    out_ref[:, :cols] = dot_tn(branch, co_ref[...].T).astype(jnp.bfloat16)
+    out_ref[:, cols:] = dot_tn(branch, ct_ref[...].T).astype(jnp.bfloat16)
+
+
+def out_weight_grad(branch, context_own, context_far):
+    rows, width = branch.shape
+    cols = context_own.shape[0]
+    return pl.pallas_call(
+        out_grad_kernel,
+        out_shape=jax.ShapeDtypeStruct((width, 2 * cols), jnp.bfloat16),
+        grid=(1,),
+        in_specs=[whole((rows, width)), whole((cols, rows)), whole((cols, rows))],
+        out_specs=whole((width, 2 * cols)),
+        compiler_params=kernel_params(),
+        cost_estimate=cost(4 * rows * width * cols, 4 * rows * width + 4 * width * cols),
+        name="out_weight_grad",
+    )(branch, context_own, context_far)
+
+
+def first_kernel(
+    heads, dq_ref, dk_ref, dv_ref, weight_ref, frames_ref, pack_ref, terms_ref, sums_ref, bias_ref
+):
+    rows, width = frames_ref.shape
+    cols = heads * HD
+    q_factor = HD ** (-0.5)
+    pieces = row_pieces(rows, 256)
+    for part, ref in enumerate((dq_ref, dk_ref, dv_ref)):
+        for head in range(heads):
+            offset = part * cols + head * HD
+            pack_ref[:, offset : offset + HD] = ref[head, :, :HD]
+
+    def begin(piece):
+        take = slice(piece[0], piece[0] + piece[1])
+        return dot_nt(pack_ref[take, :cols], weight_ref[:, :cols]) * q_factor + dot_nt(
+            pack_ref[take, cols:], weight_ref[:, cols:]
+        )
+
+    totals = None
+    current = begin(pieces[0])
+    for number, piece in enumerate(pieces):
+        coming = begin(pieces[number + 1]) if number + 1 < len(pieces) else None
+        take = slice(piece[0], piece[0] + piece[1])
+        terms_ref[take, :] = current.astype(jnp.bfloat16)
+        normed, _ = normalise(frames_ref[take, :].astype(jnp.float32))
+        sums = [
+            jnp.sum(current * normed, axis=0, keepdims=True),
+            jnp.sum(current, axis=0, keepdims=True),
+            jnp.sum(pack_ref[take, :].astype(jnp.float32), axis=0, keepdims=True),
+        ]
+        totals = sums if totals is None else [a + b for a, b in zip(totals, sums)]
+        current = coming
+    sums_ref[0:1, :] = totals[0]
+    sums_ref[1:2, :] = totals[1]
+    bias_ref[...] = totals[2]
+
+
+def first_back(dq, dk, dv, weights, frames):
+    heads, rows, _ = dq.shape
+    width = frames.shape[1]
+    cols = heads * HD
+    return pl.pallas_call(
+        functools.partial(first_kernel, heads),
+        out_shape=(
+            jax.ShapeDtypeStruct((rows, 3 * cols), jnp.bfloat16),
+            jax.ShapeDtypeStruct((rows, width), jnp.bfloat16),
+            jax.ShapeDtypeStruct((2, width), jnp.float32),
+            jax.ShapeDtypeStruct((1, 3 * cols), jnp.float32),
+        ),
+        grid=(1,),
+        in_specs=[whole(dq.shape)] * 3 + [whole((width, 3 * cols)), whole((rows, width))],
+        out_specs=(
+            whole((rows, 3 * cols)), whole((rows, width)), whole((2, width)), whole((1, 3 * cols))
+        ),
+        compiler_params=kernel_params(),
+        cost_estimate=cost(6 * rows * width * cols, 6 * heads * rows * PAD + 6 * width * cols),
+        name="first_back",
+    )(dq, dk, dv, weights, frames)
+
+
+def frames_kernel(frames_ref, own_ref, far_ref, mgrad_ref, gain_ref, out_ref):
+    normed, inverse = normalise(frames_ref[...].astype(jnp.float32))
+    tilted = (own_ref[...].astype(jnp.float32) + far_ref[...].astype(jnp.float32)) * gain_ref[...]
+    out_ref[...] = (
+        mgrad_ref[...]
+        + inverse
+        * (
+            tilted
+            - jnp.mean(tilted, axis=-1, keepdims=True)
+            - normed * jnp.mean(tilted * normed, axis=-1, keepdims=True)
+        )
+    ).astype(jnp.bfloat16)
+
+
+def frames_back(frames, own, far, mgrad, gain):
+    rows, width = frames.shape
+    block = 376 if rows % 376 == 0 else rows
+    spec = pl.BlockSpec((block, width), lambda i: (i, 0))
+    return pl.pallas_call(
+        frames_kernel,
+        out_shape=jax.ShapeDtypeStruct((rows, width), jnp.bfloat16),
+        grid=(rows // block,),
+        in_specs=[spec] * 4 + [whole((1, width))],
+        out_specs=spec,
+        compiler_params=kernel_params(),
+        cost_estimate=cost(20 * rows * width, 12 * rows * width),
+        name="frames_back",
+    )(frames, own, far, mgrad, gain)
+
+
+def swap_tp(piece):
+    return lax.ppermute(piece, "tp", [(0, 1), (1, 0)])
+
+
+def gather_steps(vector, fsdp):
+    index = lax.axis_index("fsdp")
+    other = swap_tp(vector)
+    side = lax.axis_index("tp")
+    held = jnp.where(side == 0, jnp.stack([vector, other]), jnp.stack([other, vector]))
+    bit = 1
+    while bit < fsdp:
+        other = lax.ppermute(held, "fsdp", [(i, i ^ bit) for i in range(fsdp)])
+        low = (index & bit) == 0
+        held = jnp.where(low, jnp.concatenate([held, other]), jnp.concatenate([other, held]))
+        bit *= 2
+    return held
+
+
+def scatter_steps(held, fsdp):
+    index = lax.axis_index("fsdp")
+    bit = fsdp // 2
+    while bit >= 1:
+        low = (index & bit) == 0
+        first, second = held[:bit], held[bit:]
+        send = jnp.where(low, second, first)
+        held = jnp.where(low, first, second) + lax.ppermute(
+            send, "fsdp", [(i, i ^ bit) for i in range(fsdp)]
+        )
+        bit //= 2
+    return held[0]
+
+
+def per_device_pair(
+    frames, out_grad, clip_lengths, clip_order, w_query, w_key, w_value, b_query, b_value,
+    w_out, b_out, w_expand, b_expand, w_reduce, b_reduce,
+    first_gain, first_shift, second_gain, second_shift, *, fsdp,
+):
+    side = lax.axis_index("tp")
+    slot = lax.axis_index("fsdp")
+    clip_count = clip_order.shape[0]
+    every_clip = jnp.arange(clip_count, dtype=jnp.int32)
+    clip_id = jnp.sum(jnp.where(every_clip == slot, clip_order, 0))
+    length = jnp.sum(jnp.where(every_clip == clip_id, clip_lengths, 0))
+    frames, out_grad = frames[0], out_grad[0]
+    rows, width = frames.shape
+    cols = w_query.shape[1]
+    heads = cols // HD
+    units = w_expand.shape[1]
+    q_factor = HD ** (-0.5)
+    scal_own = jnp.stack([length, side * rows]).astype(jnp.int32)
+    scal_far = jnp.stack([length, (1 - side) * rows]).astype(jnp.int32)
+
+    qkv = lax.all_gather(
+        jnp.concatenate([w_query, w_key, w_value], axis=1), "fsdp", axis=0, tiled=True
+    )
+    frames_far = swap_tp(frames)
+    wide_six = [first_gain, first_shift, second_gain, second_shift, b_out, b_reduce]
+    small = gather_steps(jnp.concatenate(wide_six + [b_query, b_value, b_expand]), fsdp)
+    lot = first_gain.shape[0]
+    whole_six = small[:, : 6 * lot].astype(jnp.float32).reshape(2 * fsdp, 6, lot)
+    whole_six = whole_six.transpose(1, 0, 2).reshape(6, 1, width)
+    gain_one, shift_one, gain_two, shift_two, out_bias, reduce_bias = [whole_six[i] for i in range(6)]
+    mine = lax.dynamic_index_in_dim(
+        small[:, 6 * lot :].astype(jnp.float32).reshape(fsdp, 2, -1), side, axis=1, keepdims=False
+    )
+    part = b_query.shape[0]
+    bias_q = mine[:, :part].reshape(1, -1)
+    bias_v = mine[:, part : 2 * part].reshape(1, -1)
+    bias_e = mine[:, 2 * part :].reshape(1, -1)
+    out_turned = w_out.T
+    out_other = swap_tp(out_turned)
+    pack_two = lax.all_gather(
+        jnp.concatenate([w_expand, out_turned, out_other], axis=1), "fsdp", axis=0, tiled=True
+    )
+    out_slot = units // (2 * cols)
+    reduce_all = lax.all_gather(w_reduce.T, "fsdp", axis=0, tiled=True)
+    grads_far = swap_tp(out_grad)
+
+    first_own, q_own, k_own, v_own = project(
+        scal_own, frames, gain_one, shift_one, qkv, bias_q, bias_v, heads
+    )
+    first_far, q_far, k_far, v_far = project(
+        scal_far, frames_far, gain_one, shift_one, qkv, bias_q, bias_v, heads
+    )
+    context_send, log_far = attend_rows(q_far, k_own, k_far, v_own, v_far)
+    context_far = swap_tp(context_send.reshape(cols, rows))
+    context_own, log_own = attend_rows(q_own, k_own, k_far, v_own, v_far)
+    context_own = context_own.reshape(cols, rows)
+    middle, second_own = merge_heads(
+        context_own, context_far, pack_two, out_slot, frames, out_bias, gain_two, shift_two
+    )
+
+    second_far = swap_tp(second_own)
+    hid_own, back_own, bsum_own, out_own, terms_own = feed(
+        second_own, out_grad, pack_two, reduce_all, bias_e, units
+    )
+    hid_far, back_far, bsum_far, out_send, terms_send = feed(
+        second_far, grads_far, pack_two, reduce_all, bias_e, units
+    )
+    terms_far = swap_tp(terms_send)
+    out_far = swap_tp(out_send)
+    block = 512 if units % 512 == 0 else units
+    d_reduce = weight_grad([out_grad, grads_far], [hid_own, hid_far], block)
+    d_expand = weight_grad([second_own, second_far], [back_own, back_far], block)
+    out_frames = (
+        middle + out_own.astype(jnp.float32) + out_far.astype(jnp.float32) + reduce_bias
+    ).astype(jnp.bfloat16)
+    mgrad, branch, up_own, up_send, sums_two = branch_back(
+        terms_own, terms_far, middle, out_grad, gain_two, pack_two, out_slot, cols
+    )
+    up_far = swap_tp(up_send)
+    d_out = out_weight_grad(branch, context_own, context_far)
+
+    turned = (heads, HD, rows)
+    dq_own, dq_far, dk_own, dk_far, dv_own, dv_far = attend_back_rows(
+        (q_own, q_far), (k_own, k_far), (v_own, v_far),
+        (up_own.reshape(turned), up_far.reshape(turned)), (log_own, log_far),
+    )
+    pack_far, first_send, sums_far, bias_far = first_back(dq_far, dk_far, dv_far, qkv, frames_far)
+    first_recv = swap_tp(first_send)
+    pack_own, first_keep, sums_own, bias_own = first_back(dq_own, dk_own, dv_own, qkv, frames)
+    d_qkv = weight_grad([first_own, first_far], [pack_own, pack_far], cols, cols, q_factor)
+    frames_grad = frames_back(frames, first_keep, first_recv, mgrad, gain_one)
+
+    def scatter(grad):
+        return lax.psum_scatter(grad, "fsdp", scatter_dimension=0, tiled=True).astype(jnp.float32)
+
+    g_reduce, g_expand, g_qkv = scatter(d_reduce), scatter(d_expand), scatter(d_qkv)
+    g_out = lax.psum_scatter(d_out, "fsdp", scatter_dimension=0, tiled=True)
+    sums_one = sums_own + sums_far
+    bias_sum = bias_own + bias_far
+    wide_sums = jnp.concatenate([sums_one, sums_two])
+    wide_sums = wide_sums.reshape(6, fsdp, 2, lot).transpose(1, 2, 0, 3).reshape(fsdp, 12 * lot)
+    tall = jnp.concatenate(
+        [
+            wide_sums,
+            (bias_sum[:, :cols] * q_factor).reshape(fsdp, -1),
+            bias_sum[:, 2 * cols :].reshape(fsdp, -1),
+            (bsum_own + bsum_far).reshape(fsdp, -1),
+        ],
+        axis=1,
+    )
+    small_sum = scatter_steps(tall, fsdp)
+    six = small_sum[: 12 * lot].reshape(2, 6 * lot)
+    keep = lax.dynamic_index_in_dim(six, side, 0, keepdims=False)
+    send = lax.dynamic_index_in_dim(six, 1 - side, 0, keepdims=False)
+    six = (keep + swap_tp(send)).reshape(6, lot)
+    rest = small_sum[12 * lot :]
+    g_bq, g_bv, g_be = rest[:part], rest[part : 2 * part], rest[2 * part :]
+    g_out_sum = g_out[:, :cols].astype(jnp.float32) + swap_tp(g_out[:, cols:]).astype(jnp.float32)
+    return (
+        out_frames[None],
+        frames_grad[None],
+        g_qkv[:, :cols],
+        g_qkv[:, cols : 2 * cols],
+        g_qkv[:, 2 * cols :],
+        g_bq,
+        g_bv,
+        g_out_sum.T,
+        six[4],
+        g_expand,
+        g_be,
+        g_reduce.T,
+        six[5],
+        six[0],
+        six[1],
+        six[2],
+        six[3],
+    )
+
+
 def solution(mesh):
+    fsdp = mesh.shape["fsdp"]
+    if mesh.shape["tp"] == 2 and fsdp & (fsdp - 1) == 0:
+
+        def body(*args):
+            return per_device_pair(*args, fsdp=fsdp) if args[0].shape[0] == 1 else per_device(*args)
+    else:
+        body = per_device
     return jax.shard_map(
-        per_device,
+        body,
         mesh=mesh,
         in_specs=(
             P("fsdp", "tp", None),

time: 1340 us -> 662 us (0.49)
  matrix products: 381 us -> 0 us
  Pallas kernels: 0 us -> 270 us
  waiting for transfers between devices: 571 us -> 301 us
  blocking collectives: 204 us -> 0 us
  other arithmetic: 133 us -> 17.8 us
  starting transfers between devices: 2.31 us -> 27 us
    dot_general x24 -> x0, matrix products: 381 us -> none  [the longest x1 50.4 us: attend_back(): jnp.einsum('qhe,khe->hqk', context_grad, value_rows, preferred_element_ty...]
    pallas_call x0 -> x16, Pallas kernels: none -> 270 us  [the longest x2 64.9 us: feed(): pl.pallas_call(feed_kernel, out_shape=(jax.ShapeDtypeStruct((rows, units)...]
    reduce_scatter x10 -> x4, waiting for transfers between devices: 312 us -> 83.1 us  [the longest x3 83.1 us: scatter(): lax.psum_scatter(grad, 'fsdp', scatter_dimension=0, tiled=True)]
    unnamed x4 -> x0, blocking collectives: 204 us -> none
    all_gather x10 -> x3, waiting for transfers between devices: 255 us -> 100 us  [the longest x1 52.7 us: per_device_pair(): reduce_all = lax.all_gather(w_reduce.T, 'fsdp', axis=0, tiled=True)]
    ppermute x0 -> x20, waiting for transfers between devices: none -> 116 us  [the longest x12 101 us: swap_tp(): return lax.ppermute(piece, 'tp', [(0, 1), (1, 0)])]
    convert_element_type x23 -> x1, other arithmetic: 83.2 us -> 1.96 us  [scatter(): lax.psum_scatter(grad, 'fsdp', scatter_dimension=0, tiled=True)]
    reduce_sum x10 -> x2, other arithmetic: 48.6 us -> 1.91 us  [the longest x1 1.28 us: per_device_pair(): length = jnp.sum(jnp.where(every_clip == clip_id, clip_lengths, 0))]
  transfers between devices with their start and end apart: 20 -> 27, of which waited for: 14 -> 18; matrix products, arithmetic and copies ran while one was open for 35% -> 5% of each run, Pallas kernels for 0% -> 33%
where the time goes in v1:
time: 662 us; the launch traced here: 653 us
  waiting for transfers between devices  301 us (45%)
  Pallas kernels  270 us (41%)
  starting transfers between devices  27 us (4%)
  local copies, waits for them, and re-layouts  22.5 us (3%)
  other arithmetic  17.8 us (3%)
  between operations  15.2 us (2%)
    ppermute x12, waiting for transfers between devices, swap_tp(): return lax.ppermute(piece, 'tp', [(0, 1), (1, 0)])  101 us
    reduce_scatter x3, waiting for transfers between devices, scatter(): lax.psum_scatter(grad, 'fsdp', scatter_dimension=0, tiled=True)  83.1 us
    pallas_call x2, Pallas kernels, feed(): pl.pallas_call(feed_kernel, out_shape=(jax.ShapeDtypeStruct((rows, units)...  64.9 us
    all_gather x1, waiting for transfers between devices, per_device_pair(): reduce_all = lax.all_gather(w_reduce.T, 'fsdp', axis=0, tiled=True)  52.7 us
    pallas_call x1, Pallas kernels, attend_back_rows(): pl.pallas_call(attend_back_kernel, out_shape=(jax.ShapeDtypeStruct((heads...  52.7 us
    pallas_call x3, Pallas kernels, weight_grad(): pl.pallas_call(functools.partial(weight_grad_kernel, len(lefts), scale_co...  44.7 us
    pallas_call x2, Pallas kernels, attend_rows(): pl.pallas_call(attend_kernel, out_shape=(jax.ShapeDtypeStruct((heads, HD,...  30.8 us
    all_gather x1, waiting for transfers between devices, per_device_pair(): lax.all_gather(jnp.concatenate([w_query, w_key, w_value], axis=1), 'fsdp'...  25.8 us
  transfers between devices with their start and end apart: 27, of which 18 were waited for; matrix products, arithmetic and copies ran while one was open for 5% of the time, Pallas kernels for 33%

profile of v1, /device:TPU:0, one launch (start us, length us, event | category | flops | bytes accessed | tf_op | source)
XLA Modules:
  0.0 653.0 jit_solution(11989740326855331614)
XLA Ops:
  9.3 3.0 collective-permute-start.7
  12.3 3.1 collective-permute-done.7
  42.4 25.8 %all-gather.4.cloned.1.call-done.weight_ref = bf16[1280,1920]{1,0:T(8,128)(2,1)} async-done(((bf16[80,1920]{1,0:T(8,128)(2,1)}), bf16[1280,1920]{1,0:T(8,128)(2,1)}) %all-gather.4.cloned.1.call-update) | async-done | bytes 4915216 | tf_op jit(solution)/shard_map/all_gather | solution.py:918
  68.2 10.3 %project.2 = (bf16[752,1280]{1,0:T(8,128)(2,1)}, bf16[8,752,128]{2,1,0:T(8,128)(2,1)}, bf16[8,752,128]{2,1,0:T(8,128)(2,1)}, bf16[8,752,128]{2,1,0:T(8,128)(2,1)}) custom-call(s32[2]{0:T(128)} %pad_add_fusion.scal_ref, bf16[752,1280]{1,0:T(8,128)(2,1)} %bitcast.32, f32[1,1280]{1,0:T(1,128)} %squeeze.41.gain_ref, f32[1,1280]{1,0:T(1,128)} %squeeze.42.shift_ref, ...), custom_call_target="tpu_custom_call" | custom-call | flops 3696230400 | bytes 8765440 | tf_op jit(solution)/shard_map/project/pallas_call | solution.py:403
  78.5 10.3 %project.3 = (bf16[752,1280]{1,0:T(8,128)(2,1)}, bf16[8,752,128]{2,1,0:T(8,128)(2,1)}, bf16[8,752,128]{2,1,0:T(8,128)(2,1)}, bf16[8,752,128]{2,1,0:T(8,128)(2,1)}) custom-call(s32[2]{0:T(128)} %pad_add_fusion.1.scal_ref, bf16[752,1280]{1,0:T(8,128)(2,1)} %collective-permute-done.5.frames_ref, f32[1,1280]{1,0:T(1,128)} %squeeze.41.gain_ref, ...), custom_call_target="tpu_custom_call" | custom-call | flops 3696230400 | bytes 8765440 | tf_op jit(solution)/shard_map/project/pallas_call | solution.py:403
  88.8 15.5 %attend.3 = (bf16[8,80,752]{2,1,0:T(8,128)(2,1)}, f32[8,1,752]{2,1,0:T(1,128)}) custom-call(bf16[8,752,128]{2,1,0:T(8,128)(2,1)} %get-tuple-element.66.q_ref.qt_ref, bf16[8,752,128]{2,1,0:T(8,128)(2,1)} %get-tuple-element.61.ko_ref, bf16[8,752,128]{2,1,0:T(8,128)(2,1)} %get-tuple-element.62.kt_ref, bf16[8,752,128]{2,1,0:T(8,128)(2,1)} %get-tuple-element.63.vo_ref, ...), custom_call_target="tpu_custom_call" | custom-call | flops 14476902400 | bytes 9240576 | tf_op jit(solution)/shard_map/attend/pallas_call | solution.py:452
  107.8 15.3 %attend.2 = (bf16[8,80,752]{2,1,0:T(8,128)(2,1)}, f32[8,1,752]{2,1,0:T(1,128)}) custom-call(bf16[8,752,128]{2,1,0:T(8,128)(2,1)} %get-tuple-element.60.q_ref.qo_ref, bf16[8,752,128]{2,1,0:T(8,128)(2,1)} %get-tuple-element.61.ko_ref, bf16[8,752,128]{2,1,0:T(8,128)(2,1)} %get-tuple-element.62.kt_ref, bf16[8,752,128]{2,1,0:T(8,128)(2,1)} %get-tuple-element.63.vo_ref, ...), custom_call_target="tpu_custom_call" | custom-call | flops 14476902400 | bytes 9240576 | tf_op jit(solution)/shard_map/attend/pallas_call | solution.py:452
  123.0 6.8 %collective-permute-done.6 = bf16[640,752]{0,1:T(8,128)(2,1)S(1)} collective-permute-done((bf16[640,752]{0,1:T(8,128)(2,1)S(1)}, bf16[640,752]{0,1:T(8,128)(2,1)S(1)}, u32[]{:S(2)}, u32[]{:S(2)}) %collective-permute-start.6) | collective-permute-done | bytes 962592 | tf_op jit(solution)/shard_map/ppermute | solution.py:867
  131.6 21.9 %all-gather.6.cloned.1.call-done.weight_ref.expand_ref = bf16[1280,3840]{1,0:T(8,128)(2,1)} async-done(((bf16[80,3840]{1,0:T(8,128)(2,1)}), bf16[1280,3840]{1,0:T(8,128)(2,1)}) %all-gather.6.cloned.1.call-update) | async-done | bytes 9830416 | tf_op jit(solution)/shard_map/all_gather | solution.py:937
  153.5 9.0 %merge_heads.1 = (f32[752,1280]{1,0:T(8,128)}, bf16[752,1280]{1,0:T(8,128)(2,1)}) custom-call(bf16[640,752]{1,0:T(8,128)(2,1)} %bitcast.42, bf16[640,752]{1,0:T(8,128)(2,1)} %copy.39.ct_ref, bf16[1280,3840]{1,0:T(8,128)(2,1)} %all-gather.6.cloned.1.call-done.weight_ref.expand_ref, bf16[752,1280]{1,0:T(8,128)(2,1)} %bitcast.33, f32[1,1280]{1,0:T(1,128)} %squeeze.44.bias_ref, ...), custom_call_target="tpu_custom_call" | custom-call | flops 2464153600 | bytes 12902400 | tf_op jit(solution)/shard_map/merge_heads/pallas_call | solution.py:568
  164.7 52.7 %all-gather.8.cloned.1.call-done.reduce_ref = bf16[1280,2560]{1,0:T(8,128)(2,1)} async-done(((bf16[80,2560]{1,0:T(8,128)(2,1)}), bf16[1280,2560]{1,0:T(8,128)(2,1)}) %all-gather.8.cloned.1.call-update) | async-done | bytes 6553616 | tf_op jit(solution)/shard_map/all_gather | solution.py:941
  218.7 32.6 %feed.3 = (bf16[752,2560]{1,0:T(8,128)(2,1)}, bf16[752,2560]{1,0:T(8,128)(2,1)}, f32[1,2560]{1,0:T(1,128)}, bf16[752,1280]{1,0:T(8,128)(2,1)}, bf16[752,1280]{1,0:T(8,128)(2,1)}) custom-call(bf16[752,1280]{1,0:T(8,128)(2,1)} %copy-done.22, bf16[752,1280]{1,0:T(8,128)(2,1)} %collective-permute-done.9.grad_ref.refs_1_, ...), custom_call_target="tpu_custom_call" | custom-call | flops 19713228800 | bytes 36208640 | tf_op jit(solution)/shard_map/feed/pallas_call | solution.py:636
  252.8 32.3 %feed.2 = (bf16[752,2560]{1,0:T(8,128)(2,1)}, bf16[752,2560]{1,0:T(8,128)(2,1)}, f32[1,2560]{1,0:T(1,128)}, bf16[752,1280]{1,0:T(8,128)(2,1)}, bf16[752,1280]{1,0:T(8,128)(2,1)}) custom-call(bf16[752,1280]{1,0:T(8,128)(2,1)} %get-tuple-element.69.second_ref.refs_0_, bf16[752,1280]{1,0:T(8,128)(2,1)} %bitcast.38, ...), custom_call_target="tpu_custom_call" | custom-call | flops 19713228800 | bytes 36208640 | tf_op jit(solution)/shard_map/feed/pallas_call | solution.py:636
  285.1 10.6 %collective-permute-done.11.far_ref = bf16[752,1280]{1,0:T(8,128)(2,1)S(1)} collective-permute-done((bf16[752,1280]{1,0:T(8,128)(2,1)}, bf16[752,1280]{1,0:T(8,128)(2,1)S(1)}, u32[]{:S(2)}, u32[]{:S(2)}) %collective-permute-start.11) | collective-permute-done | bytes 1925152 | tf_op jit(solution)/shard_map/ppermute | solution.py:867
  297.0 12.1 %branch_back.1 = (f32[752,1280]{1,0:T(8,128)}, bf16[752,1280]{1,0:T(8,128)(2,1)}, bf16[640,752]{1,0:T(8,128)(2,1)}, bf16[640,752]{1,0:T(8,128)(2,1)}, f32[4,1280]{1,0:T(4,128)}) custom-call(bf16[752,1280]{1,0:T(8,128)(2,1)} %get-tuple-element.72.own_ref, bf16[752,1280]{1,0:T(8,128)(2,1)} %copy-done.2, f32[752,1280]{1,0:T(8,128)} %get-tuple-element.68.middle_ref, ...), custom_call_target="tpu_custom_call" | custom-call | flops 2464153600 | bytes 17326080 | tf_op jit(solution)/shard_map/branch_back/pallas_call | solution.py:736
  309.1 7.1 %out_weight_grad.1 = bf16[1280,1280]{1,0:T(8,128)(2,1)} custom-call(bf16[752,1280]{1,0:T(8,128)(2,1)} %get-tuple-element.98.branch_ref, bf16[640,752]{1,0:T(8,128)(2,1)} %bitcast.43, bf16[640,752]{1,0:T(8,128)(2,1)} %copy.39.ct_ref), custom_call_target="tpu_custom_call" | custom-call | flops 2464153600 | bytes 7127040 | tf_op jit(solution)/shard_map/out_weight_grad/pallas_call | solution.py:764
  316.3 15.1 %weight_grad.4 = bf16[1280,2560]{1,0:T(8,128)(2,1)} custom-call(bf16[752,1280]{1,0:T(8,128)(2,1)} %get-tuple-element.69.second_ref.refs_0_, bf16[752,1280]{1,0:T(8,128)(2,1)} %copy-done.22, bf16[752,2560]{1,0:T(8,128)(2,1)} %get-tuple-element.99.refs_2_, bf16[752,2560]{1,0:T(8,128)(2,1)} %get-tuple-element.100.refs_3_), custom_call_target="tpu_custom_call" | custom-call | flops 9856614400 | bytes 18104320 | tf_op jit(solution)/shard_map/weight_grad/pallas_call | solution.py:670
  331.5 15.4 %weight_grad.5 = bf16[1280,2560]{1,0:T(8,128)(2,1)} custom-call(bf16[752,1280]{1,0:T(8,128)(2,1)} %bitcast.40, bf16[752,1280]{1,0:T(8,128)(2,1)} %collective-permute-done.9.grad_ref.refs_1_, bf16[752,2560]{1,0:T(8,128)(2,1)} %get-tuple-element.101.refs_2_, bf16[752,2560]{1,0:T(8,128)(2,1)} %get-tuple-element.102.refs_3_), custom_call_target="tpu_custom_call" | custom-call | flops 9856614400 | bytes 18104320 | tf_op jit(solution)/shard_map/weight_grad/pallas_call | solution.py:670
  350.8 21.2 %collective-permute-done.12 = bf16[640,752]{0,1:T(8,128)(2,1)S(1)} collective-permute-done((bf16[640,752]{0,1:T(8,128)(2,1)S(1)}, bf16[640,752]{0,1:T(8,128)(2,1)S(1)}, u32[]{:S(2)}, u32[]{:S(2)}) %collective-permute-start.12) | collective-permute-done | bytes 962592 | tf_op jit(solution)/shard_map/ppermute | solution.py:867
  373.8 52.7 %attend_back.1 = (bf16[8,752,128]{2,1,0:T(8,128)(2,1)}, bf16[8,752,128]{2,1,0:T(8,128)(2,1)}, bf16[8,752,128]{2,1,0:T(8,128)(2,1)}, bf16[8,752,128]{2,1,0:T(8,12...) custom-call(bf16[8,752,128]{2,1,0:T(8,128)(2,1)} %get-tuple-element.60.q_ref.qo_ref, ...), custom_call_target="tpu_custom_call" | custom-call | flops 32573030400 | bytes 18481152 | tf_op jit(solution)/shard_map/attend_back/pallas_call | solution.py:527
  426.5 10.7 %first_back.2 = (bf16[752,1920]{1,0:T(8,128)(2,1)}, bf16[752,1280]{1,0:T(8,128)(2,1)}, f32[2,1280]{1,0:T(2,128)}, f32[1,1920]{1,0:T(1,128)}) custom-call(bf16[8,752,128]{2,1,0:T(8,128)(2,1)} %get-tuple-element.78.dq_ref, bf16[8,752,128]{2,1,0:T(8,128)(2,1)} %get-tuple-element.79.dk_ref, bf16[8,752,128]{2,1,0:T(8,128)(2,1)} %get-tuple-element.80.dv_ref, ...), custom_call_target="tpu_custom_call" | custom-call | flops 3696230400 | bytes 9535488 | tf_op jit(solution)/shard_map/first_back/pallas_call | solution.py:817
  437.1 10.8 %first_back.3 = (bf16[752,1920]{1,0:T(8,128)(2,1)}, bf16[752,1280]{1,0:T(8,128)(2,1)}, f32[2,1280]{1,0:T(2,128)}, f32[1,1920]{1,0:T(1,128)}) custom-call(bf16[8,752,128]{2,1,0:T(8,128)(2,1)} %get-tuple-element.82.dq_ref, bf16[8,752,128]{2,1,0:T(8,128)(2,1)} %get-tuple-element.83.dk_ref, bf16[8,752,128]{2,1,0:T(8,128)(2,1)} %get-tuple-element.84.dv_ref, ...), custom_call_target="tpu_custom_call" | custom-call | flops 3696230400 | bytes 9535488 | tf_op jit(solution)/shard_map/first_back/pallas_call | solution.py:817
  448.0 14.2 %weight_grad.3 = bf16[1280,1920]{1,0:T(8,128)(2,1)} custom-call(bf16[752,1280]{1,0:T(8,128)(2,1)} %get-tuple-element.87.refs_0_, bf16[752,1280]{1,0:T(8,128)(2,1)} %get-tuple-element.88.refs_1_, bf16[752,1920]{1,0:T(8,128)(2,1)} %get-tuple-element.89.refs_2_, bf16[752,1920]{1,0:T(8,128)(2,1)} %get-tuple-element.90.refs_3_), custom_call_target="tpu_custom_call" | custom-call | flops 7392460800 | bytes 14540800 | tf_op jit(solution)/shard_map/weight_grad/pallas_call | solution.py:670
  466.8 4.8 collective-permute-done.14
  471.7 3.6 collective-permute-done.15
  476.6 2.5 collective-permute-done.16
  479.1 28.4 %collective-permute-done.10 = bf16[752,1280]{1,0:T(8,128)(2,1)} collective-permute-done((bf16[752,1280]{1,0:T(8,128)(2,1)}, bf16[752,1280]{1,0:T(8,128)(2,1)}, u32[]{:S(2)}, u32[]{:S(2)}) %collective-permute-start.10) | collective-permute-done | bytes 1925152 | tf_op jit(solution)/shard_map/ppermute | solution.py:867
  507.6 4.6 fusion
  515.1 31.4 %collective-permute-done.19 = f32[240]{0:T(256)S(1)} collective-permute-done((f32[240]{0:T(256)S(1)}, f32[240]{0:T(256)S(1)}, u32[]{:S(2)}, u32[]{:S(2)}) %collective-permute-start.19) | collective-permute-done | bytes 992 | tf_op jit(solution)/shard_map/ppermute | solution.py:867
  549.5 6.6 %frames_back.1 = bf16[752,1280]{1,0:T(8,128)(2,1)} custom-call(bf16[752,1280]{1,0:T(8,128)(2,1)} %bitcast.35, bf16[752,1280]{1,0:T(8,128)(2,1)} %get-tuple-element.81.own_ref, bf16[752,1280]{1,0:T(8,128)(2,1)} %collective-permute-done.13.far_ref, f32[752,1280]{1,0:T(8,128)} %get-tuple-element.86.mgrad_ref, f32[1,1280]{1,0:T(1,128)} %squeeze.41.gain_ref), custom_call_target="tpu_custom_call" | custom-call | flops 19251200 | bytes 11550720 | tf_op jit(solution)/shard_map/frames_back/pallas_call | solution.py:854
  558.7 4.1 reduce-scatter.11.cloned.1.call-done
  564.8 79.0 %reduce-scatter.5.cloned.1.call-done = bf16[80,1920]{1,0:T(8,128)(2,1)} async-done(((bf16[1280,1920]{1,0:T(8,128)(2,1)}), bf16[80,1920]{1,0:T(8,128)(2,1)}) %reduce-scatter.5.cloned.1.call-update) | async-done | bytes 307216 | tf_op jit(solution)/shard_map/reduce_scatter | solution.py:991
  (163 shorter events, 64.5 us)
Async XLA Ops:
  7.3 12.9 %copy-start = (bf16[1,752,1280]{2,1,0:T(8,128)(2,1)S(1)}, bf16[1,752,1280]{2,1,0:T(8,128)(2,1)}, u32[]{:S(2)}) copy-start(bf16[1,752,1280]{2,1,0:T(8,128)(2,1)} %param.19) | copy-start | bytes 5775364
  7.3 15.0 %copy-start.23 = (s32[16]{0:T(128)S(1)}, s32[16]{0:T(128)}, u32[]{:S(2)}) copy-start(s32[16]{0:T(128)} %param.22) | copy-start | bytes 196
  7.3 17.8 %copy-start.24 = (s32[16]{0:T(128)S(1)}, s32[16]{0:T(128)}, u32[]{:S(2)}) copy-start(s32[16]{0:T(128)} %param.21) | copy-start | bytes 196
  7.3 60.9 %all-gather.4.cloned.1.call-start = ((), (), s32[]{:S(2)}) async-start(), calls=%async_computation.4 | async-start | bytes 5222400 | tf_op jit(solution)/shard_map/all_gather | solution.py:918
  9.3 144.2 %all-gather.6.cloned.1.call-start = ((), (), s32[]{:S(2)}) async-start(), calls=%async_computation.5 | async-start | bytes 10444800 | tf_op jit(solution)/shard_map/all_gather | solution.py:937
  9.3 6.1 collective-permute-start.7
  17.4 200.1 %all-gather.8.cloned.1.call-start = ((), (), s32[]{:S(2)}) async-start(), calls=%async_computation.6 | async-start | bytes 6963200 | tf_op jit(solution)/shard_map/all_gather | solution.py:941
  18.1 528.4 %reduce-scatter.7.cloned.1.call-start = ((), (), s32[]{:S(2)}) async-start(), calls=%async_computation.8 | async-start | bytes 3481600 | tf_op jit(solution)/shard_map/reduce_scatter | solution.py:994
  18.3 3.9 collective-permute-start
  20.2 58.3 %collective-permute-start.5 = (bf16[752,1280]{1,0:T(8,128)(2,1)S(1)}, bf16[752,1280]{1,0:T(8,128)(2,1)}, u32[]{:S(2)}, u32[]{:S(2)}) collective-permute-start(bf16[752,1280]{1,0:T(8,128)(2,1)S(1)} %bitcast.36), channel_id=1, source_target_pairs={{0,1},{1,0},{2,3},{3,2},{4,5},{5,4},{6,7},{7,6},{8,9},{9,8},{10,11... | collective-permute-start | bytes 5775368 | tf_op jit(solution)/shard_map/ppermute | solution.py:867
  20.4 144.3 %collective-permute-start.9 = (bf16[752,1280]{1,0:T(8,128)(2,1)}, bf16[752,1280]{1,0:T(8,128)(2,1)}, u32[]{:S(2)}, u32[]{:S(2)}) collective-permute-start(bf16[752,1280]{1,0:T(8,128)(2,1)} %bitcast.37), channel_id=1, source_target_pairs={{0,1},{1,0},{2,3},{3,2},{4,5},{5,4},{6,7},{7,6},{8,9},{9,8},{10,11... | collective-permute-start | bytes 5775368 | tf_op jit(solution)/shard_map/ppermute | solution.py:867
  22.2 1.2 collective-permute-start.1
  23.5 3.7 collective-permute-start.2
  27.2 4.0 collective-permute-start.3
  31.3 5.3 collective-permute-start.4
  106.3 23.5 %collective-permute-start.6 = (bf16[640,752]{0,1:T(8,128)(2,1)S(1)}, bf16[640,752]{0,1:T(8,128)(2,1)S(1)}, u32[]{:S(2)}, u32[]{:S(2)}) collective-permute-start(bf16[640,752]{0,1:T(8,128)(2,1)S(1)} %copy.38), channel_id=1, source_target_pairs={{0,1},{1,0},{2,3},{3,2},{4,5},{5,4},{6,7},{7,6},{8,9},{9,8},{10,11... | collective-permute-start | bytes 2887688 | tf_op jit(solution)/shard_map/ppermute | solution.py:867
  162.5 54.9 %collective-permute-start.8 = (bf16[752,1280]{1,0:T(8,128)(2,1)}, bf16[752,1280]{1,0:T(8,128)(2,1)S(1)}, u32[]{:S(2)}, u32[]{:S(2)}) collective-permute-start(bf16[752,1280]{1,0:T(8,128)(2,1)} %get-tuple-element.69.second_ref.refs_0_), channel_id=1, source_target_pairs={{0,1},{1,0},{2,3},{3,2},{4,5},{5,4},{6,7},{7,6},{8,9},{9,8},{10,11... | collective-permute-start | bytes 5775368 | tf_op jit(solution)/shard_map/ppermute | solution.py:867
  251.3 44.4 %collective-permute-start.11 = (bf16[752,1280]{1,0:T(8,128)(2,1)}, bf16[752,1280]{1,0:T(8,128)(2,1)S(1)}, u32[]{:S(2)}, u32[]{:S(2)}) collective-permute-start(bf16[752,1280]{1,0:T(8,128)(2,1)} %get-tuple-element.73), channel_id=1, source_target_pairs={{0,1},{1,0},{2,3},{3,2},{4,5},{5,4},{6,7},{7,6},{8,9},{9,8},{10,11... | collective-permute-start | bytes 5775368 | tf_op jit(solution)/shard_map/ppermute | solution.py:867
  316.2 240.5 %reduce-scatter.9.cloned.1.call-start = ((), (), s32[]{:S(2)}) async-start(), calls=%async_computation.9 | async-start | bytes 6963200 | tf_op jit(solution)/shard_map/reduce_scatter | solution.py:991
  331.4 231.4 %reduce-scatter.11.cloned.1.call-start = ((), (), s32[]{:S(2)}) async-start(), calls=%async_computation.10 | async-start | bytes 6963200 | tf_op jit(solution)/shard_map/reduce_scatter | solution.py:991
  346.8 296.9 %reduce-scatter.5.cloned.1.call-start = ((), (), s32[]{:S(2)}) async-start(), calls=%async_computation.7 | async-start | bytes 5222400 | tf_op jit(solution)/shard_map/reduce_scatter | solution.py:991
  349.3 22.7 %collective-permute-start.12 = (bf16[640,752]{0,1:T(8,128)(2,1)S(1)}, bf16[640,752]{0,1:T(8,128)(2,1)S(1)}, u32[]{:S(2)}, u32[]{:S(2)}) collective-permute-start(bf16[640,752]{0,1:T(8,128)(2,1)S(1)} %copy.40), channel_id=1, source_target_pairs={{0,1},{1,0},{2,3},{3,2},{4,5},{5,4},{6,7},{7,6},{8,9},{9,8},{10,11... | collective-permute-start | bytes 2887688 | tf_op jit(solution)/shard_map/ppermute | solution.py:867
  462.2 13.6 %copy-start.5 = (f32[32,40]{1,0:T(8,128)S(1)}, f32[32,40]{1,0:T(8,128)}, u32[]{:S(2)}) copy-start(f32[32,40]{1,0:T(8,128)} %get-tuple-element.103) | copy-start | bytes 15364
  462.3 45.3 %copy-start.1 = (bf16[752,1280]{1,0:T(8,128)(2,1)S(1)}, bf16[752,1280]{1,0:T(8,128)(2,1)}, u32[]{:S(2)}) copy-start(bf16[752,1280]{1,0:T(8,128)(2,1)} %get-tuple-element.70) | copy-start | bytes 5775364
  462.3 45.3 %collective-permute-start.10 = (bf16[752,1280]{1,0:T(8,128)(2,1)}, bf16[752,1280]{1,0:T(8,128)(2,1)}, u32[]{:S(2)}, u32[]{:S(2)}) collective-permute-start(bf16[752,1280]{1,0:T(8,128)(2,1)} %get-tuple-element.71), channel_id=1, source_target_pairs={{0,1},{1,0},{2,3},{3,2},{4,5},{5,4},{6,7},{7,6},{8,9},{9,8},{10,11... | collective-permute-start | bytes 5775368 | tf_op jit(solution)/shard_map/ppermute | solution.py:867
  464.7 6.8 %collective-permute-start.14 = (f32[8,720]{1,0:T(8,128)S(1)}, f32[8,720]{1,0:T(8,128)S(1)}, u32[]{:S(2)}, u32[]{:S(2)}) collective-permute-start(f32[8,720]{1,0:T(8,128)S(1)} %slice_select_fusion), channel_id=1, source_target_pairs={{0,16},{2,18},{4,20},{6,22},{8,24},{10,26},{12,28},{14,30},{16,0},... | collective-permute-start | bytes 69128 | tf_op jit(solution)/shard_map/ppermute | solution.py:891
  471.5 3.8 collective-permute-start.15
  475.3 3.7 collective-permute-start.16
  475.9 73.6 %collective-permute-start.13 = (bf16[752,1280]{1,0:T(8,128)(2,1)}, bf16[752,1280]{1,0:T(8,128)(2,1)}, u32[]{:S(2)}, u32[]{:S(2)}) collective-permute-start(bf16[752,1280]{1,0:T(8,128)(2,1)} %get-tuple-element.85), channel_id=1, source_target_pairs={{0,1},{1,0},{2,3},{3,2},{4,5},{5,4},{6,7},{7,6},{8,9},{9,8},{10,11... | collective-permute-start | bytes 5775368 | tf_op jit(solution)/shard_map/ppermute | solution.py:867
  479.0 33.1 %collective-permute-start.17 = (f32[1,720]{1,0:T(1,128)S(1)}, f32[1,720]{1,0:T(1,128)S(1)}, u32[]{:S(2)}, u32[]{:S(2)}) collective-permute-start(f32[1,720]{1,0:T(1,128)S(1)} %broadcast_select_fusion.1), channel_id=1, source_target_pairs={{0,2},{2,0},{4,6},{6,4},{8,10},{10,8},{12,14},{14,12},{16,18},{18,... | collective-permute-start | bytes 8648 | tf_op jit(solution)/shard_map/ppermute | solution.py:891
  512.3 34.2 %collective-permute-start.19 = (f32[240]{0:T(256)S(1)}, f32[240]{0:T(256)S(1)}, u32[]{:S(2)}, u32[]{:S(2)}) collective-permute-start(f32[240]{0:T(256)S(1)} %bitcast.54), channel_id=1, source_target_pairs={{0,1},{1,0},{2,3},{3,2},{4,5},{5,4},{6,7},{7,6},{8,9},{9,8},{10,11... | collective-permute-start | bytes 2888 | tf_op jit(solution)/shard_map/ppermute | solution.py:867
  547.4 8.6 %collective-permute-start.18 = (bf16[80,640]{1,0:T(8,128)(2,1)S(1)}, bf16[80,640]{1,0:T(8,128)(2,1)S(1)}, u32[]{:S(2)}, u32[]{:S(2)}) collective-permute-start(bf16[80,640]{1,0:T(8,128)(2,1)S(1)} %slice.201), channel_id=1, source_target_pairs={{0,1},{1,0},{2,3},{3,2},{4,5},{5,4},{6,7},{7,6},{8,9},{9,8},{10,11... | collective-permute-start | bytes 307208 | tf_op jit(solution)/shard_map/ppermute | solution.py:867
  (20 other events, 121.5 us)
Sparse Core Ops, SparseCore 0:
  10.9 57.2 all-gather.3
  71.1 82.3 all-gather.5
  155.8 61.5 all-gather.7
  316.4 65.3 reduce-scatter.6
  386.1 87.2 reduce-scatter.8
  477.2 85.5 reduce-scatter.10
  567.3 76.3 reduce-scatter.4

commit v2 on v1

--- a/solution.py
+++ b/solution.py
@@ -312,6 +312,7 @@
 
 VMEM_LIMIT = 60 << 20
 PAD = 128
+COST = 3.0
 
 
 def kernel_params():
@@ -319,7 +320,7 @@
 
 
 def cost(flops, moved):
-    return pl.CostEstimate(flops=int(flops), bytes_accessed=int(moved), transcendentals=0)
+    return pl.CostEstimate(flops=int(COST * flops), bytes_accessed=int(moved), transcendentals=0)
 
 
 def row_pieces(rows, size):
@@ -469,14 +470,15 @@
 
 def attend_back_kernel(
     qo_ref, qt_ref, ko_ref, kt_ref, vo_ref, vt_ref, go_ref, gt_ref, lo_ref, lt_ref,
-    dqo_ref, dqt_ref, dko_ref, dkt_ref, dvo_ref, dvt_ref,
+    own_ref, far_ref, dq_ref,
 ):
     rows = qo_ref.shape[1]
+    cols = own_ref.shape[1] // 3
     keys = jnp.concatenate([ko_ref[0], kt_ref[0]], axis=0)
     values = jnp.concatenate([vo_ref[0], vt_ref[0]], axis=0)
     keys_turned = keys.T[:HD]
     pieces = [(side, start, size) for side in range(2) for start, size in row_pieces(rows, 256)]
-    sides = ((qo_ref, go_ref, lo_ref, dqo_ref), (qt_ref, gt_ref, lt_ref, dqt_ref))
+    sides = ((qo_ref, go_ref, lo_ref), (qt_ref, gt_ref, lt_ref))
 
     def query(piece):
         side, start, size = piece
@@ -509,27 +511,35 @@
         key_part = dot_nn(score_grad, query(piece))
         query_grad = dot_nn(keys_turned, score_grad)
         side, start, size = piece
-        sides[side][3][0, start : start + size, :HD] = query_grad.T.astype(jnp.bfloat16)
+        dq_ref[side * rows + start : side * rows + start + size, :] = query_grad.T.astype(jnp.bfloat16)
         total_v = value_part if total_v is None else total_v + value_part
         total_k = key_part if total_k is None else total_k + key_part
         current = coming
-    dko_ref[0] = total_k[:rows].astype(jnp.bfloat16)
-    dkt_ref[0] = total_k[rows:].astype(jnp.bfloat16)
-    dvo_ref[0, :, :HD] = total_v[:rows].astype(jnp.bfloat16)
-    dvt_ref[0, :, :HD] = total_v[rows:].astype(jnp.bfloat16)
-
-
-def attend_back_rows(queries, keys, values, upstream, logs):
-    heads, rows, _ = queries[0].shape
-    spec = pl.BlockSpec((1, rows, PAD), lambda h: (h, 0, 0))
-    turned = pl.BlockSpec((1, HD, rows), lambda h: (h, 0, 0))
-    line = pl.BlockSpec((1, 1, rows), lambda h: (h, 0, 0))
+    key_grad = total_k[:, :HD].astype(jnp.bfloat16)
+    value_grad = total_v.astype(jnp.bfloat16)
+    for head in range(cols // HD):
+
+        @pl.when(pl.program_id(0) == head)
+        def _(head=head):
+            for part, grad in enumerate((dq_ref[...], key_grad, value_grad)):
+                take = slice(part * cols + head * HD, part * cols + (head + 1) * HD)
+                own_ref[:, take] = grad[:rows]
+                far_ref[:, take] = grad[rows:]
+
+
+def attend_back_rows(queries, keys, values, upstream, logs, start, heads):
+    rows = queries[0].shape[1]
+    spec = pl.BlockSpec((1, rows, PAD), lambda h: (h + start, 0, 0))
+    turned = pl.BlockSpec((1, HD, rows), lambda h: (h + start, 0, 0))
+    line = pl.BlockSpec((1, 1, rows), lambda h: (h + start, 0, 0))
+    packed = (rows, 3 * heads * HD)
     return pl.pallas_call(
         attend_back_kernel,
-        out_shape=(jax.ShapeDtypeStruct((heads, rows, PAD), jnp.bfloat16),) * 6,
+        out_shape=(jax.ShapeDtypeStruct(packed, jnp.bfloat16),) * 2,
         grid=(heads,),
         in_specs=[spec] * 6 + [turned] * 2 + [line] * 2,
-        out_specs=(spec,) * 6,
+        out_specs=(whole(packed),) * 2,
+        scratch_shapes=[pltpu.VMEM((2 * rows, HD), jnp.bfloat16)],
         compiler_params=kernel_params(),
         cost_estimate=cost(heads * 4 * rows * rows * 2 * 900, heads * rows * PAD * 24),
         name="attend_back",
@@ -537,16 +547,15 @@
 
 
 def merge_kernel(
-    co_ref, ct_ref, weight_ref, frames_ref, bias_ref, gain_ref, shift_ref, middle_ref, second_ref
+    co_ref, ct_ref, wo_ref, wt_ref, frames_ref, bias_ref, gain_ref, shift_ref, middle_ref, second_ref,
 ):
     rows = frames_ref.shape[0]
-    cols = co_ref.shape[0]
     own, far = co_ref[...].T, ct_ref[...].T
     pieces = row_pieces(rows, 256)
 
     def branch(piece):
         take = slice(piece[0], piece[0] + piece[1])
-        return dot_nt(own[take], weight_ref[:, :cols]) + dot_nt(far[take], weight_ref[:, cols:])
+        return dot_nt(own[take], wo_ref[...]) + dot_nt(far[take], wt_ref[...])
 
     def finish(piece, part):
         take = slice(piece[0], piece[0] + piece[1])
@@ -562,7 +571,7 @@
         current = coming
 
 
-def merge_heads(context_own, context_far, pack, slot, frames, bias, gain, shift):
+def merge_heads(context_own, context_far, pack, frames, bias, gain, shift):
     rows, width = frames.shape
     cols = context_own.shape[0]
     return pl.pallas_call(
@@ -573,14 +582,14 @@
         ),
         grid=(1,),
         in_specs=[
-            whole((cols, rows)), whole((cols, rows)), whole((width, 2 * cols), (0, slot)),
-            whole((rows, width)), whole((1, width)), whole((1, width)), whole((1, width)),
+            whole((cols, rows)), whole((cols, rows)), whole((width, cols), (0, 3)),
+            whole((width, cols), (0, 4)), whole((rows, width)), whole((1, width)), whole((1, width)), whole((1, width)),
         ],
         out_specs=(whole((rows, width)),) * 2,
         compiler_params=kernel_params(),
         cost_estimate=cost(4 * rows * width * cols, 10 * rows * width + 4 * width * cols),
         name="merge_heads",
-    )(context_own, context_far, pack, frames, bias, gain, shift)
+    )(context_own, context_far, pack, pack, frames, bias, gain, shift)
 
 
 def feed_kernel(
@@ -627,11 +636,15 @@
         terms_ref[...] = terms_acc[...].astype(jnp.bfloat16)
 
 
-def feed(second, grads, expand_pack, reduce_pack, bias, units):
+def feed(second, grads, pack, bias, units):
     rows, width = second.shape
     block = 512 if units % 512 == 0 else units
     wide = pl.BlockSpec((rows, block), lambda j: (0, j))
-    weight = pl.BlockSpec((width, block), lambda j: (0, j))
+    steps = units // block
+    weights = [
+        pl.BlockSpec((width, block), lambda j: (0, j)),
+        pl.BlockSpec((width, block), lambda j: (0, j + steps)),
+    ]
     line = pl.BlockSpec((1, block), lambda j: (0, j))
     return pl.pallas_call(
         feed_kernel,
@@ -643,49 +656,83 @@
             jax.ShapeDtypeStruct((rows, width), jnp.bfloat16),
         ),
         grid=(units // block,),
-        in_specs=[whole((rows, width)), whole((rows, width)), weight, weight, line],
+        in_specs=[whole((rows, width)), whole((rows, width)), *weights, line],
         out_specs=(wide, wide, line, whole((rows, width)), whole((rows, width))),
         scratch_shapes=[pltpu.VMEM((rows, width), jnp.float32)] * 2,
         compiler_params=kernel_params(),
         cost_estimate=cost(8 * rows * width * units, 8 * rows * (units + width) + 4 * width * units),
         name="feed",
-    )(second, grads, expand_pack, reduce_pack, bias)
-
-
-def weight_grad_kernel(count, scale_cols, scale, *refs):
-    lefts, rights, out_ref = refs[:count], refs[count : 2 * count], refs[2 * count]
-    total = None
-    for left, right in zip(lefts, rights):
-        part = dot_tn(left[...], right[...])
-        total = part if total is None else total + part
-    if scale_cols:
-        block = out_ref.shape[1]
-        total = total * jnp.where(pl.program_id(0) * block < scale_cols, scale, 1.0)
-    out_ref[...] = total.astype(jnp.bfloat16)
-
-
-def weight_grad(lefts, rights, block, scale_cols=0, scale=1.0):
-    width, units = lefts[0].shape[1], rights[0].shape[1]
-    rows = sum(left.shape[0] for left in lefts)
+    )(second, grads, pack, pack, bias)
+
+
+def feed_grad_kernel(go_ref, gt_ref, so_ref, st_ref, ho_ref, ht_ref, bo_ref, bt_ref, out_ref):
+    step = pl.program_id(0)
+    half = pl.num_programs(0) // 2
+
+    @pl.when(step < half)
+    def _():
+        total = dot_tn(go_ref[...], ho_ref[...]) + dot_tn(gt_ref[...], ht_ref[...])
+        out_ref[...] = total.astype(jnp.bfloat16)
+
+    @pl.when(step >= half)
+    def _():
+        total = dot_tn(so_ref[...], bo_ref[...]) + dot_tn(st_ref[...], bt_ref[...])
+        out_ref[...] = total.astype(jnp.bfloat16)
+
+
+def feed_grads(grads, second, hidden, back):
+    rows, width = grads[0].shape
+    units = hidden[0].shape[1]
+    block = 512 if units % 512 == 0 else units
+    steps = units // block
+    early = pl.BlockSpec((rows, block), lambda j: (0, jnp.minimum(j, steps - 1)))
+    late = pl.BlockSpec((rows, block), lambda j: (0, jnp.maximum(j - steps, 0)))
     return pl.pallas_call(
-        functools.partial(weight_grad_kernel, len(lefts), scale_cols, scale),
-        out_shape=jax.ShapeDtypeStruct((width, units), jnp.bfloat16),
-        grid=(units // block,),
-        in_specs=[whole(left.shape) for left in lefts]
-        + [pl.BlockSpec((right.shape[0], block), lambda j: (0, j)) for right in rights],
+        feed_grad_kernel,
+        out_shape=jax.ShapeDtypeStruct((width, 2 * units), jnp.bfloat16),
+        grid=(2 * steps,),
+        in_specs=[whole((rows, width))] * 4 + [early] * 2 + [late] * 2,
         out_specs=pl.BlockSpec((width, block), lambda j: (0, j)),
         compiler_params=kernel_params(),
-        cost_estimate=cost(2 * rows * width * units, 2 * (rows * (width + units) + width * units)),
-        name="weight_grad",
-    )(*lefts, *rights)
+        cost_estimate=cost(8 * rows * width * units, 8 * rows * (width + units) + 4 * width * units),
+        name="feed_grads",
+    )(*grads, *second, *hidden, *back)
+
+
+def head_grad_kernel(count, lo_ref, lt_ref, *refs):
+    out_ref = refs[2 * count]
+    offset = 0
+    for own_ref, far_ref in zip(refs[:count], refs[count : 2 * count]):
+        wide = own_ref.shape[1]
+        total = dot_tn(lo_ref[...], own_ref[...]) + dot_tn(lt_ref[...], far_ref[...])
+        lane = lax.broadcasted_iota(jnp.int32, (1, wide), 1)
+        total = total * jnp.where(lane < wide // 3, HD ** (-0.5), 1.0)
+        out_ref[:, offset : offset + wide] = total.astype(jnp.bfloat16)
+        offset += wide
+
+
+def head_grad(lefts, own, far):
+    rows, width = lefts[0].shape
+    units = sum(pack.shape[1] for pack in own)
+    block = 256 if width % 256 == 0 else width
+    left = pl.BlockSpec((rows, block), lambda j: (0, j))
+    return pl.pallas_call(
+        functools.partial(head_grad_kernel, len(own)),
+        out_shape=jax.ShapeDtypeStruct((width, units), jnp.bfloat16),
+        grid=(width // block,),
+        in_specs=[left] * 2 + [whole(pack.shape) for pack in (*own, *far)],
+        out_specs=pl.BlockSpec((block, units), lambda j: (j, 0)),
+        compiler_params=kernel_params(),
+        cost_estimate=cost(4 * rows * width * units, 4 * rows * (width + units) + 2 * width * units),
+        name="head_grad",
+    )(*lefts, *own, *far)
 
 
 def branch_kernel(
-    own_ref, far_ref, middle_ref, grad_ref, gain_ref, weight_ref,
+    own_ref, far_ref, middle_ref, grad_ref, gain_ref, wo_ref, wt_ref,
     mgrad_ref, branch_ref, go_ref, gt_ref, sums_ref,
 ):
     rows, width = middle_ref.shape
-    cols = go_ref.shape[0]
     pieces = row_pieces(rows, 256)
 
     def step_back(piece):
@@ -713,9 +760,8 @@
 
     def finish(piece, branch):
         take = slice(piece[0], piece[0] + piece[1])
-        out = dot_nn(branch, weight_ref[...]).astype(jnp.bfloat16).T
-        go_ref[:, take] = out[:cols]
-        gt_ref[:, take] = out[cols:]
+        go_ref[:, take] = dot_nn(branch, wo_ref[...]).astype(jnp.bfloat16).T
+        gt_ref[:, take] = dot_nn(branch, wt_ref[...]).astype(jnp.bfloat16).T
 
     totals = None
     branch, sums = step_back(pieces[0])
@@ -730,7 +776,7 @@
         sums_ref[index : index + 1, :] = line
 
 
-def branch_back(own, far, middle, grads, gain, pack, slot, cols):
+def branch_back(own, far, middle, grads, gain, pack, cols):
     rows, width = middle.shape
     full = whole((rows, width))
     return pl.pallas_call(
@@ -743,12 +789,14 @@
             jax.ShapeDtypeStruct((4, width), jnp.float32),
         ),
         grid=(1,),
-        in_specs=[full, full, full, full, whole((1, width)), whole((width, 2 * cols), (0, slot))],
+        in_specs=[
+            full, full, full, full, whole((1, width)), whole((width, cols), (0, 3)), whole((width, cols), (0, 4))
+        ],
         out_specs=(full, full, whole((cols, rows)), whole((cols, rows)), whole((4, width))),
         compiler_params=kernel_params(),
         cost_estimate=cost(4 * rows * width * cols, 18 * rows * width),
         name="branch_back",
-    )(own, far, middle, grads, gain, pack)
+    )(own, far, middle, grads, gain, pack, pack)
 
 
 def out_grad_kernel(branch_ref, co_ref, ct_ref, out_ref):
@@ -773,17 +821,19 @@
     )(branch, context_own, context_far)
 
 
-def first_kernel(
-    heads, dq_ref, dk_ref, dv_ref, weight_ref, frames_ref, pack_ref, terms_ref, sums_ref, bias_ref
-):
+def first_kernel(count, *refs):
+    packs, (weight_ref, frames_ref, terms_ref, sums_ref, bias_ref, pack_ref) = refs[:count], refs[count:]
     rows, width = frames_ref.shape
-    cols = heads * HD
+    cols = pack_ref.shape[1] // 3
     q_factor = HD ** (-0.5)
     pieces = row_pieces(rows, 256)
-    for part, ref in enumerate((dq_ref, dk_ref, dv_ref)):
-        for head in range(heads):
-            offset = part * cols + head * HD
-            pack_ref[:, offset : offset + HD] = ref[head, :, :HD]
+    offset = 0
+    for ref in packs:
+        wide = ref.shape[1] // 3
+        for part in range(3):
+            place = part * cols + offset
+            pack_ref[:, place : place + wide] = ref[:, part * wide : (part + 1) * wide]
+        offset += wide
 
     def begin(piece):
         take = slice(piece[0], piece[0] + piece[1])
@@ -810,27 +860,24 @@
     bias_ref[...] = totals[2]
 
 
-def first_back(dq, dk, dv, weights, frames):
-    heads, rows, _ = dq.shape
-    width = frames.shape[1]
-    cols = heads * HD
+def first_back(packs, weights, frames):
+    rows, width = frames.shape
+    wide = sum(pack.shape[1] for pack in packs)
     return pl.pallas_call(
-        functools.partial(first_kernel, heads),
+        functools.partial(first_kernel, len(packs)),
         out_shape=(
-            jax.ShapeDtypeStruct((rows, 3 * cols), jnp.bfloat16),
             jax.ShapeDtypeStruct((rows, width), jnp.bfloat16),
             jax.ShapeDtypeStruct((2, width), jnp.float32),
-            jax.ShapeDtypeStruct((1, 3 * cols), jnp.float32),
+            jax.ShapeDtypeStruct((1, wide), jnp.float32),
         ),
         grid=(1,),
-        in_specs=[whole(dq.shape)] * 3 + [whole((width, 3 * cols)), whole((rows, width))],
-        out_specs=(
-            whole((rows, 3 * cols)), whole((rows, width)), whole((2, width)), whole((1, 3 * cols))
-        ),
+        in_specs=[whole(pack.shape) for pack in packs] + [whole((width, wide)), whole((rows, width))],
+        out_specs=(whole((rows, width)), whole((2, width)), whole((1, wide))),
+        scratch_shapes=[pltpu.VMEM((rows, wide), jnp.bfloat16)],
         compiler_params=kernel_params(),
-        cost_estimate=cost(6 * rows * width * cols, 6 * heads * rows * PAD + 6 * width * cols),
+        cost_estimate=cost(2 * rows * width * wide, 2 * (rows + width) * wide + 4 * rows * width),
         name="first_back",
-    )(dq, dk, dv, weights, frames)
+    )(*packs, weights, frames)
 
 
 def frames_kernel(frames_ref, own_ref, far_ref, mgrad_ref, gain_ref, out_ref):
@@ -867,9 +914,12 @@
     return lax.ppermute(piece, "tp", [(0, 1), (1, 0)])
 
 
-def gather_steps(vector, fsdp):
+def tie(*values):
+    return lax.optimization_barrier(values)
+
+
+def gather_steps(vector, other, fsdp):
     index = lax.axis_index("fsdp")
-    other = swap_tp(vector)
     side = lax.axis_index("tp")
     held = jnp.where(side == 0, jnp.stack([vector, other]), jnp.stack([other, vector]))
     bit = 1
@@ -879,6 +929,27 @@
         held = jnp.where(low, jnp.concatenate([held, other]), jnp.concatenate([other, held]))
         bit *= 2
     return held
+
+
+def halving_order(fsdp):
+    return [bit for bit in (1, 2, 8, 4, 16, 32, 64, 128) if bit < fsdp]
+
+
+def halve(held, bit, left, fsdp, last=False):
+    index = lax.axis_index("fsdp")
+    mine = (index // bit) % 2
+    parts = held if isinstance(held, list) else [held]
+    outer = 2 ** sorted(left, reverse=True).index(bit)
+    views = [part.reshape(outer, 2, -1, part.shape[-1]) for part in parts]
+
+    def chosen(which):
+        return jnp.concatenate(
+            [lax.dynamic_index_in_dim(view, which, 1, keepdims=False) for view in views], axis=-1
+        )
+
+    other = lax.ppermute(chosen(1 - mine), "fsdp", [(i, i ^ bit) for i in range(fsdp)])
+    total = chosen(mine).astype(jnp.float32) + other.astype(jnp.float32)
+    return (total if last else total.astype(jnp.bfloat16)).reshape(-1, total.shape[-1])
 
 
 def scatter_steps(held, fsdp):
@@ -915,12 +986,22 @@
     scal_own = jnp.stack([length, side * rows]).astype(jnp.int32)
     scal_far = jnp.stack([length, (1 - side) * rows]).astype(jnp.int32)
 
-    qkv = lax.all_gather(
-        jnp.concatenate([w_query, w_key, w_value], axis=1), "fsdp", axis=0, tiled=True
-    )
-    frames_far = swap_tp(frames)
     wide_six = [first_gain, first_shift, second_gain, second_shift, b_out, b_reduce]
-    small = gather_steps(jnp.concatenate(wide_six + [b_query, b_value, b_expand]), fsdp)
+    small_own = jnp.concatenate(wide_six + [b_query, b_value, b_expand])
+    out_turned = w_out.T
+    small_far, out_other = swap_tp(small_own), swap_tp(out_turned)
+    pack_one = lax.all_gather(
+        jnp.concatenate([w_query, w_key, w_value, out_turned, out_other], axis=1),
+        "fsdp", axis=0, tiled=True,
+    )
+    pack_two = lax.all_gather(
+        jnp.concatenate([w_expand, w_reduce.T], axis=1), "fsdp", axis=0, tiled=True
+    )
+    sent_frames, small_far, out_other = tie(frames, small_far, out_other)
+    frames_far = swap_tp(sent_frames)
+    sent_grads, frames_far = tie(out_grad, frames_far)
+    grads_far = swap_tp(sent_grads)
+    small = gather_steps(small_own, small_far, fsdp)
     lot = first_gain.shape[0]
     whole_six = small[:, : 6 * lot].astype(jnp.float32).reshape(2 * fsdp, 6, lot)
     whole_six = whole_six.transpose(1, 0, 2).reshape(6, 1, width)
@@ -932,66 +1013,100 @@
     bias_q = mine[:, :part].reshape(1, -1)
     bias_v = mine[:, part : 2 * part].reshape(1, -1)
     bias_e = mine[:, 2 * part :].reshape(1, -1)
-    out_turned = w_out.T
-    out_other = swap_tp(out_turned)
-    pack_two = lax.all_gather(
-        jnp.concatenate([w_expand, out_turned, out_other], axis=1), "fsdp", axis=0, tiled=True
-    )
-    out_slot = units // (2 * cols)
-    reduce_all = lax.all_gather(w_reduce.T, "fsdp", axis=0, tiled=True)
-    grads_far = swap_tp(out_grad)
 
     first_own, q_own, k_own, v_own = project(
-        scal_own, frames, gain_one, shift_one, qkv, bias_q, bias_v, heads
+        scal_own, frames, gain_one, shift_one, pack_one, bias_q, bias_v, heads
     )
     first_far, q_far, k_far, v_far = project(
-        scal_far, frames_far, gain_one, shift_one, qkv, bias_q, bias_v, heads
+        scal_far, frames_far, gain_one, shift_one, pack_one, bias_q, bias_v, heads
     )
     context_send, log_far = attend_rows(q_far, k_own, k_far, v_own, v_far)
+    context_send, q_own = tie(context_send, q_own)
     context_far = swap_tp(context_send.reshape(cols, rows))
     context_own, log_own = attend_rows(q_own, k_own, k_far, v_own, v_far)
     context_own = context_own.reshape(cols, rows)
     middle, second_own = merge_heads(
-        context_own, context_far, pack_two, out_slot, frames, out_bias, gain_two, shift_two
+        context_own, context_far, pack_one, frames, out_bias, gain_two, shift_two
     )
 
     second_far = swap_tp(second_own)
+    hid_far, back_far, bsum_far, out_send, terms_send = feed(
+        second_far, grads_far, pack_two, bias_e, units
+    )
+    terms_send, second_own = tie(terms_send, second_own)
+    terms_far = swap_tp(terms_send)
     hid_own, back_own, bsum_own, out_own, terms_own = feed(
-        second_own, out_grad, pack_two, reduce_all, bias_e, units
-    )
-    hid_far, back_far, bsum_far, out_send, terms_send = feed(
-        second_far, grads_far, pack_two, reduce_all, bias_e, units
-    )
-    terms_far = swap_tp(terms_send)
+        second_own, out_grad, pack_two, bias_e, units
+    )
+    mgrad, branch, up_own, up_send, sums_two = branch_back(
+        terms_own, terms_far, middle, out_grad, gain_two, pack_one, cols
+    )
+    up_send, second_own = tie(up_send, second_own)
+    up_far = swap_tp(up_send)
+    d_feed = feed_grads(
+        (out_grad, grads_far), (second_own, second_far), (hid_own, hid_far), (back_own, back_far)
+    )
+    g_feed = lax.psum_scatter(d_feed, "fsdp", scatter_dimension=0, tiled=True)
+    d_out = out_weight_grad(branch, context_own, context_far)
+
+    turned = (heads, HD, rows)
+    up_far, d_out, out_send = tie(up_far, d_out, out_send)
     out_far = swap_tp(out_send)
-    block = 512 if units % 512 == 0 else units
-    d_reduce = weight_grad([out_grad, grads_far], [hid_own, hid_far], block)
-    d_expand = weight_grad([second_own, second_far], [back_own, back_far], block)
+    ups = (up_own.reshape(turned), up_far.reshape(turned))
+    steps = halving_order(fsdp)
+    firsts = (first_own, first_far)
+
+    def back(q_first, start, count):
+        return attend_back_rows(
+            (q_first, q_far), (k_own, k_far), (v_own, v_far), ups, (log_own, log_far), start, count
+        )
+
+    many = heads // 2
+    few = many // 2
+    own_a, far_a = back(q_own, 0, many)
+    d_heads = head_grad(firsts, [own_a], [far_a])
+    d_heads, q_own = tie(d_heads, q_own)
+    held_a = [d_out, d_heads]
+    own_b, far_b = back(q_own, many, few)
+    held_a = halve(held_a, steps[0], steps, fsdp)
+    own_b, held_a, q_own = tie(own_b, held_a, q_own)
+    own_c, far_c = back(q_own, many + few, many - few)
+    held_a = halve(held_a, steps[1], steps[1:], fsdp)
+    far_c, out_far = tie(far_c, out_far)
+    first_send, sums_far, bias_far = first_back([far_a, far_b, far_c], pack_one, frames_far)
+    first_send, far_c = tie(first_send, far_c)
+    first_recv = swap_tp(first_send)
+    held_b = head_grad(firsts, [own_b, own_c], [far_b, far_c])
+    held_b, own_c = tie(held_b, own_c)
+    first_keep, sums_own, bias_own = first_back([own_a, own_b, own_c], pack_one, frames)
+    held_b = halve(held_b, steps[0], steps, fsdp)
+    held_b = halve(held_b, steps[1], steps[1:], fsdp)
+    frames_grad = frames_back(frames, first_keep, first_recv, mgrad, gain_one)
     out_frames = (
         middle + out_own.astype(jnp.float32) + out_far.astype(jnp.float32) + reduce_bias
     ).astype(jnp.bfloat16)
-    mgrad, branch, up_own, up_send, sums_two = branch_back(
-        terms_own, terms_far, middle, out_grad, gain_two, pack_two, out_slot, cols
-    )
-    up_far = swap_tp(up_send)
-    d_out = out_weight_grad(branch, context_own, context_far)
-
-    turned = (heads, HD, rows)
-    dq_own, dq_far, dk_own, dk_far, dv_own, dv_far = attend_back_rows(
-        (q_own, q_far), (k_own, k_far), (v_own, v_far),
-        (up_own.reshape(turned), up_far.reshape(turned)), (log_own, log_far),
-    )
-    pack_far, first_send, sums_far, bias_far = first_back(dq_far, dk_far, dv_far, qkv, frames_far)
-    first_recv = swap_tp(first_send)
-    pack_own, first_keep, sums_own, bias_own = first_back(dq_own, dk_own, dv_own, qkv, frames)
-    d_qkv = weight_grad([first_own, first_far], [pack_own, pack_far], cols, cols, q_factor)
-    frames_grad = frames_back(frames, first_keep, first_recv, mgrad, gain_one)
-
-    def scatter(grad):
-        return lax.psum_scatter(grad, "fsdp", scatter_dimension=0, tiled=True).astype(jnp.float32)
-
-    g_reduce, g_expand, g_qkv = scatter(d_reduce), scatter(d_expand), scatter(d_qkv)
-    g_out = lax.psum_scatter(d_out, "fsdp", scatter_dimension=0, tiled=True)
+    for place in range(2, len(steps)):
+        last = place + 1 == len(steps)
+        held_a = halve(held_a, steps[place], steps[place:], fsdp, last)
+        if place == 2:
+            held_b, frames_grad, out_frames = tie(held_b, frames_grad, out_frames)
+        held_b = halve(held_b, steps[place], steps[place:], fsdp, last)
+    g_out, held_a = held_a[:, : 2 * cols], held_a[:, 2 * cols :]
+    some, fewer = many * HD, few * HD
+
+    def joined(kind):
+        ends = 3 * fewer
+        return jnp.concatenate(
+            [
+                held_a[:, kind * some : (kind + 1) * some],
+                held_b[:, kind * fewer : (kind + 1) * fewer],
+                held_b[:, ends + kind * (some - fewer) : ends + (kind + 1) * (some - fewer)],
+            ],
+            axis=1,
+        )
+
+    g_query, g_key, g_value = joined(0), joined(1), joined(2)
+
     sums_one = sums_own + sums_far
     bias_sum = bias_own + bias_far
     wide_sums = jnp.concatenate([sums_one, sums_two])
@@ -1012,20 +1127,20 @@
     six = (keep + swap_tp(send)).reshape(6, lot)
     rest = small_sum[12 * lot :]
     g_bq, g_bv, g_be = rest[:part], rest[part : 2 * part], rest[2 * part :]
-    g_out_sum = g_out[:, :cols].astype(jnp.float32) + swap_tp(g_out[:, cols:]).astype(jnp.float32)
+    g_out_sum = g_out[:, :cols] + swap_tp(g_out[:, cols:].astype(jnp.bfloat16)).astype(jnp.float32)
     return (
         out_frames[None],
         frames_grad[None],
-        g_qkv[:, :cols],
-        g_qkv[:, cols : 2 * cols],
-        g_qkv[:, 2 * cols :],
+        g_query,
+        g_key,
+        g_value,
         g_bq,
         g_bv,
         g_out_sum.T,
         six[4],
-        g_expand,
+        g_feed[:, units:].astype(jnp.float32),
         g_be,
-        g_reduce.T,
+        g_feed[:, :units].T.astype(jnp.float32),
         six[5],
         six[0],
         six[1],

time: 662 us -> 595 us (0.90)
  waiting for transfers between devices: 301 us -> 193 us
  Pallas kernels: 270 us -> 283 us
  local copies, waits for them, and re-layouts: 22.5 us -> 34.2 us
  other arithmetic: 17.8 us -> 26.1 us
  starting transfers between devices: 27 us -> 34.2 us
    reduce_scatter x4 -> x1, waiting for transfers between devices: 83.1 us -> 0.01 us  [per_device_pair(): g_feed = lax.psum_scatter(d_feed, 'fsdp', scatter_dimension=0, tiled=True)]
    all_gather x3 -> x2, waiting for transfers between devices: 100 us -> 26.4 us  [the longest x1 26.4 us: per_device_pair(): lax.all_gather(jnp.concatenate([w_query, w_key, w_value, out_turned, out_...]
    ppermute x0 -> x8, waiting for transfers between devices: none -> 70.6 us  [halve(): lax.ppermute(chosen(1 - mine), 'fsdp', [(i, i ^ bit) for i in range(fsdp)])]
    ppermute x12, waiting for transfers between devices: 101 us -> 87.2 us  [swap_tp(): return lax.ppermute(piece, 'tp', [(0, 1), (1, 0)])]
    convert_element_type x1 -> x8, other arithmetic: 1.96 us -> 14 us  [the longest x6 7.87 us: halve(): total.astype(jnp.bfloat16)]
    pallas_call x6 -> x8, Pallas kernels: 119 us -> 131 us  [the longest x3 63.3 us: attend_back_rows(): pl.pallas_call(attend_back_kernel, out_shape=(jax.ShapeDtypeStruct(packed...]
    squeeze x0 -> x9, local copies, waits for them, and re-layouts: none -> 8.72 us  [chosen(): lax.dynamic_index_in_dim(view, which, 1, keepdims=False)]
    ppermute x0 -> x8, starting transfers between devices: none -> 8.19 us  [halve(): lax.ppermute(chosen(1 - mine), 'fsdp', [(i, i ^ bit) for i in range(fsdp)])]
  transfers between devices with their start and end apart: 27 -> 31, of which waited for: 18 -> 20; matrix products, arithmetic and copies ran while one was open for 5% -> 9% of each run, Pallas kernels for 33% -> 41%
where the time goes in v2:
time: 595 us; the launch traced here: 585 us
  Pallas kernels  283 us (48%)
  waiting for transfers between devices  193 us (32%)
  starting transfers between devices  34.2 us (6%)
  local copies, waits for them, and re-layouts  34.2 us (6%)
  other arithmetic  26.1 us (4%)
  between operations  14.8 us (2%)
    ppermute x12, waiting for transfers between devices, swap_tp(): return lax.ppermute(piece, 'tp', [(0, 1), (1, 0)])  87.2 us
    ppermute x8, waiting for transfers between devices, halve(): lax.ppermute(chosen(1 - mine), 'fsdp', [(i, i ^ bit) for i in range(fsdp)])  70.6 us
    pallas_call x2, Pallas kernels, feed(): pl.pallas_call(feed_kernel, out_shape=(jax.ShapeDtypeStruct((rows, units)...  65.6 us
    pallas_call x3, Pallas kernels, attend_back_rows(): pl.pallas_call(attend_back_kernel, out_shape=(jax.ShapeDtypeStruct(packed...  63.3 us
    pallas_call x2, Pallas kernels, attend_rows(): pl.pallas_call(attend_kernel, out_shape=(jax.ShapeDtypeStruct((heads, HD,...  30.8 us
    pallas_call x1, Pallas kernels, feed_grads(): pl.pallas_call(feed_grad_kernel, out_shape=jax.ShapeDtypeStruct((width, 2...  28.8 us
    all_gather x1, waiting for transfers between devices, per_device_pair(): lax.all_gather(jnp.concatenate([w_query, w_key, w_value, out_turned, out_...  26.4 us
    pallas_call x2, Pallas kernels, first_back(): pl.pallas_call(functools.partial(first_kernel, len(packs)), out_shape=(ja...  20.6 us
  transfers between devices with their start and end apart: 31, of which 20 were waited for; matrix products, arithmetic and copies ran while one was open for 9% of the time, Pallas kernels for 41%

profile of v2, /device:TPU:0, one launch (start us, length us, event | category | flops | bytes accessed | tf_op | source)
XLA Modules:
  0.0 585.3 jit_solution(388787833474605773)
XLA Ops:
  42.3 21.1 %collective-permute-done.6.frames_ref.refs_4_ = bf16[752,1280]{1,0:T(8,128)(2,1)} collective-permute-done((bf16[752,1280]{1,0:T(8,128)(2,1)S(1)}, bf16[752,1280]{1,0:T(8,128)(2,1)}, u32[]{:S(2)}, u32[]{:S(2)}) %collective-permute-start.6) | collective-permute-done | bytes 1925152 | tf_op jit(solution)/shard_map/ppermute | solution.py:914
  63.7 26.4 %all-gather.3.cloned.1.call-done.weight_ref.wo_ref.wt_ref.refs_3_ = bf16[1280,3200]{1,0:T(8,128)(2,1)} async-done(((bf16[80,3200]{1,0:T(8,128)(2,1)}), bf16[1280,3200]{1,0:T(8,128)(2,1)}) %all-gather.3.cloned.1.call-update) | async-done | bytes 8192016 | tf_op jit(solution)/shard_map/all_gather | solution.py:993
  90.1 10.3 %project.2 = (bf16[752,1280]{1,0:T(8,128)(2,1)}, bf16[8,752,128]{2,1,0:T(8,128)(2,1)}, bf16[8,752,128]{2,1,0:T(8,128)(2,1)}, bf16[8,752,128]{2,1,0:T(8,128)(2,1)}) custom-call(s32[2]{0:T(128)} %get-tuple-element.190.scal_ref, bf16[752,1280]{1,0:T(8,128)(2,1)} %bitcast.104, f32[1,1280]{1,0:T(1,128)} %squeeze.89.gain_ref, f32[1,1280]{1,0:T(1,128)} %squeeze.90.shift_ref, ...), custom_call_target="tpu_custom_call" | custom-call | flops 11088691200 | bytes 8765440 | tf_op jit(solution)/shard_map/project/pallas_call | solution.py:404
  100.4 10.3 %project.3 = (bf16[752,1280]{1,0:T(8,128)(2,1)}, bf16[8,752,128]{2,1,0:T(8,128)(2,1)}, bf16[8,752,128]{2,1,0:T(8,128)(2,1)}, bf16[8,752,128]{2,1,0:T(8,128)(2,1)}) custom-call(s32[2]{0:T(128)} %get-tuple-element.191.scal_ref, bf16[752,1280]{1,0:T(8,128)(2,1)} %collective-permute-done.6.frames_ref.refs_4_, f32[1,1280]{1,0:T(1,128)} %squeeze.89.gain_ref, ...), custom_call_target="tpu_custom_call" | custom-call | flops 11088691200 | bytes 8765440 | tf_op jit(solution)/shard_map/project/pallas_call | solution.py:404
  110.7 15.5 %attend.2 = (bf16[8,80,752]{2,1,0:T(8,128)(2,1)}, f32[8,1,752]{2,1,0:T(1,128)}) custom-call(bf16[8,752,128]{2,1,0:T(8,128)(2,1)} %get-tuple-element.90.q_ref.qt_ref, bf16[8,752,128]{2,1,0:T(8,128)(2,1)} %get-tuple-element.91.ko_ref, bf16[8,752,128]{2,1,0:T(8,128)(2,1)} %get-tuple-element.92.kt_ref, bf16[8,752,128]{2,1,0:T(8,128)(2,1)} %get-tuple-element.93.vo_ref, ...), custom_call_target="tpu_custom_call" | custom-call | flops 43430707200 | bytes 9240576 | tf_op jit(solution)/shard_map/attend/pallas_call | solution.py:453
  129.7 15.3 %attend.3 = (bf16[8,80,752]{2,1,0:T(8,128)(2,1)}, f32[8,1,752]{2,1,0:T(1,128)}) custom-call(bf16[8,752,128]{2,1,0:T(8,128)(2,1)} %get-tuple-element.122.q_ref.qo_ref, bf16[8,752,128]{2,1,0:T(8,128)(2,1)} %get-tuple-element.91.ko_ref, bf16[8,752,128]{2,1,0:T(8,128)(2,1)} %get-tuple-element.92.kt_ref, bf16[8,752,128]{2,1,0:T(8,128)(2,1)} %get-tuple-element.93.vo_ref, ...), custom_call_target="tpu_custom_call" | custom-call | flops 43430707200 | bytes 9240576 | tf_op jit(solution)/shard_map/attend/pallas_call | solution.py:453
  145.0 6.8 %collective-permute-done.7 = bf16[640,752]{0,1:T(8,128)(2,1)S(1)} collective-permute-done((bf16[640,752]{0,1:T(8,128)(2,1)S(1)}, bf16[640,752]{0,1:T(8,128)(2,1)S(1)}, u32[]{:S(2)}, u32[]{:S(2)}) %collective-permute-start.7) | collective-permute-done | bytes 962592 | tf_op jit(solution)/shard_map/ppermute | solution.py:914
  153.5 9.1 %merge_heads.1 = (f32[752,1280]{1,0:T(8,128)}, bf16[752,1280]{1,0:T(8,128)(2,1)}) custom-call(bf16[640,752]{1,0:T(8,128)(2,1)} %bitcast.130, bf16[640,752]{1,0:T(8,128)(2,1)} %copy.39.ct_ref, bf16[1280,3200]{1,0:T(8,128)(2,1)} %all-gather.3.cloned.1.call-done.weight_ref.wo_ref.wt_ref.refs_3_, ...), custom_call_target="tpu_custom_call" | custom-call | flops 7392460800 | bytes 12902400 | tf_op jit(solution)/shard_map/merge_heads/pallas_call | solution.py:577
  164.8 41.5 %collective-permute-done.8.second_ref.st_ref = bf16[752,1280]{1,0:T(8,128)(2,1)} collective-permute-done((bf16[752,1280]{1,0:T(8,128)(2,1)}, bf16[752,1280]{1,0:T(8,128)(2,1)}, u32[]{:S(2)}, u32[]{:S(2)}) %collective-permute-start.8) | collective-permute-done | bytes 1925152 | tf_op jit(solution)/shard_map/ppermute | solution.py:914
  206.4 32.9 %feed.2 = (bf16[752,2560]{1,0:T(8,128)(2,1)}, bf16[752,2560]{1,0:T(8,128)(2,1)}, f32[1,2560]{1,0:T(1,128)}, bf16[752,1280]{1,0:T(8,128)(2,1)}, bf16[752,1280]{1,0:T(8,128)(2,1)}) custom-call(bf16[752,1280]{1,0:T(8,128)(2,1)} %collective-permute-done.8.second_ref.st_ref, bf16[752,1280]{1,0:T(8,128)(2,1)} %collective-permute-done.9.grad_ref.gt_ref, ...), custom_call_target="tpu_custom_call" | custom-call | flops 59139686400 | bytes 36208640 | tf_op jit(solution)/shard_map/feed/pallas_call | solution.py:649
  240.8 32.7 %feed.3 = (bf16[752,2560]{1,0:T(8,128)(2,1)}, bf16[752,2560]{1,0:T(8,128)(2,1)}, f32[1,2560]{1,0:T(1,128)}, bf16[752,1280]{1,0:T(8,128)(2,1)}, bf16[752,1280]{1,0:T(8,128)(2,1)}) custom-call(bf16[752,1280]{1,0:T(8,128)(2,1)} %get-tuple-element.148.second_ref.so_ref, bf16[752,1280]{1,0:T(8,128)(2,1)} %bitcast.127, ...), custom_call_target="tpu_custom_call" | custom-call | flops 59139686400 | bytes 36208640 | tf_op jit(solution)/shard_map/feed/pallas_call | solution.py:649
  273.5 8.6 %collective-permute-done.10.far_ref = bf16[752,1280]{1,0:T(8,128)(2,1)S(1)} collective-permute-done((bf16[752,1280]{1,0:T(8,128)(2,1)}, bf16[752,1280]{1,0:T(8,128)(2,1)S(1)}, u32[]{:S(2)}, u32[]{:S(2)}) %collective-permute-start.10) | collective-permute-done | bytes 1925152 | tf_op jit(solution)/shard_map/ppermute | solution.py:914
  283.3 12.5 %branch_back.1 = (f32[752,1280]{1,0:T(8,128)}, bf16[752,1280]{1,0:T(8,128)(2,1)}, bf16[640,752]{1,0:T(8,128)(2,1)}, bf16[640,752]{1,0:T(8,128)(2,1)}, f32[4,1280]{1,0:T(4,128)}) custom-call(bf16[752,1280]{1,0:T(8,128)(2,1)} %get-tuple-element.104.own_ref, bf16[752,1280]{1,0:T(8,128)(2,1)} %copy-done.23, f32[752,1280]{1,0:T(8,128)} %get-tuple-element.106.middle_ref, ...), custom_call_target="tpu_custom_call" | custom-call | flops 7392460800 | bytes 17326080 | tf_op jit(solution)/shard_map/branch_back/pallas_call | solution.py:782
  299.3 28.8 %feed_grads.1 = bf16[1280,5120]{1,0:T(8,128)(2,1)} custom-call(bf16[752,1280]{1,0:T(8,128)(2,1)} %bitcast.129, bf16[752,1280]{1,0:T(8,128)(2,1)} %collective-permute-done.9.grad_ref.gt_ref, bf16[752,1280]{1,0:T(8,128)(2,1)} %get-tuple-element.148.second_ref.so_ref, bf16[752,1280]{1,0:T(8,128)(2,1)} %collective-permute-done.8.second_ref.st_ref, ...), custom_call_target="tpu_custom_call" | custom-call | flops 59139686400 | bytes 36208640 | tf_op jit(solution)/shard_map/feed_grads/pallas_call | solution.py:690
  328.2 7.1 %out_weight_grad.1 = bf16[1280,1280]{1,0:T(8,128)(2,1)} custom-call(bf16[752,1280]{1,0:T(8,128)(2,1)} %get-tuple-element.110.branch_ref, bf16[640,752]{1,0:T(8,128)(2,1)} %bitcast.131, bf16[640,752]{1,0:T(8,128)(2,1)} %copy.39.ct_ref), custom_call_target="tpu_custom_call" | custom-call | flops 7392460800 | bytes 7127040 | tf_op jit(solution)/shard_map/out_weight_grad/pallas_call | solution.py:812
  337.0 30.7 %attend_back.3 = (bf16[752,960]{1,0:T(8,128)(2,1)}, bf16[752,960]{1,0:T(8,128)(2,1)}) custom-call(bf16[8,752,128]{2,1,0:T(8,128)(2,1)} %get-tuple-element.122.q_ref.qo_ref, bf16[8,752,128]{2,1,0:T(8,128)(2,1)} %get-tuple-element.90.q_ref.qt_ref, bf16[8,752,128]{2,1,0:T(8,128)(2,1)} %get-tuple-element.91.ko_ref, ...), custom_call_target="tpu_custom_call" | custom-call | flops 48859545600 | bytes 9240576 | tf_op jit(solution)/shard_map/attend_back/pallas_call | solution.py:536
  367.7 9.0 %head_grad.2 = bf16[1280,960]{1,0:T(8,128)(2,1)} custom-call(bf16[752,1280]{1,0:T(8,128)(2,1)} %get-tuple-element.86.lo_ref, bf16[752,1280]{1,0:T(8,128)(2,1)} %get-tuple-element.89.lt_ref, bf16[752,960]{1,0:T(8,128)(2,1)} %get-tuple-element.115.refs_0_, bf16[752,960]{1,0:T(8,128)(2,1)} %get-tuple-element.116.refs_1_.refs_0_), custom_call_target="tpu_custom_call" | custom-call | flops 11088691200 | bytes 9195520 | tf_op jit(solution)/shard_map/head_grad/pallas_call | solution.py:719
  384.0 16.2 %attend_back.4 = (bf16[752,480]{1,0:T(8,128)(2,1)}, bf16[752,480]{1,0:T(8,128)(2,1)}) custom-call(bf16[8,752,128]{2,1,0:T(8,128)(2,1)} %get-tuple-element.122.q_ref.qo_ref, bf16[8,752,128]{2,1,0:T(8,128)(2,1)} %get-tuple-element.90.q_ref.qt_ref, bf16[8,752,128]{2,1,0:T(8,128)(2,1)} %get-tuple-element.91.ko_ref, ...), custom_call_target="tpu_custom_call" | custom-call | flops 24429772800 | bytes 4620288 | tf_op jit(solution)/shard_map/attend_back/pallas_call | solution.py:536
  401.7 3.4 add_convert_fusion
  405.2 16.5 %attend_back.5 = (bf16[752,480]{1,0:T(8,128)(2,1)}, bf16[752,480]{1,0:T(8,128)(2,1)}) custom-call(bf16[8,752,128]{2,1,0:T(8,128)(2,1)} %get-tuple-element.122.q_ref.qo_ref, bf16[8,752,128]{2,1,0:T(8,128)(2,1)} %get-tuple-element.90.q_ref.qt_ref, bf16[8,752,128]{2,1,0:T(8,128)(2,1)} %get-tuple-element.91.ko_ref, ...), custom_call_target="tpu_custom_call" | custom-call | flops 24429772800 | bytes 4620288 | tf_op jit(solution)/shard_map/attend_back/pallas_call | solution.py:536
  421.6 6.4 %collective-permute-done.13 = bf16[752,1280]{1,0:T(8,128)(2,1)} collective-permute-done((bf16[752,1280]{1,0:T(8,128)(2,1)}, bf16[752,1280]{1,0:T(8,128)(2,1)}, u32[]{:S(2)}, u32[]{:S(2)}) %collective-permute-start.13) | collective-permute-done | bytes 1925152 | tf_op jit(solution)/shard_map/ppermute | solution.py:914
  428.0 10.2 %first_back.2 = (bf16[752,1280]{1,0:T(8,128)(2,1)}, f32[2,1280]{1,0:T(2,128)}, f32[1,1920]{1,0:T(1,128)}) custom-call(bf16[752,960]{1,0:T(8,128)(2,1)} %get-tuple-element.116.refs_1_.refs_0_, bf16[752,480]{1,0:T(8,128)(2,1)} %get-tuple-element.124.refs_1_.refs_2_, bf16[752,480]{1,0:T(8,128)(2,1)} %get-tuple-element.129.refs_2_.refs_3_, ...), custom_call_target="tpu_custom_call" | custom-call | flops 11088691200 | bytes 11653120 | tf_op jit(solution)/shard_map/first_back/pallas_call | solution.py:866
  438.2 9.0 %head_grad.3 = bf16[1280,960]{1,0:T(8,128)(2,1)} custom-call(bf16[752,1280]{1,0:T(8,128)(2,1)} %get-tuple-element.86.lo_ref, bf16[752,1280]{1,0:T(8,128)(2,1)} %get-tuple-element.89.lt_ref, bf16[752,480]{1,0:T(8,128)(2,1)} %get-tuple-element.121.refs_0_.refs_1_, bf16[752,480]{1,0:T(8,128)(2,1)} %get-tuple-element.131.refs_1_.refs_2_, ...), custom_call_target="tpu_custom_call" | custom-call | flops 11088691200 | bytes 9195520 | tf_op jit(solution)/shard_map/head_grad/pallas_call | solution.py:719
  447.3 10.4 %first_back.3 = (bf16[752,1280]{1,0:T(8,128)(2,1)}, f32[2,1280]{1,0:T(2,128)}, f32[1,1920]{1,0:T(1,128)}) custom-call(bf16[752,960]{1,0:T(8,128)(2,1)} %get-tuple-element.115.refs_0_, bf16[752,480]{1,0:T(8,128)(2,1)} %get-tuple-element.121.refs_0_.refs_1_, bf16[752,480]{1,0:T(8,128)(2,1)} %get-tuple-element.131.refs_1_.refs_2_, ...), custom_call_target="tpu_custom_call" | custom-call | flops 11088691200 | bytes 11653120 | tf_op jit(solution)/shard_map/first_back/pallas_call | solution.py:866
  473.4 3.7 add_convert_fusion.1
  481.7 25.4 %collective-permute-done.17 = bf16[4,80,2240]{2,1,0:T(8,128)(2,1)} collective-permute-done((bf16[4,80,2240]{2,1,0:T(8,128)(2,1)}, bf16[4,80,2240]{2,1,0:T(8,128)(2,1)}, u32[]{:S(2)}, u32[]{:S(2)}) %collective-permute-start.17) | collective-permute-done | bytes 1433632 | tf_op jit(solution)/shard_map/ppermute | solution.py:950
  513.7 6.4 %collective-permute-done.15 = bf16[4,80,960]{2,1,0:T(8,128)(2,1)S(1)} collective-permute-done((bf16[4,80,960]{2,1,0:T(8,128)(2,1)S(1)}, bf16[4,80,960]{2,1,0:T(8,128)(2,1)S(1)}, u32[]{:S(2)}, u32[]{:S(2)}) %collective-permute-start.15) | collective-permute-done | bytes 614432 | tf_op jit(solution)/shard_map/ppermute | solution.py:950
  520.4 6.6 %frames_back.1 = bf16[752,1280]{1,0:T(8,128)(2,1)} custom-call(bf16[752,1280]{1,0:T(8,128)(2,1)} %bitcast.107, bf16[752,1280]{1,0:T(8,128)(2,1)} %get-tuple-element.132.own_ref, bf16[752,1280]{1,0:T(8,128)(2,1)} %collective-permute-done.16.far_ref, f32[752,1280]{1,0:T(8,128)} %get-tuple-element.134.mgrad_ref, f32[1,1280]{1,0:T(1,128)} %squeeze.89.gain_ref), custom_call_target="tpu_custom_call" | custom-call | flops 57753600 | bytes 11550720 | tf_op jit(solution)/shard_map/frames_back/pallas_call | solution.py:901
  528.8 22.9 %collective-permute-done.18 = bf16[1,160,2240]{2,1,0:T(8,128)(2,1)S(1)} collective-permute-done((bf16[1,160,2240]{2,1,0:T(8,128)(2,1)S(1)}, bf16[1,160,2240]{2,1,0:T(8,128)(2,1)S(1)}, u32[]{:S(2)}, u32[]{:S(2)}) %collective-permute-start.18) | collective-permute-done | bytes 716832 | tf_op jit(solution)/shard_map/ppermute | solution.py:950
  551.8 5.5 collective-permute-done.20
  559.6 5.0 collective-permute-done.21
  564.8 5.4 collective-permute-done.19
  (195 shorter events, 99.1 us)
Async XLA Ops:
  7.2 82.9 %all-gather.3.cloned.1.call-start = ((), (), s32[]{:S(2)}) async-start(), calls=%async_computation.1 | async-start | bytes 8704000 | tf_op jit(solution)/shard_map/all_gather | solution.py:993
  7.2 6.9 %collective-permute-start.1 = (bf16[80,640]{1,0:T(8,128)(2,1)}, bf16[80,640]{1,0:T(8,128)(2,1)S(1)}, u32[]{:S(2)}, u32[]{:S(2)}) collective-permute-start(bf16[80,640]{1,0:T(8,128)(2,1)} %bitcast.122), channel_id=1, source_target_pairs={{0,1},{1,0},{2,3},{3,2},{4,5},{5,4},{6,7},{7,6},{8,9},{9,8},{10,11... | collective-permute-start | bytes 307208 | tf_op jit(solution)/shard_map/ppermute | solution.py:914
  15.0 191.3 %all-gather.5.cloned.1.call-start = ((), (), s32[]{:S(2)}) async-start(), calls=%async_computation.2 | async-start | bytes 13926400 | tf_op jit(solution)/shard_map/all_gather | solution.py:997
  17.2 558.8 %reduce-scatter.2.cloned.1.call-start = ((), (), s32[]{:S(2)}) async-start(), calls=%async_computation.3 | async-start | bytes 13926400 | tf_op jit(solution)/shard_map/reduce_scatter | solution.py:1049
  17.4 3.6 collective-permute-start
  21.0 42.4 %collective-permute-start.6 = (bf16[752,1280]{1,0:T(8,128)(2,1)S(1)}, bf16[752,1280]{1,0:T(8,128)(2,1)}, u32[]{:S(2)}, u32[]{:S(2)}) collective-permute-start(bf16[752,1280]{1,0:T(8,128)(2,1)S(1)} %bitcast.108), channel_id=1, source_target_pairs={{0,1},{1,0},{2,3},{3,2},{4,5},{5,4},{6,7},{7,6},{8,9},{9,8},{10,11... | collective-permute-start | bytes 5775368 | tf_op jit(solution)/shard_map/ppermute | solution.py:914
  22.0 1.2 collective-permute-start.2
  23.2 3.7 collective-permute-start.3
  26.9 4.0 collective-permute-start.4
  31.0 5.5 collective-permute-start.5
  63.4 101.4 %collective-permute-start.9 = (bf16[752,1280]{1,0:T(8,128)(2,1)}, bf16[752,1280]{1,0:T(8,128)(2,1)}, u32[]{:S(2)}, u32[]{:S(2)}) collective-permute-start(bf16[752,1280]{1,0:T(8,128)(2,1)} %bitcast.126), channel_id=1, source_target_pairs={{0,1},{1,0},{2,3},{3,2},{4,5},{5,4},{6,7},{7,6},{8,9},{9,8},{10,11... | collective-permute-start | bytes 5775368 | tf_op jit(solution)/shard_map/ppermute | solution.py:914
  128.2 23.6 %collective-permute-start.7 = (bf16[640,752]{0,1:T(8,128)(2,1)S(1)}, bf16[640,752]{0,1:T(8,128)(2,1)S(1)}, u32[]{:S(2)}, u32[]{:S(2)}) collective-permute-start(bf16[640,752]{0,1:T(8,128)(2,1)S(1)} %copy.38), channel_id=1, source_target_pairs={{0,1},{1,0},{2,3},{3,2},{4,5},{5,4},{6,7},{7,6},{8,9},{9,8},{10,11... | collective-permute-start | bytes 2887688 | tf_op jit(solution)/shard_map/ppermute | solution.py:914
  162.6 43.7 %collective-permute-start.8 = (bf16[752,1280]{1,0:T(8,128)(2,1)}, bf16[752,1280]{1,0:T(8,128)(2,1)}, u32[]{:S(2)}, u32[]{:S(2)}) collective-permute-start(bf16[752,1280]{1,0:T(8,128)(2,1)} %get-tuple-element.148.second_ref.so_ref), channel_id=1, source_target_pairs={{0,1},{1,0},{2,3},{3,2},{4,5},{5,4},{6,7},{7,6},{8,9},{9,8},{10,11... | collective-permute-start | bytes 5775368 | tf_op jit(solution)/shard_map/ppermute | solution.py:914
  239.3 42.8 %collective-permute-start.10 = (bf16[752,1280]{1,0:T(8,128)(2,1)}, bf16[752,1280]{1,0:T(8,128)(2,1)S(1)}, u32[]{:S(2)}, u32[]{:S(2)}) collective-permute-start(bf16[752,1280]{1,0:T(8,128)(2,1)} %get-tuple-element.105), channel_id=1, source_target_pairs={{0,1},{1,0},{2,3},{3,2},{4,5},{5,4},{6,7},{7,6},{8,9},{9,8},{10,11... | collective-permute-start | bytes 5775368 | tf_op jit(solution)/shard_map/ppermute | solution.py:914
  297.8 37.4 %collective-permute-start.11 = (bf16[640,752]{0,1:T(8,128)(2,1)S(1)}, bf16[640,752]{0,1:T(8,128)(2,1)S(1)}, u32[]{:S(2)}, u32[]{:S(2)}) collective-permute-start(bf16[640,752]{0,1:T(8,128)(2,1)S(1)} %copy.40), channel_id=1, source_target_pairs={{0,1},{1,0},{2,3},{3,2},{4,5},{5,4},{6,7},{7,6},{8,9},{9,8},{10,11... | collective-permute-start | bytes 2887688 | tf_op jit(solution)/shard_map/ppermute | solution.py:914
  383.2 16.9 %collective-permute-start.12 = (bf16[8,80,2240]{2,1,0:T(8,128)(2,1)}, bf16[8,80,2240]{2,1,0:T(8,128)(2,1)S(1)}, u32[]{:S(2)}, u32[]{:S(2)}) collective-permute-start(bf16[8,80,2240]{2,1,0:T(8,128)(2,1)} %pad_maximum_fusion), channel_id=1, source_target_pairs={{0,2},{2,0},{4,6},{6,4},{8,10},{10,8},{12,14},{14,12},{16,18},{18,... | collective-permute-start | bytes 8601608 | tf_op jit(solution)/shard_map/ppermute | solution.py:950
  383.4 44.7 %collective-permute-start.13 = (bf16[752,1280]{1,0:T(8,128)(2,1)}, bf16[752,1280]{1,0:T(8,128)(2,1)}, u32[]{:S(2)}, u32[]{:S(2)}) collective-permute-start(bf16[752,1280]{1,0:T(8,128)(2,1)} %get-tuple-element.126), channel_id=1, source_target_pairs={{0,1},{1,0},{2,3},{3,2},{4,5},{5,4},{6,7},{7,6},{8,9},{9,8},{10,11... | collective-permute-start | bytes 5775368 | tf_op jit(solution)/shard_map/ppermute | solution.py:914
  459.8 4.8 collective-permute-start.22
  464.7 4.9 collective-permute-start.23
  468.4 9.7 %collective-permute-start.14 = (bf16[8,80,960]{2,1,0:T(8,128)(2,1)}, bf16[8,80,960]{2,1,0:T(8,128)(2,1)}, u32[]{:S(2)}, u32[]{:S(2)}) collective-permute-start(bf16[8,80,960]{2,1,0:T(8,128)(2,1)} %dynamic-slice_bitcast_fusion.3), channel_id=1, source_target_pairs={{0,2},{2,0},{4,6},{6,4},{8,10},{10,8},{12,14},{14,12},{16,18},{18,... | collective-permute-start | bytes 3686408 | tf_op jit(solution)/shard_map/ppermute | solution.py:950
  468.4 51.9 %collective-permute-start.16 = (bf16[752,1280]{1,0:T(8,128)(2,1)}, bf16[752,1280]{1,0:T(8,128)(2,1)}, u32[]{:S(2)}, u32[]{:S(2)}) collective-permute-start(bf16[752,1280]{1,0:T(8,128)(2,1)} %get-tuple-element.133), channel_id=1, source_target_pairs={{0,1},{1,0},{2,3},{3,2},{4,5},{5,4},{6,7},{7,6},{8,9},{9,8},{10,11... | collective-permute-start | bytes 5775368 | tf_op jit(solution)/shard_map/ppermute | solution.py:914
  469.6 3.7 collective-permute-start.24
  471.7 35.5 %collective-permute-start.17 = (bf16[4,80,2240]{2,1,0:T(8,128)(2,1)}, bf16[4,80,2240]{2,1,0:T(8,128)(2,1)}, u32[]{:S(2)}, u32[]{:S(2)}) collective-permute-start(bf16[4,80,2240]{2,1,0:T(8,128)(2,1)} %dynamic-slice_bitcast_fusion.2), channel_id=1, source_target_pairs={{0,4},{2,6},{4,0},{6,2},{8,12},{10,14},{12,8},{14,10},{16,20},{18,... | collective-permute-start | bytes 4300808 | tf_op jit(solution)/shard_map/ppermute | solution.py:950
  473.3 3.8 collective-permute-start.25
  477.2 35.9 %collective-permute-start.27 = (f32[240]{0:T(256)S(1)}, f32[240]{0:T(256)S(1)}, u32[]{:S(2)}, u32[]{:S(2)}) collective-permute-start(f32[240]{0:T(256)S(1)} %bitcast.124), channel_id=1, source_target_pairs={{0,1},{1,0},{2,3},{3,2},{4,5},{5,4},{6,7},{7,6},{8,9},{9,8},{10,11... | collective-permute-start | bytes 2888 | tf_op jit(solution)/shard_map/ppermute | solution.py:914
  480.5 39.6 %collective-permute-start.15 = (bf16[4,80,960]{2,1,0:T(8,128)(2,1)S(1)}, bf16[4,80,960]{2,1,0:T(8,128)(2,1)S(1)}, u32[]{:S(2)}, u32[]{:S(2)}) collective-permute-start(bf16[4,80,960]{2,1,0:T(8,128)(2,1)S(1)} %dynamic-slice_bitcast_fusion.7), channel_id=1, source_target_pairs={{0,4},{2,6},{4,0},{6,2},{8,12},{10,14},{12,8},{14,10},{16,20},{18,... | collective-permute-start | bytes 1843208 | tf_op jit(solution)/shard_map/ppermute | solution.py:950
  510.0 41.6 %collective-permute-start.18 = (bf16[1,160,2240]{2,1,0:T(8,128)(2,1)S(1)}, bf16[1,160,2240]{2,1,0:T(8,128)(2,1)S(1)}, u32[]{:S(2)}, u32[]{:S(2)}) collective-permute-start(bf16[1,160,2240]{2,1,0:T(8,128)(2,1)S(1)} %dynamic-slice_bitcast_fusion.6), channel_id=1, source_target_pairs={{0,16},{2,18},{4,20},{6,22},{8,24},{10,26},{12,28},{14,30},{16,0},... | collective-permute-start | bytes 2150408 | tf_op jit(solution)/shard_map/ppermute | solution.py:950
  520.3 31.3 %copy-start.1 = (bf16[4,80,2240]{2,1,0:T(8,128)(2,1)S(1)}, bf16[4,80,2240]{2,1,0:T(8,128)(2,1)}, u32[]{:S(2)}) copy-start(bf16[4,80,2240]{2,1,0:T(8,128)(2,1)} %copy-done) | copy-start | bytes 4300804
  527.0 30.3 %collective-permute-start.20 = (bf16[1,160,960]{2,1,0:T(8,128)(2,1)S(1)}, bf16[1,160,960]{2,1,0:T(8,128)(2,1)S(1)}, u32[]{:S(2)}, u32[]{:S(2)}) collective-permute-start(bf16[1,160,960]{2,1,0:T(8,128)(2,1)S(1)} %dynamic-slice_bitcast_fusion.9), channel_id=1, source_target_pairs={{0,16},{2,18},{4,20},{6,22},{8,24},{10,26},{12,28},{14,30},{16,0},... | collective-permute-start | bytes 921608 | tf_op jit(solution)/shard_map/ppermute | solution.py:950
  557.4 7.2 %collective-permute-start.21 = (bf16[1,80,960]{2,1,0:T(8,128)(2,1)S(1)}, bf16[1,80,960]{2,1,0:T(8,128)(2,1)S(1)}, u32[]{:S(2)}, u32[]{:S(2)}) collective-permute-start(bf16[1,80,960]{2,1,0:T(8,128)(2,1)S(1)} %dynamic-slice_bitcast_fusion.10), channel_id=1, source_target_pairs={{0,8},{2,10},{4,12},{6,14},{8,0},{10,2},{12,4},{14,6},{16,24},{18,... | collective-permute-start | bytes 460808 | tf_op jit(solution)/shard_map/ppermute | solution.py:950
  557.5 12.7 %collective-permute-start.19 = (bf16[1,80,2240]{2,1,0:T(8,128)(2,1)S(1)}, bf16[1,80,2240]{2,1,0:T(8,128)(2,1)S(1)}, u32[]{:S(2)}, u32[]{:S(2)}) collective-permute-start(bf16[1,80,2240]{2,1,0:T(8,128)(2,1)S(1)} %dynamic-slice_bitcast_fusion.8), channel_id=1, source_target_pairs={{0,8},{2,10},{4,12},{6,14},{8,0},{10,2},{12,4},{14,6},{16,24},{18,... | collective-permute-start | bytes 1075208 | tf_op jit(solution)/shard_map/ppermute | solution.py:950
  570.3 4.9 collective-permute-start.26
  (25 other events, 171.7 us)
Sparse Core Ops, SparseCore 0:
  15.1 74.9 all-gather.2
  93.0 102.2 all-gather.4
  328.3 136.1 reduce-scatter.1

commit v3 on v2

--- a/solution.py
+++ b/solution.py
@@ -312,15 +312,15 @@
 
 VMEM_LIMIT = 60 << 20
 PAD = 128
-COST = 3.0
+COSTS = {'project': 3.0, 'attend': 3.0, 'merge_heads': 3.0, 'feed': 3.0, 'weight_grad': 3.0, 'head_grad': 0.02, 'branch_back': 3.0, 'out_weight_grad': 0.02, 'first_back': 0.02, 'frames_back': 0.02, 'attend_back': (8.0, 0.02)}
 
 
 def kernel_params():
     return pltpu.CompilerParams(vmem_limit_bytes=VMEM_LIMIT)
 
 
-def cost(flops, moved):
-    return pl.CostEstimate(flops=int(COST * flops), bytes_accessed=int(moved), transcendentals=0)
+def cost(flops, moved, scale):
+    return pl.CostEstimate(flops=int(scale * flops), bytes_accessed=int(min(1.0, scale) * moved), transcendentals=0)
 
 
 def row_pieces(rows, size):
@@ -414,7 +414,7 @@
             out_specs=(whole((rows, width)),) + (whole((heads, rows, PAD)),) * 3,
         ),
         compiler_params=kernel_params(),
-        cost_estimate=cost(2 * rows * width * 3 * cols, 4 * rows * width + 6 * width * cols),
+        cost_estimate=cost(2 * rows * width * 3 * cols, 4 * rows * width + 6 * width * cols, COSTS["project"]),
         name="project",
     )(scalars, frames, gain, shift, weights, bias_q, bias_v)
 
@@ -463,7 +463,7 @@
             pl.BlockSpec((per_step, 1, rows), lambda h: (h, 0, 0)),
         ),
         compiler_params=kernel_params(),
-        cost_estimate=cost(heads * 2 * rows * 2 * rows * 2 * 400, heads * rows * PAD * 12),
+        cost_estimate=cost(heads * 2 * rows * 2 * rows * 2 * 400, heads * rows * PAD * 12, COSTS["attend"]),
         name="attend",
     )(queries, keys_own, keys_far, values_own, values_far)
 
@@ -541,7 +541,7 @@
         out_specs=(whole(packed),) * 2,
         scratch_shapes=[pltpu.VMEM((2 * rows, HD), jnp.bfloat16)],
         compiler_params=kernel_params(),
-        cost_estimate=cost(heads * 4 * rows * rows * 2 * 900, heads * rows * PAD * 24),
+        cost_estimate=cost(heads * 4 * rows * rows * 2 * 900, heads * rows * PAD * 24, COSTS["attend_back"][start > 0]),
         name="attend_back",
     )(*queries, *keys, *values, *upstream, *logs)
 
@@ -587,15 +587,18 @@
         ],
         out_specs=(whole((rows, width)),) * 2,
         compiler_params=kernel_params(),
-        cost_estimate=cost(4 * rows * width * cols, 10 * rows * width + 4 * width * cols),
+        cost_estimate=cost(4 * rows * width * cols, 10 * rows * width + 4 * width * cols, COSTS["merge_heads"]),
         name="merge_heads",
     )(context_own, context_far, pack, pack, frames, bias, gain, shift)
 
 
 def feed_kernel(
-    second_ref, grad_ref, expand_ref, reduce_ref, bias_ref,
-    hidden_ref, back_ref, bsum_ref, out_ref, terms_ref, out_acc, terms_acc,
+    grads_too, second_ref, grad_ref, expand_ref, reduce_ref, bias_ref, *refs,
 ):
+    if grads_too:
+        far_ref, hid_ref, back_ref, bsum_ref, out_ref, terms_ref, dred_ref, out_acc, terms_acc, hidden_ref = refs
+    else:
+        hidden_ref, back_ref, bsum_ref, out_ref, terms_ref, out_acc, terms_acc = refs
     step = pl.program_id(0)
     rows = second_ref.shape[0]
     pieces = row_pieces(rows, 376 if rows % 376 == 0 else 256)
@@ -629,6 +632,9 @@
         out_acc[take, :] += dot_nt(hidden, reduce)
         current = coming
     bsum_ref[...] = sums
+    if grads_too:
+        total = dot_tn(far_ref[...], hid_ref[...]) + dot_tn(grad_ref[...], hidden_ref[...])
+        dred_ref[...] = total.astype(jnp.bfloat16)
 
     @pl.when(step == pl.num_programs(0) - 1)
     def _():
@@ -636,67 +642,41 @@
         terms_ref[...] = terms_acc[...].astype(jnp.bfloat16)
 
 
-def feed(second, grads, pack, bias, units):
+def feed(second, grads, pack, bias, units, far=None):
     rows, width = second.shape
     block = 512 if units % 512 == 0 else units
+    steps = units // block
     wide = pl.BlockSpec((rows, block), lambda j: (0, j))
-    steps = units // block
     weights = [
         pl.BlockSpec((width, block), lambda j: (0, j)),
         pl.BlockSpec((width, block), lambda j: (0, j + steps)),
     ]
     line = pl.BlockSpec((1, block), lambda j: (0, j))
+    hidden = jax.ShapeDtypeStruct((rows, units), jnp.bfloat16)
+    full = jax.ShapeDtypeStruct((rows, width), jnp.bfloat16)
+    outs = [hidden, jax.ShapeDtypeStruct((1, units), jnp.float32), full, full]
+    out_specs = [wide, line, whole((rows, width)), whole((rows, width))]
+    scratch = [pltpu.VMEM((rows, width), jnp.float32)] * 2
+    in_specs = [whole((rows, width)), whole((rows, width)), *weights, line]
+    if far is None:
+        outs, out_specs = [hidden] + outs, [wide] + out_specs
+    else:
+        outs = outs + [jax.ShapeDtypeStruct((width, units), jnp.bfloat16)]
+        out_specs = out_specs + [weights[0]]
+        in_specs = in_specs + [whole((rows, width)), wide]
+        scratch = scratch + [pltpu.VMEM((rows, block), jnp.bfloat16)]
+    flops = (8 if far is None else 12) * rows * width * units
     return pl.pallas_call(
-        feed_kernel,
-        out_shape=(
-            jax.ShapeDtypeStruct((rows, units), jnp.bfloat16),
-            jax.ShapeDtypeStruct((rows, units), jnp.bfloat16),
-            jax.ShapeDtypeStruct((1, units), jnp.float32),
-            jax.ShapeDtypeStruct((rows, width), jnp.bfloat16),
-            jax.ShapeDtypeStruct((rows, width), jnp.bfloat16),
-        ),
-        grid=(units // block,),
-        in_specs=[whole((rows, width)), whole((rows, width)), *weights, line],
-        out_specs=(wide, wide, line, whole((rows, width)), whole((rows, width))),
-        scratch_shapes=[pltpu.VMEM((rows, width), jnp.float32)] * 2,
+        functools.partial(feed_kernel, far is not None),
+        out_shape=tuple(outs),
+        grid=(steps,),
+        in_specs=in_specs,
+        out_specs=tuple(out_specs),
+        scratch_shapes=scratch,
         compiler_params=kernel_params(),
-        cost_estimate=cost(8 * rows * width * units, 8 * rows * (units + width) + 4 * width * units),
-        name="feed",
-    )(second, grads, pack, pack, bias)
-
-
-def feed_grad_kernel(go_ref, gt_ref, so_ref, st_ref, ho_ref, ht_ref, bo_ref, bt_ref, out_ref):
-    step = pl.program_id(0)
-    half = pl.num_programs(0) // 2
-
-    @pl.when(step < half)
-    def _():
-        total = dot_tn(go_ref[...], ho_ref[...]) + dot_tn(gt_ref[...], ht_ref[...])
-        out_ref[...] = total.astype(jnp.bfloat16)
-
-    @pl.when(step >= half)
-    def _():
-        total = dot_tn(so_ref[...], bo_ref[...]) + dot_tn(st_ref[...], bt_ref[...])
-        out_ref[...] = total.astype(jnp.bfloat16)
-
-
-def feed_grads(grads, second, hidden, back):
-    rows, width = grads[0].shape
-    units = hidden[0].shape[1]
-    block = 512 if units % 512 == 0 else units
-    steps = units // block
-    early = pl.BlockSpec((rows, block), lambda j: (0, jnp.minimum(j, steps - 1)))
-    late = pl.BlockSpec((rows, block), lambda j: (0, jnp.maximum(j - steps, 0)))
-    return pl.pallas_call(
-        feed_grad_kernel,
-        out_shape=jax.ShapeDtypeStruct((width, 2 * units), jnp.bfloat16),
-        grid=(2 * steps,),
-        in_specs=[whole((rows, width))] * 4 + [early] * 2 + [late] * 2,
-        out_specs=pl.BlockSpec((width, block), lambda j: (0, j)),
-        compiler_params=kernel_params(),
-        cost_estimate=cost(8 * rows * width * units, 8 * rows * (width + units) + 4 * width * units),
-        name="feed_grads",
-    )(*grads, *second, *hidden, *back)
+        cost_estimate=cost(flops, 8 * rows * (units + width) + 4 * width * units, COSTS["feed"]),
+        name="feed" if far is None else "feed_last",
+    )(second, grads, pack, pack, bias, *(far or ()))
 
 
 def head_grad_kernel(count, lo_ref, lt_ref, *refs):
@@ -723,7 +703,7 @@
         in_specs=[left] * 2 + [whole(pack.shape) for pack in (*own, *far)],
         out_specs=pl.BlockSpec((block, units), lambda j: (j, 0)),
         compiler_params=kernel_params(),
-        cost_estimate=cost(4 * rows * width * units, 4 * rows * (width + units) + 2 * width * units),
+        cost_estimate=cost(4 * rows * width * units, 4 * rows * (width + units) + 2 * width * units, COSTS["head_grad"]),
         name="head_grad",
     )(*lefts, *own, *far)
 
@@ -794,31 +774,47 @@
         ],
         out_specs=(full, full, whole((cols, rows)), whole((cols, rows)), whole((4, width))),
         compiler_params=kernel_params(),
-        cost_estimate=cost(4 * rows * width * cols, 18 * rows * width),
+        cost_estimate=cost(4 * rows * width * cols, 18 * rows * width, COSTS["branch_back"]),
         name="branch_back",
     )(own, far, middle, grads, gain, pack, pack)
 
 
-def out_grad_kernel(branch_ref, co_ref, ct_ref, out_ref):
-    cols = co_ref.shape[0]
-    branch = branch_ref[...]
-    out_ref[:, :cols] = dot_tn(branch, co_ref[...].T).astype(jnp.bfloat16)
-    out_ref[:, cols:] = dot_tn(branch, ct_ref[...].T).astype(jnp.bfloat16)
-
-
-def out_weight_grad(branch, context_own, context_far):
+def side_grad_kernel(
+    so_ref, st_ref, bo_ref, bt_ref, branch_ref, co_ref, ct_ref, out_ref
+):
+    step = pl.program_id(0)
+    last = pl.num_programs(0) - 1
+
+    @pl.when(step < last - 1)
+    def _():
+        total = dot_tn(so_ref[...], bo_ref[...]) + dot_tn(st_ref[...], bt_ref[...])
+        out_ref[...] = total.astype(jnp.bfloat16)
+
+    @pl.when(step == last - 1)
+    def _():
+        out_ref[...] = dot_tn(branch_ref[...], co_ref[...].T).astype(jnp.bfloat16)
+
+    @pl.when(step == last)
+    def _():
+        out_ref[...] = dot_tn(branch_ref[...], ct_ref[...].T).astype(jnp.bfloat16)
+
+
+def side_grads(second, back, branch, contexts):
     rows, width = branch.shape
-    cols = context_own.shape[0]
+    units, cols = back[0].shape[1], contexts[0].shape[0]
+    steps = units // cols
+    part = pl.BlockSpec((rows, cols), lambda j: (0, jnp.minimum(j, steps - 1)))
     return pl.pallas_call(
-        out_grad_kernel,
-        out_shape=jax.ShapeDtypeStruct((width, 2 * cols), jnp.bfloat16),
-        grid=(1,),
-        in_specs=[whole((rows, width)), whole((cols, rows)), whole((cols, rows))],
-        out_specs=whole((width, 2 * cols)),
+        side_grad_kernel,
+        out_shape=jax.ShapeDtypeStruct((width, units + 2 * cols), jnp.bfloat16),
+        grid=(steps + 2,),
+        in_specs=[whole((rows, width))] * 2 + [part] * 2
+        + [whole((rows, width))] + [whole((cols, rows))] * 2,
+        out_specs=pl.BlockSpec((width, cols), lambda j: (0, j)),
         compiler_params=kernel_params(),
-        cost_estimate=cost(4 * rows * width * cols, 4 * rows * width + 4 * width * cols),
-        name="out_weight_grad",
-    )(branch, context_own, context_far)
+        cost_estimate=cost(4 * rows * width * (units + cols), 4 * rows * (width + units), COSTS["weight_grad"]),
+        name="side_grads",
+    )(*second, *back, branch, *contexts)
 
 
 def first_kernel(count, *refs):
@@ -875,7 +871,7 @@
         out_specs=(whole((rows, width)), whole((2, width)), whole((1, wide))),
         scratch_shapes=[pltpu.VMEM((rows, wide), jnp.bfloat16)],
         compiler_params=kernel_params(),
-        cost_estimate=cost(2 * rows * width * wide, 2 * (rows + width) * wide + 4 * rows * width),
+        cost_estimate=cost(2 * rows * width * wide, 2 * (rows + width) * wide + 4 * rows * width, COSTS["first_back"]),
         name="first_back",
     )(*packs, weights, frames)
 
@@ -905,7 +901,7 @@
         in_specs=[spec] * 4 + [whole((1, width))],
         out_specs=spec,
         compiler_params=kernel_params(),
-        cost_estimate=cost(20 * rows * width, 12 * rows * width),
+        cost_estimate=cost(20 * rows * width, 12 * rows * width, COSTS["frames_back"]),
         name="frames_back",
     )(frames, own, far, mgrad, gain)
 
@@ -950,20 +946,6 @@
     other = lax.ppermute(chosen(1 - mine), "fsdp", [(i, i ^ bit) for i in range(fsdp)])
     total = chosen(mine).astype(jnp.float32) + other.astype(jnp.float32)
     return (total if last else total.astype(jnp.bfloat16)).reshape(-1, total.shape[-1])
-
-
-def scatter_steps(held, fsdp):
-    index = lax.axis_index("fsdp")
-    bit = fsdp // 2
-    while bit >= 1:
-        low = (index & bit) == 0
-        first, second = held[:bit], held[bit:]
-        send = jnp.where(low, second, first)
-        held = jnp.where(low, first, second) + lax.ppermute(
-            send, "fsdp", [(i, i ^ bit) for i in range(fsdp)]
-        )
-        bit //= 2
-    return held[0]
 
 
 def per_device_pair(
@@ -1035,22 +1017,21 @@
     )
     terms_send, second_own = tie(terms_send, second_own)
     terms_far = swap_tp(terms_send)
-    hid_own, back_own, bsum_own, out_own, terms_own = feed(
-        second_own, out_grad, pack_two, bias_e, units
-    )
+    back_own, bsum_own, out_own, terms_own, d_reduce = feed(
+        second_own, out_grad, pack_two, bias_e, units, (grads_far, hid_far)
+    )
+    g_reduce = lax.psum_scatter(d_reduce, "fsdp", scatter_dimension=0, tiled=True)
     mgrad, branch, up_own, up_send, sums_two = branch_back(
         terms_own, terms_far, middle, out_grad, gain_two, pack_one, cols
     )
     up_send, second_own = tie(up_send, second_own)
     up_far = swap_tp(up_send)
-    d_feed = feed_grads(
-        (out_grad, grads_far), (second_own, second_far), (hid_own, hid_far), (back_own, back_far)
-    )
-    g_feed = lax.psum_scatter(d_feed, "fsdp", scatter_dimension=0, tiled=True)
-    d_out = out_weight_grad(branch, context_own, context_far)
+    d_side = side_grads(
+        (second_own, second_far), (back_own, back_far), branch, (context_own, context_far)
+    )
 
     turned = (heads, HD, rows)
-    up_far, d_out, out_send = tie(up_far, d_out, out_send)
+    up_far, out_send, d_side = tie(up_far, out_send, d_side)
     out_far = swap_tp(out_send)
     ups = (up_own.reshape(turned), up_far.reshape(turned))
     steps = halving_order(fsdp)
@@ -1061,52 +1042,23 @@
             (q_first, q_far), (k_own, k_far), (v_own, v_far), ups, (log_own, log_far), start, count
         )
 
-    many = heads // 2
-    few = many // 2
+    many = (heads + 1) // 2
     own_a, far_a = back(q_own, 0, many)
+    own_a, out_far, d_side = tie(own_a, out_far, d_side)
+    g_side = lax.psum_scatter(d_side, "fsdp", scatter_dimension=0, tiled=True)
     d_heads = head_grad(firsts, [own_a], [far_a])
-    d_heads, q_own = tie(d_heads, q_own)
-    held_a = [d_out, d_heads]
-    own_b, far_b = back(q_own, many, few)
-    held_a = halve(held_a, steps[0], steps, fsdp)
-    own_b, held_a, q_own = tie(own_b, held_a, q_own)
-    own_c, far_c = back(q_own, many + few, many - few)
+    held_a = halve(d_heads, steps[0], steps, fsdp)
+    held_a, q_own = tie(held_a, q_own)
+    own_b, far_b = back(q_own, many, heads - many)
     held_a = halve(held_a, steps[1], steps[1:], fsdp)
-    far_c, out_far = tie(far_c, out_far)
-    first_send, sums_far, bias_far = first_back([far_a, far_b, far_c], pack_one, frames_far)
-    first_send, far_c = tie(first_send, far_c)
+    held_a, far_b = tie(held_a, far_b)
+    first_send, sums_far, bias_far = first_back([far_a, far_b], pack_one, frames_far)
+    first_send, far_b = tie(first_send, far_b)
     first_recv = swap_tp(first_send)
-    held_b = head_grad(firsts, [own_b, own_c], [far_b, far_c])
-    held_b, own_c = tie(held_b, own_c)
-    first_keep, sums_own, bias_own = first_back([own_a, own_b, own_c], pack_one, frames)
-    held_b = halve(held_b, steps[0], steps, fsdp)
-    held_b = halve(held_b, steps[1], steps[1:], fsdp)
-    frames_grad = frames_back(frames, first_keep, first_recv, mgrad, gain_one)
-    out_frames = (
-        middle + out_own.astype(jnp.float32) + out_far.astype(jnp.float32) + reduce_bias
-    ).astype(jnp.bfloat16)
-    for place in range(2, len(steps)):
-        last = place + 1 == len(steps)
-        held_a = halve(held_a, steps[place], steps[place:], fsdp, last)
-        if place == 2:
-            held_b, frames_grad, out_frames = tie(held_b, frames_grad, out_frames)
-        held_b = halve(held_b, steps[place], steps[place:], fsdp, last)
-    g_out, held_a = held_a[:, : 2 * cols], held_a[:, 2 * cols :]
-    some, fewer = many * HD, few * HD
-
-    def joined(kind):
-        ends = 3 * fewer
-        return jnp.concatenate(
-            [
-                held_a[:, kind * some : (kind + 1) * some],
-                held_b[:, kind * fewer : (kind + 1) * fewer],
-                held_b[:, ends + kind * (some - fewer) : ends + (kind + 1) * (some - fewer)],
-            ],
-            axis=1,
-        )
-
-    g_query, g_key, g_value = joined(0), joined(1), joined(2)
-
+    held_b = head_grad(firsts, [own_b], [far_b])
+    held_b, own_b = tie(held_b, own_b)
+    first_keep, sums_own, bias_own = first_back([own_a, own_b], pack_one, frames)
+    held_a = halve(held_a, steps[2], steps[2:], fsdp, len(steps) == 3)
     sums_one = sums_own + sums_far
     bias_sum = bias_own + bias_far
     wide_sums = jnp.concatenate([sums_one, sums_two])
@@ -1120,14 +1072,47 @@
         ],
         axis=1,
     )
-    small_sum = scatter_steps(tall, fsdp)
+    wide = held_b.shape[1]
+    extra = -(-tall.shape[1] // (8 * wide)) * 8
+    tall = jnp.pad(tall, ((0, 0), (0, extra * wide - tall.shape[1]))).astype(jnp.bfloat16)
+    lots = width // fsdp
+    held_b = jnp.concatenate(
+        [held_b.reshape(fsdp, lots, wide), tall.reshape(fsdp, extra, wide)], axis=1
+    ).reshape(-1, wide)
+    held_b = halve(held_b, steps[0], steps, fsdp)
+    held_b = halve(held_b, steps[1], steps[1:], fsdp)
+    out_frames = (
+        middle + out_own.astype(jnp.float32) + out_far.astype(jnp.float32) + reduce_bias
+    ).astype(jnp.bfloat16)
+    for place in range(2, len(steps)):
+        last = place + 1 == len(steps)
+        if place > 2:
+            held_a = halve(held_a, steps[place], steps[place:], fsdp, last)
+        if last:
+            held_a, held_b, first_keep, out_frames = tie(held_a, held_b, first_keep, out_frames)
+            frames_grad = frames_back(frames, first_keep, first_recv, mgrad, gain_one)
+            held_b, frames_grad, g_side = tie(held_b, frames_grad, g_side)
+        held_b = halve(held_b, steps[place], steps[place:], fsdp, last)
+    held_b, small_sum = held_b[:lots], held_b[lots:].reshape(-1)
+    g_expand, g_out = g_side[:, :units], g_side[:, units:]
+    some = many * HD
+
+    def joined(kind):
+        rest = cols - some
+        return jnp.concatenate(
+            [held_a[:, kind * some : (kind + 1) * some], held_b[:, kind * rest : (kind + 1) * rest]], axis=1
+        )
+
+    g_query, g_key, g_value = joined(0), joined(1), joined(2)
+
     six = small_sum[: 12 * lot].reshape(2, 6 * lot)
     keep = lax.dynamic_index_in_dim(six, side, 0, keepdims=False)
     send = lax.dynamic_index_in_dim(six, 1 - side, 0, keepdims=False)
     six = (keep + swap_tp(send)).reshape(6, lot)
     rest = small_sum[12 * lot :]
-    g_bq, g_bv, g_be = rest[:part], rest[part : 2 * part], rest[2 * part :]
-    g_out_sum = g_out[:, :cols] + swap_tp(g_out[:, cols:].astype(jnp.bfloat16)).astype(jnp.float32)
+    g_bq, g_bv = rest[:part], rest[part : 2 * part]
+    g_be = rest[2 * part : 2 * part + b_expand.shape[0]]
+    g_out_sum = g_out[:, :cols].astype(jnp.float32) + swap_tp(g_out[:, cols:]).astype(jnp.float32)
     return (
         out_frames[None],
         frames_grad[None],
@@ -1138,9 +1123,9 @@
         g_bv,
         g_out_sum.T,
         six[4],
-        g_feed[:, units:].astype(jnp.float32),
+        g_expand.astype(jnp.float32),
         g_be,
-        g_feed[:, :units].T.astype(jnp.float32),
+        g_reduce.T.astype(jnp.float32),
         six[5],
         six[0],
         six[1],

time: 595 us -> 555 us (0.933)
  waiting for transfers between devices: 193 us -> 164 us
    ppermute x8, waiting for transfers between devices: 70.6 us -> 46.9 us  [halve(): lax.ppermute(chosen(1 - mine), 'fsdp', [(i, i ^ bit) for i in range(fsdp)])]
    pallas_call x4 -> x3, Pallas kernels: 101 us -> 99 us  [the longest x2 76.7 us: feed(): pl.pallas_call(functools.partial(feed_kernel, far is not None), out_shape...]
    pallas_call x3 -> x2, Pallas kernels: 63.3 us -> 61.8 us  [attend_back_rows(): pl.pallas_call(attend_back_kernel, out_shape=(jax.ShapeDtypeStruct(packed...]
  transfers between devices with their start and end apart: 31 -> 28, of which waited for: 20 -> 17; matrix products, arithmetic and copies ran while one was open for 9% -> 9% of each run, Pallas kernels for 41% -> 45%
where the time goes in v3:
time: 555 us; the launch traced here: 546 us
  Pallas kernels  279 us (50%)
  waiting for transfers between devices  164 us (30%)
  local copies, waits for them, and re-layouts  31.4 us (6%)
  starting transfers between devices  29.4 us (5%)
  other arithmetic  27.2 us (5%)
  between operations  14.7 us (3%)
    ppermute x12, waiting for transfers between devices, swap_tp(): return lax.ppermute(piece, 'tp', [(0, 1), (1, 0)])  85.1 us
    pallas_call x2, Pallas kernels, feed(): pl.pallas_call(functools.partial(feed_kernel, far is not None), out_shape...  76.7 us
    pallas_call x2, Pallas kernels, attend_back_rows(): pl.pallas_call(attend_back_kernel, out_shape=(jax.ShapeDtypeStruct(packed...  61.8 us
    ppermute x8, waiting for transfers between devices, halve(): lax.ppermute(chosen(1 - mine), 'fsdp', [(i, i ^ bit) for i in range(fsdp)])  46.9 us
    pallas_call x2, Pallas kernels, attend_rows(): pl.pallas_call(attend_kernel, out_shape=(jax.ShapeDtypeStruct((heads, HD,...  30.7 us
    all_gather x1, waiting for transfers between devices, per_device_pair(): lax.all_gather(jnp.concatenate([w_query, w_key, w_value, out_turned, out_...  26.4 us
    pallas_call x1, Pallas kernels, side_grads(): pl.pallas_call(side_grad_kernel, out_shape=jax.ShapeDtypeStruct((width, u...  22.3 us
    pallas_call x2, Pallas kernels, project(): pl.pallas_call(functools.partial(project_kernel, heads), out_shape=(jax.S...  20.6 us
  transfers between devices with their start and end apart: 28, of which 17 were waited for; matrix products, arithmetic and copies ran while one was open for 9% of the time, Pallas kernels for 45%

profile of v3, /device:TPU:0, one launch (start us, length us, event | category | flops | bytes accessed | tf_op | source)
XLA Modules:
  0.0 545.6 jit_solution(3323656314275793669)
XLA Ops:
  7.2 3.0 collective-permute-start.1
  18.4 2.6 collective-permute-done
  31.0 2.5 collective-permute-start.5
  42.3 21.1 %collective-permute-done.6.frames_ref.refs_3_ = bf16[752,1280]{1,0:T(8,128)(2,1)} collective-permute-done((bf16[752,1280]{1,0:T(8,128)(2,1)S(1)}, bf16[752,1280]{1,0:T(8,128)(2,1)}, u32[]{:S(2)}, u32[]{:S(2)}) %collective-permute-start.6) | collective-permute-done | bytes 1925152 | tf_op jit(solution)/shard_map/ppermute | solution.py:910
  63.7 26.4 %all-gather.3.cloned.1.call-done.weight_ref.wo_ref.wt_ref.refs_2_ = bf16[1280,3200]{1,0:T(8,128)(2,1)} async-done(((bf16[80,3200]{1,0:T(8,128)(2,1)}), bf16[1280,3200]{1,0:T(8,128)(2,1)}) %all-gather.3.cloned.1.call-update) | async-done | bytes 8192016 | tf_op jit(solution)/shard_map/all_gather | solution.py:975
  90.1 10.3 %project.2 = (bf16[752,1280]{1,0:T(8,128)(2,1)}, bf16[8,752,128]{2,1,0:T(8,128)(2,1)}, bf16[8,752,128]{2,1,0:T(8,128)(2,1)}, bf16[8,752,128]{2,1,0:T(8,128)(2,1)}) custom-call(s32[2]{0:T(128)} %get-tuple-element.185.scal_ref, bf16[752,1280]{1,0:T(8,128)(2,1)} %bitcast.89, f32[1,1280]{1,0:T(1,128)} %squeeze.80.gain_ref, f32[1,1280]{1,0:T(1,128)} %squeeze.81.shift_ref, ...), custom_call_target="tpu_custom_call" | custom-call | flops 11088691200 | bytes 8765440 | tf_op jit(solution)/shard_map/project/pallas_call | solution.py:404
  100.4 10.3 %project.3 = (bf16[752,1280]{1,0:T(8,128)(2,1)}, bf16[8,752,128]{2,1,0:T(8,128)(2,1)}, bf16[8,752,128]{2,1,0:T(8,128)(2,1)}, bf16[8,752,128]{2,1,0:T(8,128)(2,1)}) custom-call(s32[2]{0:T(128)} %get-tuple-element.186.scal_ref, bf16[752,1280]{1,0:T(8,128)(2,1)} %collective-permute-done.6.frames_ref.refs_3_, f32[1,1280]{1,0:T(1,128)} %squeeze.80.gain_ref, ...), custom_call_target="tpu_custom_call" | custom-call | flops 11088691200 | bytes 8765440 | tf_op jit(solution)/shard_map/project/pallas_call | solution.py:404
  110.7 15.5 %attend.2 = (bf16[8,80,752]{2,1,0:T(8,128)(2,1)}, f32[8,1,752]{2,1,0:T(1,128)}) custom-call(bf16[8,752,128]{2,1,0:T(8,128)(2,1)} %get-tuple-element.92.q_ref.qt_ref, bf16[8,752,128]{2,1,0:T(8,128)(2,1)} %get-tuple-element.93.ko_ref, bf16[8,752,128]{2,1,0:T(8,128)(2,1)} %get-tuple-element.94.kt_ref, bf16[8,752,128]{2,1,0:T(8,128)(2,1)} %get-tuple-element.95.vo_ref, ...), custom_call_target="tpu_custom_call" | custom-call | flops 43430707200 | bytes 9240576 | tf_op jit(solution)/shard_map/attend/pallas_call | solution.py:453
  129.7 15.3 %attend.3 = (bf16[8,80,752]{2,1,0:T(8,128)(2,1)}, f32[8,1,752]{2,1,0:T(1,128)}) custom-call(bf16[8,752,128]{2,1,0:T(8,128)(2,1)} %get-tuple-element.127.q_ref.qo_ref, bf16[8,752,128]{2,1,0:T(8,128)(2,1)} %get-tuple-element.93.ko_ref, bf16[8,752,128]{2,1,0:T(8,128)(2,1)} %get-tuple-element.94.kt_ref, bf16[8,752,128]{2,1,0:T(8,128)(2,1)} %get-tuple-element.95.vo_ref, ...), custom_call_target="tpu_custom_call" | custom-call | flops 43430707200 | bytes 9240576 | tf_op jit(solution)/shard_map/attend/pallas_call | solution.py:453
  145.0 6.7 %collective-permute-done.7 = bf16[640,752]{0,1:T(8,128)(2,1)S(1)} collective-permute-done((bf16[640,752]{0,1:T(8,128)(2,1)S(1)}, bf16[640,752]{0,1:T(8,128)(2,1)S(1)}, u32[]{:S(2)}, u32[]{:S(2)}) %collective-permute-start.7) | collective-permute-done | bytes 962592 | tf_op jit(solution)/shard_map/ppermute | solution.py:910
  153.5 9.1 %merge_heads.1 = (f32[752,1280]{1,0:T(8,128)}, bf16[752,1280]{1,0:T(8,128)(2,1)}) custom-call(bf16[640,752]{1,0:T(8,128)(2,1)} %bitcast.124, bf16[640,752]{1,0:T(8,128)(2,1)} %copy.38.ct_ref, bf16[1280,3200]{1,0:T(8,128)(2,1)} %all-gather.3.cloned.1.call-done.weight_ref.wo_ref.wt_ref.refs_2_, ...), custom_call_target="tpu_custom_call" | custom-call | flops 7392460800 | bytes 12902400 | tf_op jit(solution)/shard_map/merge_heads/pallas_call | solution.py:577
  164.8 41.5 %collective-permute-done.8.second_ref.st_ref = bf16[752,1280]{1,0:T(8,128)(2,1)} collective-permute-done((bf16[752,1280]{1,0:T(8,128)(2,1)}, bf16[752,1280]{1,0:T(8,128)(2,1)}, u32[]{:S(2)}, u32[]{:S(2)}) %collective-permute-start.8) | collective-permute-done | bytes 1925152 | tf_op jit(solution)/shard_map/ppermute | solution.py:910
  206.3 33.0 %feed.1 = (bf16[752,2560]{1,0:T(8,128)(2,1)}, bf16[752,2560]{1,0:T(8,128)(2,1)}, f32[1,2560]{1,0:T(1,128)}, bf16[752,1280]{1,0:T(8,128)(2,1)}, bf16[752,1280]{1,0:T(8,128)(2,1)}) custom-call(bf16[752,1280]{1,0:T(8,128)(2,1)} %collective-permute-done.8.second_ref.st_ref, bf16[752,1280]{1,0:T(8,128)(2,1)} %collective-permute-done.9.grad_ref.refs_0_, ...), custom_call_target="tpu_custom_call" | custom-call | flops 59139686400 | bytes 36208640 | tf_op jit(solution)/shard_map/feed/pallas_call | solution.py:669
  240.8 43.7 %feed_last.1 = (bf16[752,2560]{1,0:T(8,128)(2,1)}, f32[1,2560]{1,0:T(1,128)}, bf16[752,1280]{1,0:T(8,128)(2,1)}, bf16[752,1280]{1,0:T(8,128)(2,1)}, bf16[1280,2560]{1,0:T(8,128)(2,1)}) custom-call(bf16[752,1280]{1,0:T(8,128)(2,1)} %get-tuple-element.114.second_ref.so_ref, bf16[752,1280]{1,0:T(8,128)(2,1)} %bitcast.122, ...), custom_call_target="tpu_custom_call" | custom-call | flops 88709529600 | bytes 36208640 | tf_op jit(solution)/shard_map/feed_last/pallas_call | solution.py:669
  286.1 13.3 %branch_back.1 = (f32[752,1280]{1,0:T(8,128)}, bf16[752,1280]{1,0:T(8,128)(2,1)}, bf16[640,752]{1,0:T(8,128)(2,1)}, bf16[640,752]{1,0:T(8,128)(2,1)}, f32[4,1280]{1,0:T(4,128)}) custom-call(bf16[752,1280]{1,0:T(8,128)(2,1)} %get-tuple-element.107.own_ref, bf16[752,1280]{1,0:T(8,128)(2,1)} %copy-done.26, f32[752,1280]{1,0:T(8,128)} %get-tuple-element.109.middle_ref, ...), custom_call_target="tpu_custom_call" | custom-call | flops 7392460800 | bytes 17326080 | tf_op jit(solution)/shard_map/branch_back/pallas_call | solution.py:762
  301.7 22.3 %side_grads.1 = bf16[1280,3840]{1,0:T(8,128)(2,1)} custom-call(bf16[752,1280]{1,0:T(8,128)(2,1)} %get-tuple-element.114.second_ref.so_ref, bf16[752,1280]{1,0:T(8,128)(2,1)} %collective-permute-done.8.second_ref.st_ref, bf16[752,2560]{1,0:T(8,128)(2,1)} %get-tuple-element.115.bo_ref, bf16[752,2560]{1,0:T(8,128)(2,1)} %get-tuple-element.116.bt_ref, ...), custom_call_target="tpu_custom_call" | custom-call | flops 36962304000 | bytes 11550720 | tf_op jit(solution)/shard_map/side_grads/pallas_call | solution.py:807
  327.6 30.7 %attend_back.2 = (bf16[752,960]{1,0:T(8,128)(2,1)}, bf16[752,960]{1,0:T(8,128)(2,1)}) custom-call(bf16[8,752,128]{2,1,0:T(8,128)(2,1)} %get-tuple-element.127.q_ref.qo_ref, bf16[8,752,128]{2,1,0:T(8,128)(2,1)} %get-tuple-element.92.q_ref.qt_ref, bf16[8,752,128]{2,1,0:T(8,128)(2,1)} %get-tuple-element.93.ko_ref, ...), custom_call_target="tpu_custom_call" | custom-call | flops 130292121600 | bytes 9240576 | tf_op jit(solution)/shard_map/attend_back/pallas_call | solution.py:536
  358.3 9.6 %collective-permute-done.12 = bf16[752,1280]{1,0:T(8,128)(2,1)} collective-permute-done((bf16[752,1280]{1,0:T(8,128)(2,1)S(1)}, bf16[752,1280]{1,0:T(8,128)(2,1)}, u32[]{:S(2)}, u32[]{:S(2)}) %collective-permute-start.12) | collective-permute-done | bytes 1925152 | tf_op jit(solution)/shard_map/ppermute | solution.py:910
  367.9 8.7 %head_grad.2 = bf16[1280,960]{1,0:T(8,128)(2,1)} custom-call(bf16[752,1280]{1,0:T(8,128)(2,1)} %get-tuple-element.88.lo_ref, bf16[752,1280]{1,0:T(8,128)(2,1)} %get-tuple-element.91.lt_ref, bf16[752,960]{1,0:T(8,128)(2,1)} %get-tuple-element.124.refs_0_, bf16[752,960]{1,0:T(8,128)(2,1)} %get-tuple-element.125.refs_1_.refs_0_), custom_call_target="tpu_custom_call" | custom-call | flops 73924608 | bytes 183910 | tf_op jit(solution)/shard_map/head_grad/pallas_call | solution.py:699
  376.6 2.6 dynamic-slice_bitcast_fusion
  379.2 3.4 collective-permute-done.13
  386.6 31.2 %attend_back.3 = (bf16[752,960]{1,0:T(8,128)(2,1)}, bf16[752,960]{1,0:T(8,128)(2,1)}) custom-call(bf16[8,752,128]{2,1,0:T(8,128)(2,1)} %get-tuple-element.127.q_ref.qo_ref, bf16[8,752,128]{2,1,0:T(8,128)(2,1)} %get-tuple-element.92.q_ref.qt_ref, bf16[8,752,128]{2,1,0:T(8,128)(2,1)} %get-tuple-element.93.ko_ref, ...), custom_call_target="tpu_custom_call" | custom-call | flops 325730304 | bytes 184811 | tf_op jit(solution)/shard_map/attend_back/pallas_call | solution.py:536
  418.0 10.2 %first_back.2 = (bf16[752,1280]{1,0:T(8,128)(2,1)}, f32[2,1280]{1,0:T(2,128)}, f32[1,1920]{1,0:T(1,128)}) custom-call(bf16[752,960]{1,0:T(8,128)(2,1)} %get-tuple-element.125.refs_1_.refs_0_, bf16[752,960]{1,0:T(8,128)(2,1)} %get-tuple-element.133.refs_1_, bf16[1280,3200]{1,0:T(8,128)(2,1)} %all-gather.3.cloned.1.call-done.weight_ref.wo_ref.wt_ref.refs_2_, ...), custom_call_target="tpu_custom_call" | custom-call | flops 73924608 | bytes 233062 | tf_op jit(solution)/shard_map/first_back/pallas_call | solution.py:862
  428.2 8.8 %head_grad.3 = bf16[1280,960]{1,0:T(8,128)(2,1)} custom-call(bf16[752,1280]{1,0:T(8,128)(2,1)} %get-tuple-element.88.lo_ref, bf16[752,1280]{1,0:T(8,128)(2,1)} %get-tuple-element.91.lt_ref, bf16[752,960]{1,0:T(8,128)(2,1)} %get-tuple-element.135.refs_0_.refs_1_, bf16[752,960]{1,0:T(8,128)(2,1)} %get-tuple-element.133.refs_1_), custom_call_target="tpu_custom_call" | custom-call | flops 73924608 | bytes 183910 | tf_op jit(solution)/shard_map/head_grad/pallas_call | solution.py:699
  437.0 10.3 %first_back.3 = (bf16[752,1280]{1,0:T(8,128)(2,1)}, f32[2,1280]{1,0:T(2,128)}, f32[1,1920]{1,0:T(1,128)}) custom-call(bf16[752,960]{1,0:T(8,128)(2,1)} %get-tuple-element.124.refs_0_, bf16[752,960]{1,0:T(8,128)(2,1)} %get-tuple-element.135.refs_0_.refs_1_, bf16[1280,3200]{1,0:T(8,128)(2,1)} %all-gather.3.cloned.1.call-done.weight_ref.wo_ref.wt_ref.refs_2_, ...), custom_call_target="tpu_custom_call" | custom-call | flops 73924608 | bytes 233062 | tf_op jit(solution)/shard_map/first_back/pallas_call | solution.py:862
  452.7 3.5 collective-permute-done.17
  465.4 29.2 %collective-permute-done.15 = bf16[1,160,960]{2,1,0:T(8,128)(2,1)} collective-permute-done((bf16[1,160,960]{2,1,0:T(8,128)(2,1)}, bf16[1,160,960]{2,1,0:T(8,128)(2,1)}, u32[]{:S(2)}, u32[]{:S(2)}) %collective-permute-start.15) | collective-permute-done | bytes 307232 | tf_op jit(solution)/shard_map/ppermute | solution.py:946
  496.1 3.8 collective-permute-start.19
  499.8 4.8 add_convert_fusion
  504.9 10.3 %collective-permute-done.19 = bf16[1,176,960]{2,1,0:T(8,128)(2,1)S(1)} collective-permute-done((bf16[1,176,960]{2,1,0:T(8,128)(2,1)S(1)}, bf16[1,176,960]{2,1,0:T(8,128)(2,1)S(1)}, u32[]{:S(2)}, u32[]{:S(2)}) %collective-permute-start.19) | collective-permute-done | bytes 337952 | tf_op jit(solution)/shard_map/ppermute | solution.py:946
  515.3 6.5 %frames_back.1 = bf16[752,1280]{1,0:T(8,128)(2,1)} custom-call(bf16[752,1280]{1,0:T(8,128)(2,1)} %bitcast.92, bf16[752,1280]{1,0:T(8,128)(2,1)} %get-tuple-element.148.own_ref, bf16[752,1280]{1,0:T(8,128)(2,1)} %collective-permute-done.20.far_ref, f32[752,1280]{1,0:T(8,128)} %get-tuple-element.150.mgrad_ref, f32[1,1280]{1,0:T(1,128)} %squeeze.80.gain_ref), custom_call_target="tpu_custom_call" | custom-call | flops 385024 | bytes 231014 | tf_op jit(solution)/shard_map/frames_back/pallas_call | solution.py:897
  527.8 3.6 collective-permute-done.22
  (190 shorter events, 77.4 us)
Async XLA Ops:
  7.2 82.9 %all-gather.3.cloned.1.call-start = ((), (), s32[]{:S(2)}) async-start(), calls=%async_computation.2 | async-start | bytes 8704000 | tf_op jit(solution)/shard_map/all_gather | solution.py:975
  7.2 6.9 %collective-permute-start.1 = (bf16[80,640]{1,0:T(8,128)(2,1)}, bf16[80,640]{1,0:T(8,128)(2,1)S(1)}, u32[]{:S(2)}, u32[]{:S(2)}) collective-permute-start(bf16[80,640]{1,0:T(8,128)(2,1)} %bitcast.118), channel_id=1, source_target_pairs={{0,1},{1,0},{2,3},{3,2},{4,5},{5,4},{6,7},{7,6},{8,9},{9,8},{10,11... | collective-permute-start | bytes 307208 | tf_op jit(solution)/shard_map/ppermute | solution.py:910
  15.0 191.3 %all-gather.5.cloned.1.call-start = ((), (), s32[]{:S(2)}) async-start(), calls=%async_computation.3 | async-start | bytes 13926400 | tf_op jit(solution)/shard_map/all_gather | solution.py:979
  17.2 504.7 %reduce-scatter.5.cloned.1.call-start = ((), (), s32[]{:S(2)}) async-start(), calls=%async_computation.5 | async-start | bytes 6963200 | tf_op jit(solution)/shard_map/reduce_scatter | solution.py:1023
  17.4 3.6 collective-permute-start
  21.0 42.4 %collective-permute-start.6 = (bf16[752,1280]{1,0:T(8,128)(2,1)S(1)}, bf16[752,1280]{1,0:T(8,128)(2,1)}, u32[]{:S(2)}, u32[]{:S(2)}) collective-permute-start(bf16[752,1280]{1,0:T(8,128)(2,1)S(1)} %bitcast.93), channel_id=1, source_target_pairs={{0,1},{1,0},{2,3},{3,2},{4,5},{5,4},{6,7},{7,6},{8,9},{9,8},{10,11... | collective-permute-start | bytes 5775368 | tf_op jit(solution)/shard_map/ppermute | solution.py:910
  22.0 1.2 collective-permute-start.2
  23.2 3.7 collective-permute-start.3
  26.9 4.0 collective-permute-start.4
  31.0 5.5 %collective-permute-start.5 = (bf16[16,480]{1,0:T(8,128)(2,1)S(1)}, bf16[16,480]{1,0:T(8,128)(2,1)S(1)}, u32[]{:S(2)}, u32[]{:S(2)}) collective-permute-start(bf16[16,480]{1,0:T(8,128)(2,1)S(1)} %maximum_select_fusion.1), channel_id=1, source_target_pairs={{0,16},{2,18},{4,20},{6,22},{8,24},{10,26},{12,28},{14,30},{16,0},... | collective-permute-start | bytes 46088 | tf_op jit(solution)/shard_map/ppermute | solution.py:923
  63.4 101.4 %collective-permute-start.9 = (bf16[752,1280]{1,0:T(8,128)(2,1)}, bf16[752,1280]{1,0:T(8,128)(2,1)}, u32[]{:S(2)}, u32[]{:S(2)}) collective-permute-start(bf16[752,1280]{1,0:T(8,128)(2,1)} %bitcast.121), channel_id=1, source_target_pairs={{0,1},{1,0},{2,3},{3,2},{4,5},{5,4},{6,7},{7,6},{8,9},{9,8},{10,11... | collective-permute-start | bytes 5775368 | tf_op jit(solution)/shard_map/ppermute | solution.py:910
  128.2 23.5 %collective-permute-start.7 = (bf16[640,752]{0,1:T(8,128)(2,1)S(1)}, bf16[640,752]{0,1:T(8,128)(2,1)S(1)}, u32[]{:S(2)}, u32[]{:S(2)}) collective-permute-start(bf16[640,752]{0,1:T(8,128)(2,1)S(1)} %copy.37), channel_id=1, source_target_pairs={{0,1},{1,0},{2,3},{3,2},{4,5},{5,4},{6,7},{7,6},{8,9},{9,8},{10,11... | collective-permute-start | bytes 2887688 | tf_op jit(solution)/shard_map/ppermute | solution.py:910
  162.6 43.7 %collective-permute-start.8 = (bf16[752,1280]{1,0:T(8,128)(2,1)}, bf16[752,1280]{1,0:T(8,128)(2,1)}, u32[]{:S(2)}, u32[]{:S(2)}) collective-permute-start(bf16[752,1280]{1,0:T(8,128)(2,1)} %get-tuple-element.114.second_ref.so_ref), channel_id=1, source_target_pairs={{0,1},{1,0},{2,3},{3,2},{4,5},{5,4},{6,7},{7,6},{8,9},{9,8},{10,11... | collective-permute-start | bytes 5775368 | tf_op jit(solution)/shard_map/ppermute | solution.py:910
  239.3 45.5 %collective-permute-start.10 = (bf16[752,1280]{1,0:T(8,128)(2,1)}, bf16[752,1280]{1,0:T(8,128)(2,1)S(1)}, u32[]{:S(2)}, u32[]{:S(2)}) collective-permute-start(bf16[752,1280]{1,0:T(8,128)(2,1)} %get-tuple-element.108), channel_id=1, source_target_pairs={{0,1},{1,0},{2,3},{3,2},{4,5},{5,4},{6,7},{7,6},{8,9},{9,8},{10,11... | collective-permute-start | bytes 5775368 | tf_op jit(solution)/shard_map/ppermute | solution.py:910
  284.6 239.3 %reduce-scatter.3.cloned.1.call-start = ((), (), s32[]{:S(2)}) async-start(), calls=%async_computation.4 | async-start | bytes 10444800 | tf_op jit(solution)/shard_map/reduce_scatter | solution.py:1048
  301.4 22.5 %collective-permute-start.11 = (bf16[640,752]{0,1:T(8,128)(2,1)S(1)}, bf16[640,752]{0,1:T(8,128)(2,1)S(1)}, u32[]{:S(2)}, u32[]{:S(2)}) collective-permute-start(bf16[640,752]{0,1:T(8,128)(2,1)S(1)} %copy.39), channel_id=1, source_target_pairs={{0,1},{1,0},{2,3},{3,2},{4,5},{5,4},{6,7},{7,6},{8,9},{9,8},{10,11... | collective-permute-start | bytes 2887688 | tf_op jit(solution)/shard_map/ppermute | solution.py:910
  325.8 42.1 %collective-permute-start.12 = (bf16[752,1280]{1,0:T(8,128)(2,1)S(1)}, bf16[752,1280]{1,0:T(8,128)(2,1)}, u32[]{:S(2)}, u32[]{:S(2)}) collective-permute-start(bf16[752,1280]{1,0:T(8,128)(2,1)S(1)} %copy-done.25), channel_id=1, source_target_pairs={{0,1},{1,0},{2,3},{3,2},{4,5},{5,4},{6,7},{7,6},{8,9},{9,8},{10,11... | collective-permute-start | bytes 5775368 | tf_op jit(solution)/shard_map/ppermute | solution.py:910
  379.2 3.4 collective-permute-start.13
  385.6 32.2 %collective-permute-start.14 = (bf16[4,80,960]{2,1,0:T(8,128)(2,1)S(1)}, bf16[4,80,960]{2,1,0:T(8,128)(2,1)S(1)}, u32[]{:S(2)}, u32[]{:S(2)}) collective-permute-start(bf16[4,80,960]{2,1,0:T(8,128)(2,1)S(1)} %dynamic-slice_bitcast_fusion.2), channel_id=1, source_target_pairs={{0,4},{2,6},{4,0},{6,2},{8,12},{10,14},{12,8},{14,10},{16,20},{18,... | collective-permute-start | bytes 1843208 | tf_op jit(solution)/shard_map/ppermute | solution.py:946
  386.6 31.2 %copy-start.6 = (bf16[8,80,960]{2,1,0:T(8,128)(2,1)S(1)}, bf16[8,80,960]{2,1,0:T(8,128)(2,1)}, u32[]{:S(2)}) copy-start(bf16[8,80,960]{2,1,0:T(8,128)(2,1)} %copy-done.5) | copy-start | bytes 3686404
  452.7 3.6 collective-permute-start.17
  459.4 36.4 %copy-start.4 = (bf16[8,88,960]{2,1,0:T(8,128)(2,1)S(1)}, bf16[8,88,960]{2,1,0:T(8,128)(2,1)}, u32[]{:S(2)}) copy-start(bf16[8,88,960]{2,1,0:T(8,128)(2,1)} %copy-done.3) | copy-start | bytes 4055044
  459.4 36.3 %collective-permute-start.18 = (bf16[4,88,960]{2,1,0:T(8,128)(2,1)S(1)}, bf16[4,88,960]{2,1,0:T(8,128)(2,1)S(1)}, u32[]{:S(2)}, u32[]{:S(2)}) collective-permute-start(bf16[4,88,960]{2,1,0:T(8,128)(2,1)S(1)} %dynamic-slice_bitcast_fusion.1), channel_id=1, source_target_pairs={{0,4},{2,6},{4,0},{6,2},{8,12},{10,14},{12,8},{14,10},{16,20},{18,... | collective-permute-start | bytes 2027528 | tf_op jit(solution)/shard_map/ppermute | solution.py:946
  461.5 33.1 %collective-permute-start.15 = (bf16[1,160,960]{2,1,0:T(8,128)(2,1)}, bf16[1,160,960]{2,1,0:T(8,128)(2,1)}, u32[]{:S(2)}, u32[]{:S(2)}) collective-permute-start(bf16[1,160,960]{2,1,0:T(8,128)(2,1)} %dynamic-slice_bitcast_fusion.4), channel_id=1, source_target_pairs={{0,16},{2,18},{4,20},{6,22},{8,24},{10,26},{12,28},{14,30},{16,0},... | collective-permute-start | bytes 921608 | tf_op jit(solution)/shard_map/ppermute | solution.py:946
  463.9 35.9 %copy-start.7 = (bf16[752,1280]{1,0:T(8,128)(2,1)S(1)}, bf16[752,1280]{1,0:T(8,128)(2,1)}, u32[]{:S(2)}) copy-start(bf16[752,1280]{1,0:T(8,128)(2,1)} %get-tuple-element.144) | copy-start | bytes 5775364
  463.9 35.9 %copy-start.10 = (f32[1280]{0:T(1024)S(1)}, f32[1280]{0:T(1024)}, u32[]{:S(2)}) copy-start(f32[1280]{0:T(1024)} %add.161) | copy-start | bytes 15364
  463.9 51.4 %collective-permute-start.20 = (bf16[752,1280]{1,0:T(8,128)(2,1)}, bf16[752,1280]{1,0:T(8,128)(2,1)}, u32[]{:S(2)}, u32[]{:S(2)}) collective-permute-start(bf16[752,1280]{1,0:T(8,128)(2,1)} %get-tuple-element.149), channel_id=1, source_target_pairs={{0,1},{1,0},{2,3},{3,2},{4,5},{5,4},{6,7},{7,6},{8,9},{9,8},{10,11... | collective-permute-start | bytes 5775368 | tf_op jit(solution)/shard_map/ppermute | solution.py:910
  495.7 9.2 %collective-permute-start.16 = (bf16[1,80,960]{2,1,0:T(8,128)(2,1)S(1)}, bf16[1,80,960]{2,1,0:T(8,128)(2,1)S(1)}, u32[]{:S(2)}, u32[]{:S(2)}) collective-permute-start(bf16[1,80,960]{2,1,0:T(8,128)(2,1)S(1)} %dynamic-slice_bitcast_fusion.6), channel_id=1, source_target_pairs={{0,8},{2,10},{4,12},{6,14},{8,0},{10,2},{12,4},{14,6},{16,24},{18,... | collective-permute-start | bytes 460808 | tf_op jit(solution)/shard_map/ppermute | solution.py:946
  496.1 19.1 %collective-permute-start.19 = (bf16[1,176,960]{2,1,0:T(8,128)(2,1)S(1)}, bf16[1,176,960]{2,1,0:T(8,128)(2,1)S(1)}, u32[]{:S(2)}, u32[]{:S(2)}) collective-permute-start(bf16[1,176,960]{2,1,0:T(8,128)(2,1)S(1)} %dynamic-slice_bitcast_fusion.3), channel_id=1, source_target_pairs={{0,16},{2,18},{4,20},{6,22},{8,24},{10,26},{12,28},{14,30},{16,0},... | collective-permute-start | bytes 1013768 | tf_op jit(solution)/shard_map/ppermute | solution.py:946
  526.7 4.7 collective-permute-start.22
  527.7 5.6 %collective-permute-start.21 = (bf16[1,88,960]{2,1,0:T(8,128)(2,1)S(1)}, bf16[1,88,960]{2,1,0:T(8,128)(2,1)S(1)}, u32[]{:S(2)}, u32[]{:S(2)}) collective-permute-start(bf16[1,88,960]{2,1,0:T(8,128)(2,1)S(1)} %dynamic-slice_bitcast_fusion.5), channel_id=1, source_target_pairs={{0,8},{2,10},{4,12},{6,14},{8,0},{10,2},{12,4},{14,6},{16,24},{18,... | collective-permute-start | bytes 506888 | tf_op jit(solution)/shard_map/ppermute | solution.py:946
  534.2 4.2 collective-permute-start.23
  (25 other events, 170.0 us)
Sparse Core Ops, SparseCore 0:
  15.1 74.9 all-gather.2
  93.0 102.3 all-gather.4
  284.7 84.7 reduce-scatter.4
  374.1 126.0 reduce-scatter.2

commit v4 on v3

--- a/solution.py
+++ b/solution.py
@@ -323,6 +323,10 @@
     return pl.CostEstimate(flops=int(scale * flops), bytes_accessed=int(min(1.0, scale) * moved), transcendentals=0)
 
 
+def lanes(rows):
+    return -(-rows // PAD) * PAD
+
+
 def row_pieces(rows, size):
     return [(start, min(size, rows - start)) for start in range(0, rows, size)]
 
@@ -439,6 +443,8 @@
         out_ref[head, :, start : start + size] = context.astype(jnp.bfloat16)
         log_ref[head, :, start : start + size] = top + jnp.log(total)
 
+    if out_ref.shape[2] > rows:
+        out_ref[:, :, rows:] = jnp.zeros((per_step, HD, out_ref.shape[2] - rows), jnp.bfloat16)
     current = scores(pieces[0])
     for number, piece in enumerate(pieces):
         coming = scores(pieces[number + 1]) if number + 1 < len(pieces) else None
@@ -453,13 +459,13 @@
     return pl.pallas_call(
         attend_kernel,
         out_shape=(
-            jax.ShapeDtypeStruct((heads, HD, rows), jnp.bfloat16),
+            jax.ShapeDtypeStruct((heads, HD, lanes(rows)), jnp.bfloat16),
             jax.ShapeDtypeStruct((heads, 1, rows), jnp.float32),
         ),
         grid=(heads // per_step,),
         in_specs=[spec] * 5,
         out_specs=(
-            pl.BlockSpec((per_step, HD, rows), lambda h: (h, 0, 0)),
+            pl.BlockSpec((per_step, HD, lanes(rows)), lambda h: (h, 0, 0)),
             pl.BlockSpec((per_step, 1, rows), lambda h: (h, 0, 0)),
         ),
         compiler_params=kernel_params(),
@@ -530,7 +536,7 @@
 def attend_back_rows(queries, keys, values, upstream, logs, start, heads):
     rows = queries[0].shape[1]
     spec = pl.BlockSpec((1, rows, PAD), lambda h: (h + start, 0, 0))
-    turned = pl.BlockSpec((1, HD, rows), lambda h: (h + start, 0, 0))
+    turned = pl.BlockSpec((1, HD, lanes(rows)), lambda h: (h + start, 0, 0))
     line = pl.BlockSpec((1, 1, rows), lambda h: (h + start, 0, 0))
     packed = (rows, 3 * heads * HD)
     return pl.pallas_call(
@@ -550,7 +556,7 @@
     co_ref, ct_ref, wo_ref, wt_ref, frames_ref, bias_ref, gain_ref, shift_ref, middle_ref, second_ref,
 ):
     rows = frames_ref.shape[0]
-    own, far = co_ref[...].T, ct_ref[...].T
+    own, far = co_ref[:, :rows].T, ct_ref[:, :rows].T
     pieces = row_pieces(rows, 256)
 
     def branch(piece):
@@ -582,7 +588,7 @@
         ),
         grid=(1,),
         in_specs=[
-            whole((cols, rows)), whole((cols, rows)), whole((width, cols), (0, 3)),
+            whole((cols, lanes(rows))), whole((cols, lanes(rows))), whole((width, cols), (0, 3)),
             whole((width, cols), (0, 4)), whole((rows, width)), whole((1, width)), whole((1, width)), whole((1, width)),
         ],
         out_specs=(whole((rows, width)),) * 2,
@@ -752,6 +758,10 @@
             branch, sums = step_back(pieces[number + 1])
             totals = [a + b for a, b in zip(totals, sums)]
         finish(piece, now)
+    if go_ref.shape[1] > rows:
+        blank = jnp.zeros((go_ref.shape[0], go_ref.shape[1] - rows), jnp.bfloat16)
+        go_ref[:, rows:] = blank
+        gt_ref[:, rows:] = blank
     for index, line in enumerate(totals):
         sums_ref[index : index + 1, :] = line
 
@@ -764,15 +774,15 @@
         out_shape=(
             jax.ShapeDtypeStruct((rows, width), jnp.float32),
             jax.ShapeDtypeStruct((rows, width), jnp.bfloat16),
-            jax.ShapeDtypeStruct((cols, rows), jnp.bfloat16),
-            jax.ShapeDtypeStruct((cols, rows), jnp.bfloat16),
+            jax.ShapeDtypeStruct((cols, lanes(rows)), jnp.bfloat16),
+            jax.ShapeDtypeStruct((cols, lanes(rows)), jnp.bfloat16),
             jax.ShapeDtypeStruct((4, width), jnp.float32),
         ),
         grid=(1,),
         in_specs=[
             full, full, full, full, whole((1, width)), whole((width, cols), (0, 3)), whole((width, cols), (0, 4))
         ],
-        out_specs=(full, full, whole((cols, rows)), whole((cols, rows)), whole((4, width))),
+        out_specs=(full, full, whole((cols, lanes(rows))), whole((cols, lanes(rows))), whole((4, width))),
         compiler_params=kernel_params(),
         cost_estimate=cost(4 * rows * width * cols, 18 * rows * width, COSTS["branch_back"]),
         name="branch_back",
@@ -792,11 +802,11 @@
 
     @pl.when(step == last - 1)
     def _():
-        out_ref[...] = dot_tn(branch_ref[...], co_ref[...].T).astype(jnp.bfloat16)
+        out_ref[...] = dot_tn(branch_ref[...], co_ref[:, : branch_ref.shape[0]].T).astype(jnp.bfloat16)
 
     @pl.when(step == last)
     def _():
-        out_ref[...] = dot_tn(branch_ref[...], ct_ref[...].T).astype(jnp.bfloat16)
+        out_ref[...] = dot_tn(branch_ref[...], ct_ref[:, : branch_ref.shape[0]].T).astype(jnp.bfloat16)
 
 
 def side_grads(second, back, branch, contexts):
@@ -809,7 +819,7 @@
         out_shape=jax.ShapeDtypeStruct((width, units + 2 * cols), jnp.bfloat16),
         grid=(steps + 2,),
         in_specs=[whole((rows, width))] * 2 + [part] * 2
-        + [whole((rows, width))] + [whole((cols, rows))] * 2,
+        + [whole((rows, width))] + [whole((cols, lanes(rows)))] * 2,
         out_specs=pl.BlockSpec((width, cols), lambda j: (0, j)),
         compiler_params=kernel_params(),
         cost_estimate=cost(4 * rows * width * (units + cols), 4 * rows * (width + units), COSTS["weight_grad"]),
@@ -1004,9 +1014,9 @@
     )
     context_send, log_far = attend_rows(q_far, k_own, k_far, v_own, v_far)
     context_send, q_own = tie(context_send, q_own)
-    context_far = swap_tp(context_send.reshape(cols, rows))
+    context_far = swap_tp(context_send.reshape(cols, -1))
     context_own, log_own = attend_rows(q_own, k_own, k_far, v_own, v_far)
-    context_own = context_own.reshape(cols, rows)
+    context_own = context_own.reshape(cols, -1)
     middle, second_own = merge_heads(
         context_own, context_far, pack_one, frames, out_bias, gain_two, shift_two
     )
@@ -1030,7 +1040,7 @@
         (second_own, second_far), (back_own, back_far), branch, (context_own, context_far)
     )
 
-    turned = (heads, HD, rows)
+    turned = (heads, HD, lanes(rows))
     up_far, out_send, d_side = tie(up_far, out_send, d_side)
     out_far = swap_tp(out_send)
     ups = (up_own.reshape(turned), up_far.reshape(turned))
@@ -1087,9 +1097,10 @@
     for place in range(2, len(steps)):
         last = place + 1 == len(steps)
         if place > 2:
+            held_a, held_b = tie(held_a, held_b)
             held_a = halve(held_a, steps[place], steps[place:], fsdp, last)
         if last:
-            held_a, held_b, first_keep, out_frames = tie(held_a, held_b, first_keep, out_frames)
+            held_b, first_keep, out_frames = tie(held_b, first_keep, out_frames)
             frames_grad = frames_back(frames, first_keep, first_recv, mgrad, gain_one)
             held_b, frames_grad, g_side = tie(held_b, frames_grad, g_side)
         held_b = halve(held_b, steps[place], steps[place:], fsdp, last)

time: 555 us -> 554 us (level)
  local copies, waits for them, and re-layouts: 31.4 us -> 25 us
  waiting for transfers between devices: 164 us -> 170 us
    ppermute x8, waiting for transfers between devices: 46.9 us -> 53.5 us  [halve(): lax.ppermute(chosen(1 - mine), 'fsdp', [(i, i ^ bit) for i in range(fsdp)])]
  transfers between devices with their start and end apart: 28 -> 28, of which waited for: 17 -> 16; matrix products, arithmetic and copies ran while one was open for 9% -> 8% of each run, Pallas kernels for 45% -> 45%
where the time goes in v4:
time: 554 us; the launch traced here: 544 us
  Pallas kernels  280 us (51%)
  waiting for transfers between devices  170 us (31%)
  starting transfers between devices  28.7 us (5%)
  other arithmetic  26.6 us (5%)
  local copies, waits for them, and re-layouts  25 us (5%)
  between operations  14.6 us (3%)
    ppermute x12, waiting for transfers between devices, swap_tp(): return lax.ppermute(piece, 'tp', [(0, 1), (1, 0)])  84.1 us
    pallas_call x2, Pallas kernels, feed(): pl.pallas_call(functools.partial(feed_kernel, far is not None), out_shape...  76.6 us
    pallas_call x2, Pallas kernels, attend_back_rows(): pl.pallas_call(attend_back_kernel, out_shape=(jax.ShapeDtypeStruct(packed...  61.9 us
    ppermute x8, waiting for transfers between devices, halve(): lax.ppermute(chosen(1 - mine), 'fsdp', [(i, i ^ bit) for i in range(fsdp)])  53.5 us
    pallas_call x2, Pallas kernels, attend_rows(): pl.pallas_call(attend_kernel, out_shape=(jax.ShapeDtypeStruct((heads, HD,...  30.8 us
    all_gather x1, waiting for transfers between devices, per_device_pair(): lax.all_gather(jnp.concatenate([w_query, w_key, w_value, out_turned, out_...  26.4 us
    pallas_call x1, Pallas kernels, side_grads(): pl.pallas_call(side_grad_kernel, out_shape=jax.ShapeDtypeStruct((width, u...  22.7 us
    pallas_call x2, Pallas kernels, project(): pl.pallas_call(functools.partial(project_kernel, heads), out_shape=(jax.S...  20.6 us
  transfers between devices with their start and end apart: 28, of which 16 were waited for; matrix products, arithmetic and copies ran while one was open for 8% of the time, Pallas kernels for 45%

profile of v4, /device:TPU:0, one launch (start us, length us, event | category | flops | bytes accessed | tf_op | source)
XLA Modules:
  0.0 544.0 jit_solution(3165390580394462165)
XLA Ops:
  7.2 3.0 collective-permute-start.1
  18.4 2.6 collective-permute-done
  31.0 2.5 collective-permute-start.5
  42.3 21.1 %collective-permute-done.6.frames_ref.refs_3_ = bf16[752,1280]{1,0:T(8,128)(2,1)} collective-permute-done((bf16[752,1280]{1,0:T(8,128)(2,1)S(1)}, bf16[752,1280]{1,0:T(8,128)(2,1)}, u32[]{:S(2)}, u32[]{:S(2)}) %collective-permute-start.6) | collective-permute-done | bytes 1925152 | tf_op jit(solution)/shard_map/ppermute | solution.py:920
  63.7 26.4 %all-gather.3.cloned.1.call-done.weight_ref.wo_ref.wt_ref.refs_2_ = bf16[1280,3200]{1,0:T(8,128)(2,1)} async-done(((bf16[80,3200]{1,0:T(8,128)(2,1)}), bf16[1280,3200]{1,0:T(8,128)(2,1)}) %all-gather.3.cloned.1.call-update) | async-done | bytes 8192016 | tf_op jit(solution)/shard_map/all_gather | solution.py:985
  90.1 10.3 %project.2 = (bf16[752,1280]{1,0:T(8,128)(2,1)}, bf16[8,752,128]{2,1,0:T(8,128)(2,1)}, bf16[8,752,128]{2,1,0:T(8,128)(2,1)}, bf16[8,752,128]{2,1,0:T(8,128)(2,1)}) custom-call(s32[2]{0:T(128)} %get-tuple-element.187.scal_ref, bf16[752,1280]{1,0:T(8,128)(2,1)} %bitcast.91, f32[1,1280]{1,0:T(1,128)} %squeeze.80.gain_ref, f32[1,1280]{1,0:T(1,128)} %squeeze.81.shift_ref, ...), custom_call_target="tpu_custom_call" | custom-call | flops 11088691200 | bytes 8765440 | tf_op jit(solution)/shard_map/project/pallas_call | solution.py:408
  100.4 10.3 %project.3 = (bf16[752,1280]{1,0:T(8,128)(2,1)}, bf16[8,752,128]{2,1,0:T(8,128)(2,1)}, bf16[8,752,128]{2,1,0:T(8,128)(2,1)}, bf16[8,752,128]{2,1,0:T(8,128)(2,1)}) custom-call(s32[2]{0:T(128)} %get-tuple-element.188.scal_ref, bf16[752,1280]{1,0:T(8,128)(2,1)} %collective-permute-done.6.frames_ref.refs_3_, f32[1,1280]{1,0:T(1,128)} %squeeze.80.gain_ref, ...), custom_call_target="tpu_custom_call" | custom-call | flops 11088691200 | bytes 8765440 | tf_op jit(solution)/shard_map/project/pallas_call | solution.py:408
  110.7 15.5 %attend.2 = (bf16[8,80,768]{2,1,0:T(8,128)(2,1)}, f32[8,1,752]{2,1,0:T(1,128)}) custom-call(bf16[8,752,128]{2,1,0:T(8,128)(2,1)} %get-tuple-element.93.q_ref.qt_ref, bf16[8,752,128]{2,1,0:T(8,128)(2,1)} %get-tuple-element.94.ko_ref, bf16[8,752,128]{2,1,0:T(8,128)(2,1)} %get-tuple-element.95.kt_ref, bf16[8,752,128]{2,1,0:T(8,128)(2,1)} %get-tuple-element.96.vo_ref, ...), custom_call_target="tpu_custom_call" | custom-call | flops 43430707200 | bytes 9240576 | tf_op jit(solution)/shard_map/attend/pallas_call | solution.py:459
  127.8 15.3 %attend.3 = (bf16[8,80,768]{2,1,0:T(8,128)(2,1)}, f32[8,1,752]{2,1,0:T(1,128)}) custom-call(bf16[8,752,128]{2,1,0:T(8,128)(2,1)} %get-tuple-element.128.q_ref.qo_ref, bf16[8,752,128]{2,1,0:T(8,128)(2,1)} %get-tuple-element.94.ko_ref, bf16[8,752,128]{2,1,0:T(8,128)(2,1)} %get-tuple-element.95.kt_ref, bf16[8,752,128]{2,1,0:T(8,128)(2,1)} %get-tuple-element.96.vo_ref, ...), custom_call_target="tpu_custom_call" | custom-call | flops 43430707200 | bytes 9240576 | tf_op jit(solution)/shard_map/attend/pallas_call | solution.py:459
  143.1 7.3 %collective-permute-done.7.ct_ref = bf16[640,768]{1,0:T(8,128)(2,1)S(1)} collective-permute-done((bf16[640,768]{1,0:T(8,128)(2,1)}, bf16[640,768]{1,0:T(8,128)(2,1)S(1)}, u32[]{:S(2)}, u32[]{:S(2)}) %collective-permute-start.7) | collective-permute-done | bytes 983072 | tf_op jit(solution)/shard_map/ppermute | solution.py:920
  151.3 9.0 %merge_heads.1 = (f32[752,1280]{1,0:T(8,128)}, bf16[752,1280]{1,0:T(8,128)(2,1)}) custom-call(bf16[640,768]{1,0:T(8,128)(2,1)} %bitcast.126, bf16[640,768]{1,0:T(8,128)(2,1)} %copy-done.27, bf16[1280,3200]{1,0:T(8,128)(2,1)} %all-gather.3.cloned.1.call-done.weight_ref.wo_ref.wt_ref.refs_2_, ...), custom_call_target="tpu_custom_call" | custom-call | flops 7392460800 | bytes 12902400 | tf_op jit(solution)/shard_map/merge_heads/pallas_call | solution.py:583
  162.6 41.5 %collective-permute-done.8.second_ref.st_ref = bf16[752,1280]{1,0:T(8,128)(2,1)} collective-permute-done((bf16[752,1280]{1,0:T(8,128)(2,1)}, bf16[752,1280]{1,0:T(8,128)(2,1)}, u32[]{:S(2)}, u32[]{:S(2)}) %collective-permute-start.8) | collective-permute-done | bytes 1925152 | tf_op jit(solution)/shard_map/ppermute | solution.py:920
  204.0 32.9 %feed.1 = (bf16[752,2560]{1,0:T(8,128)(2,1)}, bf16[752,2560]{1,0:T(8,128)(2,1)}, f32[1,2560]{1,0:T(1,128)}, bf16[752,1280]{1,0:T(8,128)(2,1)}, bf16[752,1280]{1,0:T(8,128)(2,1)}) custom-call(bf16[752,1280]{1,0:T(8,128)(2,1)} %collective-permute-done.8.second_ref.st_ref, bf16[752,1280]{1,0:T(8,128)(2,1)} %copy-done.24, ...), custom_call_target="tpu_custom_call" | custom-call | flops 59139686400 | bytes 36208640 | tf_op jit(solution)/shard_map/feed/pallas_call | solution.py:675
  238.5 43.7 %feed_last.1 = (bf16[752,2560]{1,0:T(8,128)(2,1)}, f32[1,2560]{1,0:T(1,128)}, bf16[752,1280]{1,0:T(8,128)(2,1)}, bf16[752,1280]{1,0:T(8,128)(2,1)}, bf16[1280,2560]{1,0:T(8,128)(2,1)}) custom-call(bf16[752,1280]{1,0:T(8,128)(2,1)} %get-tuple-element.115.second_ref.so_ref, bf16[752,1280]{1,0:T(8,128)(2,1)} %bitcast.123, ...), custom_call_target="tpu_custom_call" | custom-call | flops 88709529600 | bytes 36208640 | tf_op jit(solution)/shard_map/feed_last/pallas_call | solution.py:675
  283.8 13.4 %branch_back.1 = (f32[752,1280]{1,0:T(8,128)}, bf16[752,1280]{1,0:T(8,128)(2,1)}, bf16[640,768]{1,0:T(8,128)(2,1)}, bf16[640,768]{1,0:T(8,128)(2,1)}, f32[4,1280]{1,0:T(4,128)}) custom-call(bf16[752,1280]{1,0:T(8,128)(2,1)} %get-tuple-element.108.own_ref, bf16[752,1280]{1,0:T(8,128)(2,1)} %copy-done.26, f32[752,1280]{1,0:T(8,128)} %get-tuple-element.110.middle_ref, ...), custom_call_target="tpu_custom_call" | custom-call | flops 7392460800 | bytes 17326080 | tf_op jit(solution)/shard_map/branch_back/pallas_call | solution.py:772
  297.4 22.7 %side_grads.1 = bf16[1280,3840]{1,0:T(8,128)(2,1)} custom-call(bf16[752,1280]{1,0:T(8,128)(2,1)} %get-tuple-element.115.second_ref.so_ref, bf16[752,1280]{1,0:T(8,128)(2,1)} %collective-permute-done.8.second_ref.st_ref, bf16[752,2560]{1,0:T(8,128)(2,1)} %get-tuple-element.116.bo_ref, bf16[752,2560]{1,0:T(8,128)(2,1)} %get-tuple-element.117.bt_ref, ...), custom_call_target="tpu_custom_call" | custom-call | flops 36962304000 | bytes 11550720 | tf_op jit(solution)/shard_map/side_grads/pallas_call | solution.py:817
  322.0 30.7 %attend_back.2 = (bf16[752,960]{1,0:T(8,128)(2,1)}, bf16[752,960]{1,0:T(8,128)(2,1)}) custom-call(bf16[8,752,128]{2,1,0:T(8,128)(2,1)} %get-tuple-element.128.q_ref.qo_ref, bf16[8,752,128]{2,1,0:T(8,128)(2,1)} %get-tuple-element.93.q_ref.qt_ref, bf16[8,752,128]{2,1,0:T(8,128)(2,1)} %get-tuple-element.94.ko_ref, ...), custom_call_target="tpu_custom_call" | custom-call | flops 130292121600 | bytes 9240576 | tf_op jit(solution)/shard_map/attend_back/pallas_call | solution.py:542
  352.7 9.3 %collective-permute-done.12 = bf16[752,1280]{1,0:T(8,128)(2,1)} collective-permute-done((bf16[752,1280]{1,0:T(8,128)(2,1)S(1)}, bf16[752,1280]{1,0:T(8,128)(2,1)}, u32[]{:S(2)}, u32[]{:S(2)}) %collective-permute-start.12) | collective-permute-done | bytes 1925152 | tf_op jit(solution)/shard_map/ppermute | solution.py:920
  362.0 8.7 %head_grad.2 = bf16[1280,960]{1,0:T(8,128)(2,1)} custom-call(bf16[752,1280]{1,0:T(8,128)(2,1)} %get-tuple-element.89.lo_ref, bf16[752,1280]{1,0:T(8,128)(2,1)} %get-tuple-element.92.lt_ref, bf16[752,960]{1,0:T(8,128)(2,1)} %get-tuple-element.125.refs_0_, bf16[752,960]{1,0:T(8,128)(2,1)} %get-tuple-element.126.refs_1_.refs_0_), custom_call_target="tpu_custom_call" | custom-call | flops 73924608 | bytes 183910 | tf_op jit(solution)/shard_map/head_grad/pallas_call | solution.py:705
  370.7 2.6 dynamic-slice_bitcast_fusion
  373.3 3.4 collective-permute-done.13
  380.8 31.2 %attend_back.3 = (bf16[752,960]{1,0:T(8,128)(2,1)}, bf16[752,960]{1,0:T(8,128)(2,1)}) custom-call(bf16[8,752,128]{2,1,0:T(8,128)(2,1)} %get-tuple-element.128.q_ref.qo_ref, bf16[8,752,128]{2,1,0:T(8,128)(2,1)} %get-tuple-element.93.q_ref.qt_ref, bf16[8,752,128]{2,1,0:T(8,128)(2,1)} %get-tuple-element.94.ko_ref, ...), custom_call_target="tpu_custom_call" | custom-call | flops 325730304 | bytes 184811 | tf_op jit(solution)/shard_map/attend_back/pallas_call | solution.py:542
  412.3 10.2 %first_back.2 = (bf16[752,1280]{1,0:T(8,128)(2,1)}, f32[2,1280]{1,0:T(2,128)}, f32[1,1920]{1,0:T(1,128)}) custom-call(bf16[752,960]{1,0:T(8,128)(2,1)} %get-tuple-element.126.refs_1_.refs_0_, bf16[752,960]{1,0:T(8,128)(2,1)} %get-tuple-element.134.refs_1_, bf16[1280,3200]{1,0:T(8,128)(2,1)} %all-gather.3.cloned.1.call-done.weight_ref.wo_ref.wt_ref.refs_2_, ...), custom_call_target="tpu_custom_call" | custom-call | flops 73924608 | bytes 233062 | tf_op jit(solution)/shard_map/first_back/pallas_call | solution.py:872
  422.5 8.8 %head_grad.3 = bf16[1280,960]{1,0:T(8,128)(2,1)} custom-call(bf16[752,1280]{1,0:T(8,128)(2,1)} %get-tuple-element.89.lo_ref, bf16[752,1280]{1,0:T(8,128)(2,1)} %get-tuple-element.92.lt_ref, bf16[752,960]{1,0:T(8,128)(2,1)} %get-tuple-element.136.refs_0_.refs_1_, bf16[752,960]{1,0:T(8,128)(2,1)} %get-tuple-element.134.refs_1_), custom_call_target="tpu_custom_call" | custom-call | flops 73924608 | bytes 183910 | tf_op jit(solution)/shard_map/head_grad/pallas_call | solution.py:705
  431.4 10.3 %first_back.3 = (bf16[752,1280]{1,0:T(8,128)(2,1)}, f32[2,1280]{1,0:T(2,128)}, f32[1,1920]{1,0:T(1,128)}) custom-call(bf16[752,960]{1,0:T(8,128)(2,1)} %get-tuple-element.125.refs_0_, bf16[752,960]{1,0:T(8,128)(2,1)} %get-tuple-element.136.refs_0_.refs_1_, bf16[1280,3200]{1,0:T(8,128)(2,1)} %all-gather.3.cloned.1.call-done.weight_ref.wo_ref.wt_ref.refs_2_, ...), custom_call_target="tpu_custom_call" | custom-call | flops 73924608 | bytes 233062 | tf_op jit(solution)/shard_map/first_back/pallas_call | solution.py:872
  446.0 3.2 collective-permute-done.16
  456.4 18.9 %collective-permute-done.17 = bf16[4,88,960]{2,1,0:T(8,128)(2,1)S(1)} collective-permute-done((bf16[4,88,960]{2,1,0:T(8,128)(2,1)S(1)}, bf16[4,88,960]{2,1,0:T(8,128)(2,1)S(1)}, u32[]{:S(2)}, u32[]{:S(2)}) %collective-permute-start.17) | collective-permute-done | bytes 675872 | tf_op jit(solution)/shard_map/ppermute | solution.py:956
  478.3 17.3 %collective-permute-done.15 = bf16[1,160,960]{2,1,0:T(8,128)(2,1)} collective-permute-done((bf16[1,160,960]{2,1,0:T(8,128)(2,1)}, bf16[1,160,960]{2,1,0:T(8,128)(2,1)}, u32[]{:S(2)}, u32[]{:S(2)}) %collective-permute-start.15) | collective-permute-done | bytes 307232 | tf_op jit(solution)/shard_map/ppermute | solution.py:956
  496.6 10.9 %collective-permute-done.18 = bf16[1,176,960]{2,1,0:T(8,128)(2,1)} collective-permute-done((bf16[1,176,960]{2,1,0:T(8,128)(2,1)}, bf16[1,176,960]{2,1,0:T(8,128)(2,1)}, u32[]{:S(2)}, u32[]{:S(2)}) %collective-permute-start.18) | collective-permute-done | bytes 337952 | tf_op jit(solution)/shard_map/ppermute | solution.py:956
  508.7 4.6 add_convert_fusion
  513.3 6.5 %frames_back.1 = bf16[752,1280]{1,0:T(8,128)(2,1)} custom-call(bf16[752,1280]{1,0:T(8,128)(2,1)} %bitcast.94, bf16[752,1280]{1,0:T(8,128)(2,1)} %get-tuple-element.150.own_ref, bf16[752,1280]{1,0:T(8,128)(2,1)} %collective-permute-done.19.far_ref, f32[752,1280]{1,0:T(8,128)} %get-tuple-element.152.mgrad_ref, f32[1,1280]{1,0:T(1,128)} %squeeze.80.gain_ref), custom_call_target="tpu_custom_call" | custom-call | flops 385024 | bytes 231014 | tf_op jit(solution)/shard_map/frames_back/pallas_call | solution.py:907
  527.3 2.2 collective-permute-done.22
  (188 shorter events, 73.0 us)
Async XLA Ops:
  7.2 82.9 %all-gather.3.cloned.1.call-start = ((), (), s32[]{:S(2)}) async-start(), calls=%async_computation.2 | async-start | bytes 8704000 | tf_op jit(solution)/shard_map/all_gather | solution.py:985
  7.2 6.9 %collective-permute-start.1 = (bf16[80,640]{1,0:T(8,128)(2,1)}, bf16[80,640]{1,0:T(8,128)(2,1)S(1)}, u32[]{:S(2)}, u32[]{:S(2)}) collective-permute-start(bf16[80,640]{1,0:T(8,128)(2,1)} %bitcast.119), channel_id=1, source_target_pairs={{0,1},{1,0},{2,3},{3,2},{4,5},{5,4},{6,7},{7,6},{8,9},{9,8},{10,11... | collective-permute-start | bytes 307208 | tf_op jit(solution)/shard_map/ppermute | solution.py:920
  15.0 189.0 %all-gather.5.cloned.1.call-start = ((), (), s32[]{:S(2)}) async-start(), calls=%async_computation.3 | async-start | bytes 13926400 | tf_op jit(solution)/shard_map/all_gather | solution.py:989
  17.2 502.8 %reduce-scatter.5.cloned.1.call-start = ((), (), s32[]{:S(2)}) async-start(), calls=%async_computation.5 | async-start | bytes 6963200 | tf_op jit(solution)/shard_map/reduce_scatter | solution.py:1033
  17.4 3.6 collective-permute-start
  21.0 42.4 %collective-permute-start.6 = (bf16[752,1280]{1,0:T(8,128)(2,1)S(1)}, bf16[752,1280]{1,0:T(8,128)(2,1)}, u32[]{:S(2)}, u32[]{:S(2)}) collective-permute-start(bf16[752,1280]{1,0:T(8,128)(2,1)S(1)} %bitcast.95), channel_id=1, source_target_pairs={{0,1},{1,0},{2,3},{3,2},{4,5},{5,4},{6,7},{7,6},{8,9},{9,8},{10,11... | collective-permute-start | bytes 5775368 | tf_op jit(solution)/shard_map/ppermute | solution.py:920
  22.0 1.2 collective-permute-start.2
  23.2 3.7 collective-permute-start.3
  26.9 4.0 collective-permute-start.4
  31.0 5.5 %collective-permute-start.5 = (bf16[16,480]{1,0:T(8,128)(2,1)S(1)}, bf16[16,480]{1,0:T(8,128)(2,1)S(1)}, u32[]{:S(2)}, u32[]{:S(2)}) collective-permute-start(bf16[16,480]{1,0:T(8,128)(2,1)S(1)} %maximum_select_fusion.1), channel_id=1, source_target_pairs={{0,16},{2,18},{4,20},{6,22},{8,24},{10,26},{12,28},{14,30},{16,0},... | collective-permute-start | bytes 46088 | tf_op jit(solution)/shard_map/ppermute | solution.py:933
  63.4 99.1 %collective-permute-start.9 = (bf16[752,1280]{1,0:T(8,128)(2,1)}, bf16[752,1280]{1,0:T(8,128)(2,1)S(1)}, u32[]{:S(2)}, u32[]{:S(2)}) collective-permute-start(bf16[752,1280]{1,0:T(8,128)(2,1)} %bitcast.122), channel_id=1, source_target_pairs={{0,1},{1,0},{2,3},{3,2},{4,5},{5,4},{6,7},{7,6},{8,9},{9,8},{10,11... | collective-permute-start | bytes 5775368 | tf_op jit(solution)/shard_map/ppermute | solution.py:920
  126.3 24.1 %collective-permute-start.7 = (bf16[640,768]{1,0:T(8,128)(2,1)}, bf16[640,768]{1,0:T(8,128)(2,1)S(1)}, u32[]{:S(2)}, u32[]{:S(2)}) collective-permute-start(bf16[640,768]{1,0:T(8,128)(2,1)} %bitcast.125), channel_id=1, source_target_pairs={{0,1},{1,0},{2,3},{3,2},{4,5},{5,4},{6,7},{7,6},{8,9},{9,8},{10,11... | collective-permute-start | bytes 2949128 | tf_op jit(solution)/shard_map/ppermute | solution.py:920
  160.3 43.7 %collective-permute-start.8 = (bf16[752,1280]{1,0:T(8,128)(2,1)}, bf16[752,1280]{1,0:T(8,128)(2,1)}, u32[]{:S(2)}, u32[]{:S(2)}) collective-permute-start(bf16[752,1280]{1,0:T(8,128)(2,1)} %get-tuple-element.115.second_ref.so_ref), channel_id=1, source_target_pairs={{0,1},{1,0},{2,3},{3,2},{4,5},{5,4},{6,7},{7,6},{8,9},{9,8},{10,11... | collective-permute-start | bytes 5775368 | tf_op jit(solution)/shard_map/ppermute | solution.py:920
  162.6 41.5 %copy-start.24 = (bf16[752,1280]{1,0:T(8,128)(2,1)}, bf16[752,1280]{1,0:T(8,128)(2,1)S(1)}, u32[]{:S(2)}) copy-start(bf16[752,1280]{1,0:T(8,128)(2,1)S(1)} %collective-permute-done.9.grad_ref.refs_0_) | copy-start | bytes 5775364
  237.0 45.5 %collective-permute-start.10 = (bf16[752,1280]{1,0:T(8,128)(2,1)}, bf16[752,1280]{1,0:T(8,128)(2,1)S(1)}, u32[]{:S(2)}, u32[]{:S(2)}) collective-permute-start(bf16[752,1280]{1,0:T(8,128)(2,1)} %get-tuple-element.109), channel_id=1, source_target_pairs={{0,1},{1,0},{2,3},{3,2},{4,5},{5,4},{6,7},{7,6},{8,9},{9,8},{10,11... | collective-permute-start | bytes 5775368 | tf_op jit(solution)/shard_map/ppermute | solution.py:920
  282.3 239.7 %reduce-scatter.3.cloned.1.call-start = ((), (), s32[]{:S(2)}) async-start(), calls=%async_computation.4 | async-start | bytes 10444800 | tf_op jit(solution)/shard_map/reduce_scatter | solution.py:1058
  297.2 23.0 %collective-permute-start.11 = (bf16[640,768]{1,0:T(8,128)(2,1)}, bf16[640,768]{1,0:T(8,128)(2,1)S(1)}, u32[]{:S(2)}, u32[]{:S(2)}) collective-permute-start(bf16[640,768]{1,0:T(8,128)(2,1)} %get-tuple-element.113), channel_id=1, source_target_pairs={{0,1},{1,0},{2,3},{3,2},{4,5},{5,4},{6,7},{7,6},{8,9},{9,8},{10,11... | collective-permute-start | bytes 2949128 | tf_op jit(solution)/shard_map/ppermute | solution.py:920
  320.1 41.9 %collective-permute-start.12 = (bf16[752,1280]{1,0:T(8,128)(2,1)S(1)}, bf16[752,1280]{1,0:T(8,128)(2,1)}, u32[]{:S(2)}, u32[]{:S(2)}) collective-permute-start(bf16[752,1280]{1,0:T(8,128)(2,1)S(1)} %copy-done.25), channel_id=1, source_target_pairs={{0,1},{1,0},{2,3},{3,2},{4,5},{5,4},{6,7},{7,6},{8,9},{9,8},{10,11... | collective-permute-start | bytes 5775368 | tf_op jit(solution)/shard_map/ppermute | solution.py:920
  373.3 3.4 collective-permute-start.13
  379.7 32.4 %collective-permute-start.14 = (bf16[4,80,960]{2,1,0:T(8,128)(2,1)S(1)}, bf16[4,80,960]{2,1,0:T(8,128)(2,1)S(1)}, u32[]{:S(2)}, u32[]{:S(2)}) collective-permute-start(bf16[4,80,960]{2,1,0:T(8,128)(2,1)S(1)} %dynamic-slice_bitcast_fusion.2), channel_id=1, source_target_pairs={{0,4},{2,6},{4,0},{6,2},{8,12},{10,14},{12,8},{14,10},{16,20},{18,... | collective-permute-start | bytes 1843208 | tf_op jit(solution)/shard_map/ppermute | solution.py:956
  380.8 31.2 %copy-start.5 = (bf16[8,80,960]{2,1,0:T(8,128)(2,1)S(1)}, bf16[8,80,960]{2,1,0:T(8,128)(2,1)}, u32[]{:S(2)}) copy-start(bf16[8,80,960]{2,1,0:T(8,128)(2,1)} %copy-done.4) | copy-start | bytes 3686404
  445.9 3.3 collective-permute-start.16
  451.0 27.2 %copy-start.9 = (f32[32,40]{1,0:T(8,128)S(1)}, f32[32,40]{1,0:T(8,128)}, u32[]{:S(2)}) copy-start(f32[32,40]{1,0:T(8,128)} %get-tuple-element.159) | copy-start | bytes 15364
  451.0 24.2 %collective-permute-start.17 = (bf16[4,88,960]{2,1,0:T(8,128)(2,1)S(1)}, bf16[4,88,960]{2,1,0:T(8,128)(2,1)S(1)}, u32[]{:S(2)}, u32[]{:S(2)}) collective-permute-start(bf16[4,88,960]{2,1,0:T(8,128)(2,1)S(1)} %dynamic-slice_bitcast_fusion.1), channel_id=1, source_target_pairs={{0,4},{2,6},{4,0},{6,2},{8,12},{10,14},{12,8},{14,10},{16,20},{18,... | collective-permute-start | bytes 2027528 | tf_op jit(solution)/shard_map/ppermute | solution.py:956
  452.2 61.2 %collective-permute-start.19 = (bf16[752,1280]{1,0:T(8,128)(2,1)}, bf16[752,1280]{1,0:T(8,128)(2,1)}, u32[]{:S(2)}, u32[]{:S(2)}) collective-permute-start(bf16[752,1280]{1,0:T(8,128)(2,1)} %get-tuple-element.151), channel_id=1, source_target_pairs={{0,1},{1,0},{2,3},{3,2},{4,5},{5,4},{6,7},{7,6},{8,9},{9,8},{10,11... | collective-permute-start | bytes 5775368 | tf_op jit(solution)/shard_map/ppermute | solution.py:920
  454.6 41.0 %collective-permute-start.15 = (bf16[1,160,960]{2,1,0:T(8,128)(2,1)}, bf16[1,160,960]{2,1,0:T(8,128)(2,1)}, u32[]{:S(2)}, u32[]{:S(2)}) collective-permute-start(bf16[1,160,960]{2,1,0:T(8,128)(2,1)} %dynamic-slice_bitcast_fusion.4), channel_id=1, source_target_pairs={{0,16},{2,18},{4,20},{6,22},{8,24},{10,26},{12,28},{14,30},{16,0},... | collective-permute-start | bytes 921608 | tf_op jit(solution)/shard_map/ppermute | solution.py:956
  476.6 32.1 %copy-start.6 = (bf16[752,1280]{1,0:T(8,128)(2,1)S(1)}, bf16[752,1280]{1,0:T(8,128)(2,1)}, u32[]{:S(2)}) copy-start(bf16[752,1280]{1,0:T(8,128)(2,1)} %get-tuple-element.146) | copy-start | bytes 5775364
  477.4 30.1 %collective-permute-start.18 = (bf16[1,176,960]{2,1,0:T(8,128)(2,1)}, bf16[1,176,960]{2,1,0:T(8,128)(2,1)}, u32[]{:S(2)}, u32[]{:S(2)}) collective-permute-start(bf16[1,176,960]{2,1,0:T(8,128)(2,1)} %dynamic-slice_bitcast_fusion.3), channel_id=1, source_target_pairs={{0,16},{2,18},{4,20},{6,22},{8,24},{10,26},{12,28},{14,30},{16,0},... | collective-permute-start | bytes 1013768 | tf_op jit(solution)/shard_map/ppermute | solution.py:956
  508.6 11.2 %collective-permute-start.20 = (bf16[1,80,960]{2,1,0:T(8,128)(2,1)S(1)}, bf16[1,80,960]{2,1,0:T(8,128)(2,1)S(1)}, u32[]{:S(2)}, u32[]{:S(2)}) collective-permute-start(bf16[1,80,960]{2,1,0:T(8,128)(2,1)S(1)} %dynamic-slice_bitcast_fusion.6), channel_id=1, source_target_pairs={{0,8},{2,10},{4,12},{6,14},{8,0},{10,2},{12,4},{14,6},{16,24},{18,... | collective-permute-start | bytes 460808 | tf_op jit(solution)/shard_map/ppermute | solution.py:956
  524.8 4.7 collective-permute-start.22
  525.2 5.9 %collective-permute-start.21 = (bf16[1,88,960]{2,1,0:T(8,128)(2,1)S(1)}, bf16[1,88,960]{2,1,0:T(8,128)(2,1)S(1)}, u32[]{:S(2)}, u32[]{:S(2)}) collective-permute-start(bf16[1,88,960]{2,1,0:T(8,128)(2,1)S(1)} %dynamic-slice_bitcast_fusion.5), channel_id=1, source_target_pairs={{0,8},{2,10},{4,12},{6,14},{8,0},{10,2},{12,4},{14,6},{16,24},{18,... | collective-permute-start | bytes 506888 | tf_op jit(solution)/shard_map/ppermute | solution.py:956
  532.0 4.7 collective-permute-start.23
  (26 other events, 189.4 us)
Sparse Core Ops, SparseCore 0:
  15.1 74.9 all-gather.2
  93.0 102.2 all-gather.4
  282.4 84.8 reduce-scatter.4
  371.8 132.3 reduce-scatter.2

commit v5 on v4

--- a/solution.py
+++ b/solution.py
@@ -1054,12 +1054,13 @@
 
     many = (heads + 1) // 2
     own_a, far_a = back(q_own, 0, many)
-    own_a, out_far, d_side = tie(own_a, out_far, d_side)
+    own_a, d_side = tie(own_a, d_side)
     g_side = lax.psum_scatter(d_side, "fsdp", scatter_dimension=0, tiled=True)
     d_heads = head_grad(firsts, [own_a], [far_a])
     held_a = halve(d_heads, steps[0], steps, fsdp)
     held_a, q_own = tie(held_a, q_own)
     own_b, far_b = back(q_own, many, heads - many)
+    far_b, out_far = tie(far_b, out_far)
     held_a = halve(held_a, steps[1], steps[1:], fsdp)
     held_a, far_b = tie(held_a, far_b)
     first_send, sums_far, bias_far = first_back([far_a, far_b], pack_one, frames_far)

time: 554 us -> 551 us (level)
  no operation moved by 1% of the time
where the time goes in v5:
time: 551 us; the launch traced here: 541 us
  Pallas kernels  279 us (51%)
  waiting for transfers between devices  167 us (30%)
  starting transfers between devices  27.9 us (5%)
  other arithmetic  26.6 us (5%)
  local copies, waits for them, and re-layouts  25.9 us (5%)
  between operations  14.6 us (3%)
    ppermute x12, waiting for transfers between devices, swap_tp(): return lax.ppermute(piece, 'tp', [(0, 1), (1, 0)])  80.2 us
    pallas_call x2, Pallas kernels, feed(): pl.pallas_call(functools.partial(feed_kernel, far is not None), out_shape...  76.7 us
    pallas_call x2, Pallas kernels, attend_back_rows(): pl.pallas_call(attend_back_kernel, out_shape=(jax.ShapeDtypeStruct(packed...  61.5 us
    ppermute x8, waiting for transfers between devices, halve(): lax.ppermute(chosen(1 - mine), 'fsdp', [(i, i ^ bit) for i in range(fsdp)])  54.9 us
    pallas_call x2, Pallas kernels, attend_rows(): pl.pallas_call(attend_kernel, out_shape=(jax.ShapeDtypeStruct((heads, HD,...  30.8 us
    all_gather x1, waiting for transfers between devices, per_device_pair(): lax.all_gather(jnp.concatenate([w_query, w_key, w_value, out_turned, out_...  26.4 us
    pallas_call x1, Pallas kernels, side_grads(): pl.pallas_call(side_grad_kernel, out_shape=jax.ShapeDtypeStruct((width, u...  22.6 us
    pallas_call x2, Pallas kernels, project(): pl.pallas_call(functools.partial(project_kernel, heads), out_shape=(jax.S...  20.6 us
  transfers between devices with their start and end apart: 28, of which 16 were waited for; matrix products, arithmetic and copies ran while one was open for 8% of the time, Pallas kernels for 45%

profile of v5, /device:TPU:0, one launch (start us, length us, event | category | flops | bytes accessed | tf_op | source)
XLA Modules:
  0.0 541.1 jit_solution(14487331962620576402)
XLA Ops:
  7.2 3.0 collective-permute-start.1
  15.1 2.1 pad_maximum_fusion
  18.4 2.6 collective-permute-done
  31.0 2.5 collective-permute-start.5
  42.3 21.1 %collective-permute-done.6.frames_ref.refs_3_ = bf16[752,1280]{1,0:T(8,128)(2,1)} collective-permute-done((bf16[752,1280]{1,0:T(8,128)(2,1)S(1)}, bf16[752,1280]{1,0:T(8,128)(2,1)}, u32[]{:S(2)}, u32[]{:S(2)}) %collective-permute-start.6) | collective-permute-done | bytes 1925152 | tf_op jit(solution)/shard_map/ppermute | solution.py:920
  63.7 26.4 %all-gather.3.cloned.1.call-done.weight_ref.wo_ref.wt_ref.refs_2_ = bf16[1280,3200]{1,0:T(8,128)(2,1)} async-done(((bf16[80,3200]{1,0:T(8,128)(2,1)}), bf16[1280,3200]{1,0:T(8,128)(2,1)}) %all-gather.3.cloned.1.call-update) | async-done | bytes 8192016 | tf_op jit(solution)/shard_map/all_gather | solution.py:985
  90.1 10.3 %project.2 = (bf16[752,1280]{1,0:T(8,128)(2,1)}, bf16[8,752,128]{2,1,0:T(8,128)(2,1)}, bf16[8,752,128]{2,1,0:T(8,128)(2,1)}, bf16[8,752,128]{2,1,0:T(8,128)(2,1)}) custom-call(s32[2]{0:T(128)} %get-tuple-element.189.scal_ref, bf16[752,1280]{1,0:T(8,128)(2,1)} %bitcast.91, f32[1,1280]{1,0:T(1,128)} %squeeze.80.gain_ref, f32[1,1280]{1,0:T(1,128)} %squeeze.81.shift_ref, ...), custom_call_target="tpu_custom_call" | custom-call | flops 11088691200 | bytes 8765440 | tf_op jit(solution)/shard_map/project/pallas_call | solution.py:408
  100.4 10.3 %project.3 = (bf16[752,1280]{1,0:T(8,128)(2,1)}, bf16[8,752,128]{2,1,0:T(8,128)(2,1)}, bf16[8,752,128]{2,1,0:T(8,128)(2,1)}, bf16[8,752,128]{2,1,0:T(8,128)(2,1)}) custom-call(s32[2]{0:T(128)} %get-tuple-element.190.scal_ref, bf16[752,1280]{1,0:T(8,128)(2,1)} %collective-permute-done.6.frames_ref.refs_3_, f32[1,1280]{1,0:T(1,128)} %squeeze.80.gain_ref, ...), custom_call_target="tpu_custom_call" | custom-call | flops 11088691200 | bytes 8765440 | tf_op jit(solution)/shard_map/project/pallas_call | solution.py:408
  110.7 15.5 %attend.2 = (bf16[8,80,768]{2,1,0:T(8,128)(2,1)}, f32[8,1,752]{2,1,0:T(1,128)}) custom-call(bf16[8,752,128]{2,1,0:T(8,128)(2,1)} %get-tuple-element.94.q_ref.qt_ref, bf16[8,752,128]{2,1,0:T(8,128)(2,1)} %get-tuple-element.95.ko_ref, bf16[8,752,128]{2,1,0:T(8,128)(2,1)} %get-tuple-element.96.kt_ref, bf16[8,752,128]{2,1,0:T(8,128)(2,1)} %get-tuple-element.97.vo_ref, ...), custom_call_target="tpu_custom_call" | custom-call | flops 43430707200 | bytes 9240576 | tf_op jit(solution)/shard_map/attend/pallas_call | solution.py:459
  127.7 15.3 %attend.3 = (bf16[8,80,768]{2,1,0:T(8,128)(2,1)}, f32[8,1,752]{2,1,0:T(1,128)}) custom-call(bf16[8,752,128]{2,1,0:T(8,128)(2,1)} %get-tuple-element.128.q_ref.qo_ref, bf16[8,752,128]{2,1,0:T(8,128)(2,1)} %get-tuple-element.95.ko_ref, bf16[8,752,128]{2,1,0:T(8,128)(2,1)} %get-tuple-element.96.kt_ref, bf16[8,752,128]{2,1,0:T(8,128)(2,1)} %get-tuple-element.97.vo_ref, ...), custom_call_target="tpu_custom_call" | custom-call | flops 43430707200 | bytes 9240576 | tf_op jit(solution)/shard_map/attend/pallas_call | solution.py:459
  143.0 7.4 %collective-permute-done.7.ct_ref = bf16[640,768]{1,0:T(8,128)(2,1)S(1)} collective-permute-done((bf16[640,768]{1,0:T(8,128)(2,1)}, bf16[640,768]{1,0:T(8,128)(2,1)S(1)}, u32[]{:S(2)}, u32[]{:S(2)}) %collective-permute-start.7) | collective-permute-done | bytes 983072 | tf_op jit(solution)/shard_map/ppermute | solution.py:920
  151.3 9.1 %merge_heads.1 = (f32[752,1280]{1,0:T(8,128)}, bf16[752,1280]{1,0:T(8,128)(2,1)}) custom-call(bf16[640,768]{1,0:T(8,128)(2,1)} %bitcast.126, bf16[640,768]{1,0:T(8,128)(2,1)} %copy-done.26, bf16[1280,3200]{1,0:T(8,128)(2,1)} %all-gather.3.cloned.1.call-done.weight_ref.wo_ref.wt_ref.refs_2_, ...), custom_call_target="tpu_custom_call" | custom-call | flops 7392460800 | bytes 12902400 | tf_op jit(solution)/shard_map/merge_heads/pallas_call | solution.py:583
  162.6 41.5 %collective-permute-done.8.second_ref.st_ref = bf16[752,1280]{1,0:T(8,128)(2,1)} collective-permute-done((bf16[752,1280]{1,0:T(8,128)(2,1)}, bf16[752,1280]{1,0:T(8,128)(2,1)}, u32[]{:S(2)}, u32[]{:S(2)}) %collective-permute-start.8) | collective-permute-done | bytes 1925152 | tf_op jit(solution)/shard_map/ppermute | solution.py:920
  204.1 32.9 %feed.1 = (bf16[752,2560]{1,0:T(8,128)(2,1)}, bf16[752,2560]{1,0:T(8,128)(2,1)}, f32[1,2560]{1,0:T(1,128)}, bf16[752,1280]{1,0:T(8,128)(2,1)}, bf16[752,1280]{1,0:T(8,128)(2,1)}) custom-call(bf16[752,1280]{1,0:T(8,128)(2,1)} %collective-permute-done.8.second_ref.st_ref, bf16[752,1280]{1,0:T(8,128)(2,1)} %copy-done.24, ...), custom_call_target="tpu_custom_call" | custom-call | flops 59139686400 | bytes 36208640 | tf_op jit(solution)/shard_map/feed/pallas_call | solution.py:675
  238.6 43.7 %feed_last.1 = (bf16[752,2560]{1,0:T(8,128)(2,1)}, f32[1,2560]{1,0:T(1,128)}, bf16[752,1280]{1,0:T(8,128)(2,1)}, bf16[752,1280]{1,0:T(8,128)(2,1)}, bf16[1280,2560]{1,0:T(8,128)(2,1)}) custom-call(bf16[752,1280]{1,0:T(8,128)(2,1)} %get-tuple-element.116.second_ref.so_ref, bf16[752,1280]{1,0:T(8,128)(2,1)} %bitcast.123, ...), custom_call_target="tpu_custom_call" | custom-call | flops 88709529600 | bytes 36208640 | tf_op jit(solution)/shard_map/feed_last/pallas_call | solution.py:675
  283.9 13.4 %branch_back.1 = (f32[752,1280]{1,0:T(8,128)}, bf16[752,1280]{1,0:T(8,128)(2,1)}, bf16[640,768]{1,0:T(8,128)(2,1)}, bf16[640,768]{1,0:T(8,128)(2,1)}, f32[4,1280]{1,0:T(4,128)}) custom-call(bf16[752,1280]{1,0:T(8,128)(2,1)} %get-tuple-element.109.own_ref, bf16[752,1280]{1,0:T(8,128)(2,1)} %copy-done.25, f32[752,1280]{1,0:T(8,128)} %get-tuple-element.111.middle_ref, ...), custom_call_target="tpu_custom_call" | custom-call | flops 7392460800 | bytes 17326080 | tf_op jit(solution)/shard_map/branch_back/pallas_call | solution.py:772
  297.5 22.6 %side_grads.1 = bf16[1280,3840]{1,0:T(8,128)(2,1)} custom-call(bf16[752,1280]{1,0:T(8,128)(2,1)} %get-tuple-element.116.second_ref.so_ref, bf16[752,1280]{1,0:T(8,128)(2,1)} %collective-permute-done.8.second_ref.st_ref, bf16[752,2560]{1,0:T(8,128)(2,1)} %get-tuple-element.117.bo_ref, bf16[752,2560]{1,0:T(8,128)(2,1)} %get-tuple-element.118.bt_ref, ...), custom_call_target="tpu_custom_call" | custom-call | flops 36962304000 | bytes 11550720 | tf_op jit(solution)/shard_map/side_grads/pallas_call | solution.py:817
  321.0 30.7 %attend_back.2 = (bf16[752,960]{1,0:T(8,128)(2,1)}, bf16[752,960]{1,0:T(8,128)(2,1)}) custom-call(bf16[8,752,128]{2,1,0:T(8,128)(2,1)} %get-tuple-element.128.q_ref.qo_ref, bf16[8,752,128]{2,1,0:T(8,128)(2,1)} %get-tuple-element.94.q_ref.qt_ref, bf16[8,752,128]{2,1,0:T(8,128)(2,1)} %get-tuple-element.95.ko_ref, ...), custom_call_target="tpu_custom_call" | custom-call | flops 130292121600 | bytes 9240576 | tf_op jit(solution)/shard_map/attend_back/pallas_call | solution.py:542
  351.7 8.7 %head_grad.2 = bf16[1280,960]{1,0:T(8,128)(2,1)} custom-call(bf16[752,1280]{1,0:T(8,128)(2,1)} %get-tuple-element.90.lo_ref, bf16[752,1280]{1,0:T(8,128)(2,1)} %get-tuple-element.93.lt_ref, bf16[752,960]{1,0:T(8,128)(2,1)} %get-tuple-element.125.refs_0_, bf16[752,960]{1,0:T(8,128)(2,1)} %get-tuple-element.126.refs_1_.refs_0_), custom_call_target="tpu_custom_call" | custom-call | flops 73924608 | bytes 183910 | tf_op jit(solution)/shard_map/head_grad/pallas_call | solution.py:705
  360.4 2.7 dynamic-slice_bitcast_fusion
  370.4 30.8 %attend_back.3 = (bf16[752,960]{1,0:T(8,128)(2,1)}, bf16[752,960]{1,0:T(8,128)(2,1)}) custom-call(bf16[8,752,128]{2,1,0:T(8,128)(2,1)} %get-tuple-element.128.q_ref.qo_ref, bf16[8,752,128]{2,1,0:T(8,128)(2,1)} %get-tuple-element.94.q_ref.qt_ref, bf16[8,752,128]{2,1,0:T(8,128)(2,1)} %get-tuple-element.95.ko_ref, ...), custom_call_target="tpu_custom_call" | custom-call | flops 325730304 | bytes 184811 | tf_op jit(solution)/shard_map/attend_back/pallas_call | solution.py:542
  401.4 6.3 %collective-permute-done.14 = bf16[752,1280]{1,0:T(8,128)(2,1)} collective-permute-done((bf16[752,1280]{1,0:T(8,128)(2,1)}, bf16[752,1280]{1,0:T(8,128)(2,1)}, u32[]{:S(2)}, u32[]{:S(2)}) %collective-permute-start.14) | collective-permute-done | bytes 1925152 | tf_op jit(solution)/shard_map/ppermute | solution.py:920
  407.8 10.1 %first_back.2 = (bf16[752,1280]{1,0:T(8,128)(2,1)}, f32[2,1280]{1,0:T(2,128)}, f32[1,1920]{1,0:T(1,128)}) custom-call(bf16[752,960]{1,0:T(8,128)(2,1)} %get-tuple-element.126.refs_1_.refs_0_, bf16[752,960]{1,0:T(8,128)(2,1)} %get-tuple-element.136.refs_1_, bf16[1280,3200]{1,0:T(8,128)(2,1)} %all-gather.3.cloned.1.call-done.weight_ref.wo_ref.wt_ref.refs_2_, ...), custom_call_target="tpu_custom_call" | custom-call | flops 73924608 | bytes 233062 | tf_op jit(solution)/shard_map/first_back/pallas_call | solution.py:872
  417.9 8.8 %head_grad.3 = bf16[1280,960]{1,0:T(8,128)(2,1)} custom-call(bf16[752,1280]{1,0:T(8,128)(2,1)} %get-tuple-element.90.lo_ref, bf16[752,1280]{1,0:T(8,128)(2,1)} %get-tuple-element.93.lt_ref, bf16[752,960]{1,0:T(8,128)(2,1)} %get-tuple-element.138.refs_0_.refs_1_, bf16[752,960]{1,0:T(8,128)(2,1)} %get-tuple-element.136.refs_1_), custom_call_target="tpu_custom_call" | custom-call | flops 73924608 | bytes 183910 | tf_op jit(solution)/shard_map/head_grad/pallas_call | solution.py:705
  426.8 10.4 %first_back.3 = (bf16[752,1280]{1,0:T(8,128)(2,1)}, f32[2,1280]{1,0:T(2,128)}, f32[1,1920]{1,0:T(1,128)}) custom-call(bf16[752,960]{1,0:T(8,128)(2,1)} %get-tuple-element.125.refs_0_, bf16[752,960]{1,0:T(8,128)(2,1)} %get-tuple-element.138.refs_0_.refs_1_, bf16[1280,3200]{1,0:T(8,128)(2,1)} %all-gather.3.cloned.1.call-done.weight_ref.wo_ref.wt_ref.refs_2_, ...), custom_call_target="tpu_custom_call" | custom-call | flops 73924608 | bytes 233062 | tf_op jit(solution)/shard_map/first_back/pallas_call | solution.py:872
  441.5 3.2 collective-permute-done.16
  451.2 17.6 %collective-permute-done.17 = bf16[4,88,960]{2,1,0:T(8,128)(2,1)S(1)} collective-permute-done((bf16[4,88,960]{2,1,0:T(8,128)(2,1)S(1)}, bf16[4,88,960]{2,1,0:T(8,128)(2,1)S(1)}, u32[]{:S(2)}, u32[]{:S(2)}) %collective-permute-start.17) | collective-permute-done | bytes 675872 | tf_op jit(solution)/shard_map/ppermute | solution.py:956
  473.1 31.2 %collective-permute-done.18 = bf16[1,176,960]{2,1,0:T(8,128)(2,1)} collective-permute-done((bf16[1,176,960]{2,1,0:T(8,128)(2,1)}, bf16[1,176,960]{2,1,0:T(8,128)(2,1)}, u32[]{:S(2)}, u32[]{:S(2)}) %collective-permute-start.18) | collective-permute-done | bytes 337952 | tf_op jit(solution)/shard_map/ppermute | solution.py:956
  505.5 4.6 add_convert_fusion
  510.1 6.5 %frames_back.1 = bf16[752,1280]{1,0:T(8,128)(2,1)} custom-call(bf16[752,1280]{1,0:T(8,128)(2,1)} %bitcast.94, bf16[752,1280]{1,0:T(8,128)(2,1)} %get-tuple-element.152.own_ref, bf16[752,1280]{1,0:T(8,128)(2,1)} %collective-permute-done.19.far_ref, f32[752,1280]{1,0:T(8,128)} %get-tuple-element.154.mgrad_ref, f32[1,1280]{1,0:T(1,128)} %squeeze.80.gain_ref), custom_call_target="tpu_custom_call" | custom-call | flops 385024 | bytes 231014 | tf_op jit(solution)/shard_map/frames_back/pallas_call | solution.py:907
  519.6 2.0 slice_convert_fusion
  523.1 2.1 collective-permute-start.21
  (186 shorter events, 71.2 us)
Async XLA Ops:
  7.2 82.9 %all-gather.3.cloned.1.call-start = ((), (), s32[]{:S(2)}) async-start(), calls=%async_computation.2 | async-start | bytes 8704000 | tf_op jit(solution)/shard_map/all_gather | solution.py:985
  7.2 6.9 %collective-permute-start.1 = (bf16[80,640]{1,0:T(8,128)(2,1)}, bf16[80,640]{1,0:T(8,128)(2,1)S(1)}, u32[]{:S(2)}, u32[]{:S(2)}) collective-permute-start(bf16[80,640]{1,0:T(8,128)(2,1)} %bitcast.119), channel_id=1, source_target_pairs={{0,1},{1,0},{2,3},{3,2},{4,5},{5,4},{6,7},{7,6},{8,9},{9,8},{10,11... | collective-permute-start | bytes 307208 | tf_op jit(solution)/shard_map/ppermute | solution.py:920
  15.0 189.1 %all-gather.5.cloned.1.call-start = ((), (), s32[]{:S(2)}) async-start(), calls=%async_computation.3 | async-start | bytes 13926400 | tf_op jit(solution)/shard_map/all_gather | solution.py:989
  17.2 499.6 %reduce-scatter.5.cloned.1.call-start = ((), (), s32[]{:S(2)}) async-start(), calls=%async_computation.5 | async-start | bytes 6963200 | tf_op jit(solution)/shard_map/reduce_scatter | solution.py:1033
  17.4 3.6 collective-permute-start
  21.0 42.4 %collective-permute-start.6 = (bf16[752,1280]{1,0:T(8,128)(2,1)S(1)}, bf16[752,1280]{1,0:T(8,128)(2,1)}, u32[]{:S(2)}, u32[]{:S(2)}) collective-permute-start(bf16[752,1280]{1,0:T(8,128)(2,1)S(1)} %bitcast.95), channel_id=1, source_target_pairs={{0,1},{1,0},{2,3},{3,2},{4,5},{5,4},{6,7},{7,6},{8,9},{9,8},{10,11... | collective-permute-start | bytes 5775368 | tf_op jit(solution)/shard_map/ppermute | solution.py:920
  22.0 1.2 collective-permute-start.2
  23.2 3.7 collective-permute-start.3
  26.9 4.0 collective-permute-start.4
  31.0 5.5 %collective-permute-start.5 = (bf16[16,480]{1,0:T(8,128)(2,1)S(1)}, bf16[16,480]{1,0:T(8,128)(2,1)S(1)}, u32[]{:S(2)}, u32[]{:S(2)}) collective-permute-start(bf16[16,480]{1,0:T(8,128)(2,1)S(1)} %maximum_select_fusion.1), channel_id=1, source_target_pairs={{0,16},{2,18},{4,20},{6,22},{8,24},{10,26},{12,28},{14,30},{16,0},... | collective-permute-start | bytes 46088 | tf_op jit(solution)/shard_map/ppermute | solution.py:933
  63.4 99.2 %collective-permute-start.9 = (bf16[752,1280]{1,0:T(8,128)(2,1)}, bf16[752,1280]{1,0:T(8,128)(2,1)S(1)}, u32[]{:S(2)}, u32[]{:S(2)}) collective-permute-start(bf16[752,1280]{1,0:T(8,128)(2,1)} %bitcast.122), channel_id=1, source_target_pairs={{0,1},{1,0},{2,3},{3,2},{4,5},{5,4},{6,7},{7,6},{8,9},{9,8},{10,11... | collective-permute-start | bytes 5775368 | tf_op jit(solution)/shard_map/ppermute | solution.py:920
  126.3 24.1 %collective-permute-start.7 = (bf16[640,768]{1,0:T(8,128)(2,1)}, bf16[640,768]{1,0:T(8,128)(2,1)S(1)}, u32[]{:S(2)}, u32[]{:S(2)}) collective-permute-start(bf16[640,768]{1,0:T(8,128)(2,1)} %bitcast.125), channel_id=1, source_target_pairs={{0,1},{1,0},{2,3},{3,2},{4,5},{5,4},{6,7},{7,6},{8,9},{9,8},{10,11... | collective-permute-start | bytes 2949128 | tf_op jit(solution)/shard_map/ppermute | solution.py:920
  160.4 43.7 %collective-permute-start.8 = (bf16[752,1280]{1,0:T(8,128)(2,1)}, bf16[752,1280]{1,0:T(8,128)(2,1)}, u32[]{:S(2)}, u32[]{:S(2)}) collective-permute-start(bf16[752,1280]{1,0:T(8,128)(2,1)} %get-tuple-element.116.second_ref.so_ref), channel_id=1, source_target_pairs={{0,1},{1,0},{2,3},{3,2},{4,5},{5,4},{6,7},{7,6},{8,9},{9,8},{10,11... | collective-permute-start | bytes 5775368 | tf_op jit(solution)/shard_map/ppermute | solution.py:920
  162.6 41.5 %copy-start.24 = (bf16[752,1280]{1,0:T(8,128)(2,1)}, bf16[752,1280]{1,0:T(8,128)(2,1)S(1)}, u32[]{:S(2)}) copy-start(bf16[752,1280]{1,0:T(8,128)(2,1)S(1)} %collective-permute-done.9.grad_ref.refs_0_) | copy-start | bytes 5775364
  237.1 45.5 %collective-permute-start.10 = (bf16[752,1280]{1,0:T(8,128)(2,1)}, bf16[752,1280]{1,0:T(8,128)(2,1)S(1)}, u32[]{:S(2)}, u32[]{:S(2)}) collective-permute-start(bf16[752,1280]{1,0:T(8,128)(2,1)} %get-tuple-element.110), channel_id=1, source_target_pairs={{0,1},{1,0},{2,3},{3,2},{4,5},{5,4},{6,7},{7,6},{8,9},{9,8},{10,11... | collective-permute-start | bytes 5775368 | tf_op jit(solution)/shard_map/ppermute | solution.py:920
  282.3 236.4 %reduce-scatter.3.cloned.1.call-start = ((), (), s32[]{:S(2)}) async-start(), calls=%async_computation.4 | async-start | bytes 10444800 | tf_op jit(solution)/shard_map/reduce_scatter | solution.py:1058
  297.2 22.8 %collective-permute-start.11 = (bf16[640,768]{1,0:T(8,128)(2,1)}, bf16[640,768]{1,0:T(8,128)(2,1)S(1)}, u32[]{:S(2)}, u32[]{:S(2)}) collective-permute-start(bf16[640,768]{1,0:T(8,128)(2,1)} %get-tuple-element.114), channel_id=1, source_target_pairs={{0,1},{1,0},{2,3},{3,2},{4,5},{5,4},{6,7},{7,6},{8,9},{9,8},{10,11... | collective-permute-start | bytes 2949128 | tf_op jit(solution)/shard_map/ppermute | solution.py:920
  363.1 3.4 collective-permute-start.12
  363.1 44.7 %collective-permute-start.14 = (bf16[752,1280]{1,0:T(8,128)(2,1)}, bf16[752,1280]{1,0:T(8,128)(2,1)}, u32[]{:S(2)}, u32[]{:S(2)}) collective-permute-start(bf16[752,1280]{1,0:T(8,128)(2,1)} %get-tuple-element.130), channel_id=1, source_target_pairs={{0,1},{1,0},{2,3},{3,2},{4,5},{5,4},{6,7},{7,6},{8,9},{9,8},{10,11... | collective-permute-start | bytes 5775368 | tf_op jit(solution)/shard_map/ppermute | solution.py:920
  369.4 31.8 %collective-permute-start.13 = (bf16[4,80,960]{2,1,0:T(8,128)(2,1)S(1)}, bf16[4,80,960]{2,1,0:T(8,128)(2,1)S(1)}, u32[]{:S(2)}, u32[]{:S(2)}) collective-permute-start(bf16[4,80,960]{2,1,0:T(8,128)(2,1)S(1)} %dynamic-slice_bitcast_fusion.2), channel_id=1, source_target_pairs={{0,4},{2,6},{4,0},{6,2},{8,12},{10,14},{12,8},{14,10},{16,20},{18,... | collective-permute-start | bytes 1843208 | tf_op jit(solution)/shard_map/ppermute | solution.py:956
  370.4 30.8 %copy-start.5 = (bf16[8,80,960]{2,1,0:T(8,128)(2,1)S(1)}, bf16[8,80,960]{2,1,0:T(8,128)(2,1)}, u32[]{:S(2)}) copy-start(bf16[8,80,960]{2,1,0:T(8,128)(2,1)} %copy-done.4) | copy-start | bytes 3686404
  441.4 3.3 collective-permute-start.16
  446.4 25.4 %copy-start.9 = (f32[32,40]{1,0:T(8,128)S(1)}, f32[32,40]{1,0:T(8,128)}, u32[]{:S(2)}) copy-start(f32[32,40]{1,0:T(8,128)} %get-tuple-element.161) | copy-start | bytes 15364
  446.5 22.3 %collective-permute-start.17 = (bf16[4,88,960]{2,1,0:T(8,128)(2,1)S(1)}, bf16[4,88,960]{2,1,0:T(8,128)(2,1)S(1)}, u32[]{:S(2)}, u32[]{:S(2)}) collective-permute-start(bf16[4,88,960]{2,1,0:T(8,128)(2,1)S(1)} %dynamic-slice_bitcast_fusion.1), channel_id=1, source_target_pairs={{0,4},{2,6},{4,0},{6,2},{8,12},{10,14},{12,8},{14,10},{16,20},{18,... | collective-permute-start | bytes 2027528 | tf_op jit(solution)/shard_map/ppermute | solution.py:956
  447.2 62.9 %collective-permute-start.19 = (bf16[752,1280]{1,0:T(8,128)(2,1)}, bf16[752,1280]{1,0:T(8,128)(2,1)}, u32[]{:S(2)}, u32[]{:S(2)}) collective-permute-start(bf16[752,1280]{1,0:T(8,128)(2,1)} %get-tuple-element.153), channel_id=1, source_target_pairs={{0,1},{1,0},{2,3},{3,2},{4,5},{5,4},{6,7},{7,6},{8,9},{9,8},{10,11... | collective-permute-start | bytes 5775368 | tf_op jit(solution)/shard_map/ppermute | solution.py:920
  449.6 22.4 %collective-permute-start.15 = (bf16[1,160,960]{2,1,0:T(8,128)(2,1)}, bf16[1,160,960]{2,1,0:T(8,128)(2,1)}, u32[]{:S(2)}, u32[]{:S(2)}) collective-permute-start(bf16[1,160,960]{2,1,0:T(8,128)(2,1)} %dynamic-slice_bitcast_fusion.4), channel_id=1, source_target_pairs={{0,16},{2,18},{4,20},{6,22},{8,24},{10,26},{12,28},{14,30},{16,0},... | collective-permute-start | bytes 921608 | tf_op jit(solution)/shard_map/ppermute | solution.py:956
  470.1 35.4 %copy-start.6 = (bf16[752,1280]{1,0:T(8,128)(2,1)S(1)}, bf16[752,1280]{1,0:T(8,128)(2,1)}, u32[]{:S(2)}) copy-start(bf16[752,1280]{1,0:T(8,128)(2,1)} %get-tuple-element.148) | copy-start | bytes 5775364
  470.9 33.4 %collective-permute-start.18 = (bf16[1,176,960]{2,1,0:T(8,128)(2,1)}, bf16[1,176,960]{2,1,0:T(8,128)(2,1)}, u32[]{:S(2)}, u32[]{:S(2)}) collective-permute-start(bf16[1,176,960]{2,1,0:T(8,128)(2,1)} %dynamic-slice_bitcast_fusion.3), channel_id=1, source_target_pairs={{0,16},{2,18},{4,20},{6,22},{8,24},{10,26},{12,28},{14,30},{16,0},... | collective-permute-start | bytes 1013768 | tf_op jit(solution)/shard_map/ppermute | solution.py:956
  505.4 11.2 %collective-permute-start.20 = (bf16[1,80,960]{2,1,0:T(8,128)(2,1)S(1)}, bf16[1,80,960]{2,1,0:T(8,128)(2,1)S(1)}, u32[]{:S(2)}, u32[]{:S(2)}) collective-permute-start(bf16[1,80,960]{2,1,0:T(8,128)(2,1)S(1)} %dynamic-slice_bitcast_fusion.6), channel_id=1, source_target_pairs={{0,8},{2,10},{4,12},{6,14},{8,0},{10,2},{12,4},{14,6},{16,24},{18,... | collective-permute-start | bytes 460808 | tf_op jit(solution)/shard_map/ppermute | solution.py:956
  521.6 4.7 collective-permute-start.22
  523.1 6.2 %collective-permute-start.21 = (bf16[1,88,960]{2,1,0:T(8,128)(2,1)S(1)}, bf16[1,88,960]{2,1,0:T(8,128)(2,1)S(1)}, u32[]{:S(2)}, u32[]{:S(2)}) collective-permute-start(bf16[1,88,960]{2,1,0:T(8,128)(2,1)S(1)} %dynamic-slice_bitcast_fusion.5), channel_id=1, source_target_pairs={{0,8},{2,10},{4,12},{6,14},{8,0},{10,2},{12,4},{14,6},{16,24},{18,... | collective-permute-start | bytes 506888 | tf_op jit(solution)/shard_map/ppermute | solution.py:956
  530.1 3.7 collective-permute-start.23
  (25 other events, 159.8 us)
Sparse Core Ops, SparseCore 0:
  15.1 74.9 all-gather.2
  93.0 102.2 all-gather.4
  282.5 84.9 reduce-scatter.4
  372.0 132.7 reduce-scatter.2

commit v6 on v5

--- a/solution.py
+++ b/solution.py
@@ -454,7 +454,7 @@
 
 def attend_rows(queries, keys_own, keys_far, values_own, values_far):
     heads, rows, _ = queries.shape
-    per_step = 2 if heads % 2 == 0 else 1
+    per_step = 4 if heads % 4 == 0 else 1
     spec = pl.BlockSpec((per_step, rows, PAD), lambda h: (h, 0, 0))
     return pl.pallas_call(
         attend_kernel,

time: 551 us -> 555 us (level)
  Pallas kernels: 279 us -> 289 us
    pallas_call x2, Pallas kernels: 30.8 us -> 41.6 us  [attend_rows(): pl.pallas_call(attend_kernel, out_shape=(jax.ShapeDtypeStruct((heads, HD,...]
    ppermute x12, waiting for transfers between devices: 80.2 us -> 74.3 us  [swap_tp(): return lax.ppermute(piece, 'tp', [(0, 1), (1, 0)])]
  transfers between devices with their start and end apart: 28 -> 28, of which waited for: 16 -> 15; matrix products, arithmetic and copies ran while one was open for 8% -> 8% of each run, Pallas kernels for 45% -> 47%
where the time goes in v6:
time: 555 us; the launch traced here: 545 us
  Pallas kernels  289 us (52%)
  waiting for transfers between devices  163 us (29%)
  other arithmetic  26.7 us (5%)
  starting transfers between devices  26.2 us (5%)
  local copies, waits for them, and re-layouts  25.9 us (5%)
  between operations  14.9 us (3%)
    pallas_call x2, Pallas kernels, feed(): pl.pallas_call(functools.partial(feed_kernel, far is not None), out_shape...  76.2 us
    ppermute x12, waiting for transfers between devices, swap_tp(): return lax.ppermute(piece, 'tp', [(0, 1), (1, 0)])  74.3 us
    pallas_call x2, Pallas kernels, attend_back_rows(): pl.pallas_call(attend_back_kernel, out_shape=(jax.ShapeDtypeStruct(packed...  61.3 us
    ppermute x8, waiting for transfers between devices, halve(): lax.ppermute(chosen(1 - mine), 'fsdp', [(i, i ^ bit) for i in range(fsdp)])  56.2 us
    pallas_call x2, Pallas kernels, attend_rows(): pl.pallas_call(attend_kernel, out_shape=(jax.ShapeDtypeStruct((heads, HD,...  41.6 us
    all_gather x1, waiting for transfers between devices, per_device_pair(): lax.all_gather(jnp.concatenate([w_query, w_key, w_value, out_turned, out_...  26.4 us
    pallas_call x1, Pallas kernels, side_grads(): pl.pallas_call(side_grad_kernel, out_shape=jax.ShapeDtypeStruct((width, u...  22.5 us
    pallas_call x2, Pallas kernels, project(): pl.pallas_call(functools.partial(project_kernel, heads), out_shape=(jax.S...  20.6 us
  transfers between devices with their start and end apart: 28, of which 15 were waited for; matrix products, arithmetic and copies ran while one was open for 8% of the time, Pallas kernels for 47%

profile of v6, /device:TPU:0, one launch (start us, length us, event | category | flops | bytes accessed | tf_op | source)
XLA Modules:
  0.0 545.4 jit_solution(4730588513192670448)
XLA Ops:
  7.2 3.0 collective-permute-start.1
  15.1 2.1 pad_maximum_fusion
  18.4 2.6 collective-permute-done
  31.0 2.5 collective-permute-start.5
  42.3 21.1 %collective-permute-done.6.frames_ref.refs_3_ = bf16[752,1280]{1,0:T(8,128)(2,1)} collective-permute-done((bf16[752,1280]{1,0:T(8,128)(2,1)S(1)}, bf16[752,1280]{1,0:T(8,128)(2,1)}, u32[]{:S(2)}, u32[]{:S(2)}) %collective-permute-start.6) | collective-permute-done | bytes 1925152 | tf_op jit(solution)/shard_map/ppermute | solution.py:920
  63.7 26.4 %all-gather.3.cloned.1.call-done.weight_ref.wo_ref.wt_ref.refs_2_ = bf16[1280,3200]{1,0:T(8,128)(2,1)} async-done(((bf16[80,3200]{1,0:T(8,128)(2,1)}), bf16[1280,3200]{1,0:T(8,128)(2,1)}) %all-gather.3.cloned.1.call-update) | async-done | bytes 8192016 | tf_op jit(solution)/shard_map/all_gather | solution.py:985
  90.1 10.3 %project.2 = (bf16[752,1280]{1,0:T(8,128)(2,1)}, bf16[8,752,128]{2,1,0:T(8,128)(2,1)}, bf16[8,752,128]{2,1,0:T(8,128)(2,1)}, bf16[8,752,128]{2,1,0:T(8,128)(2,1)}) custom-call(s32[2]{0:T(128)} %get-tuple-element.189.scal_ref, bf16[752,1280]{1,0:T(8,128)(2,1)} %bitcast.91, f32[1,1280]{1,0:T(1,128)} %squeeze.80.gain_ref, f32[1,1280]{1,0:T(1,128)} %squeeze.81.shift_ref, ...), custom_call_target="tpu_custom_call" | custom-call | flops 11088691200 | bytes 8765440 | tf_op jit(solution)/shard_map/project/pallas_call | solution.py:408
  100.4 10.3 %project.3 = (bf16[752,1280]{1,0:T(8,128)(2,1)}, bf16[8,752,128]{2,1,0:T(8,128)(2,1)}, bf16[8,752,128]{2,1,0:T(8,128)(2,1)}, bf16[8,752,128]{2,1,0:T(8,128)(2,1)}) custom-call(s32[2]{0:T(128)} %get-tuple-element.190.scal_ref, bf16[752,1280]{1,0:T(8,128)(2,1)} %collective-permute-done.6.frames_ref.refs_3_, f32[1,1280]{1,0:T(1,128)} %squeeze.80.gain_ref, ...), custom_call_target="tpu_custom_call" | custom-call | flops 11088691200 | bytes 8765440 | tf_op jit(solution)/shard_map/project/pallas_call | solution.py:408
  110.7 15.7 %attend.2 = (bf16[8,80,768]{2,1,0:T(8,128)(2,1)}, f32[8,1,752]{2,1,0:T(1,128)}) custom-call(bf16[8,752,128]{2,1,0:T(8,128)(2,1)} %get-tuple-element.94.q_ref.qt_ref, bf16[8,752,128]{2,1,0:T(8,128)(2,1)} %get-tuple-element.95.ko_ref, bf16[8,752,128]{2,1,0:T(8,128)(2,1)} %get-tuple-element.96.kt_ref, bf16[8,752,128]{2,1,0:T(8,128)(2,1)} %get-tuple-element.97.vo_ref, ...), custom_call_target="tpu_custom_call" | custom-call | flops 43430707200 | bytes 9240576 | tf_op jit(solution)/shard_map/attend/pallas_call | solution.py:459
  127.9 25.9 %attend.3 = (bf16[8,80,768]{2,1,0:T(8,128)(2,1)}, f32[8,1,752]{2,1,0:T(1,128)}) custom-call(bf16[8,752,128]{2,1,0:T(8,128)(2,1)} %get-tuple-element.128.q_ref.qo_ref, bf16[8,752,128]{2,1,0:T(8,128)(2,1)} %get-tuple-element.95.ko_ref, bf16[8,752,128]{2,1,0:T(8,128)(2,1)} %get-tuple-element.96.kt_ref, bf16[8,752,128]{2,1,0:T(8,128)(2,1)} %get-tuple-element.97.vo_ref, ...), custom_call_target="tpu_custom_call" | custom-call | flops 43430707200 | bytes 9240576 | tf_op jit(solution)/shard_map/attend/pallas_call | solution.py:459
  154.8 9.2 %merge_heads.1 = (f32[752,1280]{1,0:T(8,128)}, bf16[752,1280]{1,0:T(8,128)(2,1)}) custom-call(bf16[640,768]{1,0:T(8,128)(2,1)} %bitcast.126, bf16[640,768]{1,0:T(8,128)(2,1)} %copy-done.26, bf16[1280,3200]{1,0:T(8,128)(2,1)} %all-gather.3.cloned.1.call-done.weight_ref.wo_ref.wt_ref.refs_2_, ...), custom_call_target="tpu_custom_call" | custom-call | flops 7392460800 | bytes 12902400 | tf_op jit(solution)/shard_map/merge_heads/pallas_call | solution.py:583
  165.3 42.8 %collective-permute-done.8.second_ref.st_ref = bf16[752,1280]{1,0:T(8,128)(2,1)} collective-permute-done((bf16[752,1280]{1,0:T(8,128)(2,1)}, bf16[752,1280]{1,0:T(8,128)(2,1)}, u32[]{:S(2)}, u32[]{:S(2)}) %collective-permute-start.8) | collective-permute-done | bytes 1925152 | tf_op jit(solution)/shard_map/ppermute | solution.py:920
  208.1 32.5 %feed.1 = (bf16[752,2560]{1,0:T(8,128)(2,1)}, bf16[752,2560]{1,0:T(8,128)(2,1)}, f32[1,2560]{1,0:T(1,128)}, bf16[752,1280]{1,0:T(8,128)(2,1)}, bf16[752,1280]{1,0:T(8,128)(2,1)}) custom-call(bf16[752,1280]{1,0:T(8,128)(2,1)} %collective-permute-done.8.second_ref.st_ref, bf16[752,1280]{1,0:T(8,128)(2,1)} %copy-done.24, ...), custom_call_target="tpu_custom_call" | custom-call | flops 59139686400 | bytes 36208640 | tf_op jit(solution)/shard_map/feed/pallas_call | solution.py:675
  241.3 43.7 %feed_last.1 = (bf16[752,2560]{1,0:T(8,128)(2,1)}, f32[1,2560]{1,0:T(1,128)}, bf16[752,1280]{1,0:T(8,128)(2,1)}, bf16[752,1280]{1,0:T(8,128)(2,1)}, bf16[1280,2560]{1,0:T(8,128)(2,1)}) custom-call(bf16[752,1280]{1,0:T(8,128)(2,1)} %get-tuple-element.116.second_ref.so_ref, bf16[752,1280]{1,0:T(8,128)(2,1)} %bitcast.123, ...), custom_call_target="tpu_custom_call" | custom-call | flops 88709529600 | bytes 36208640 | tf_op jit(solution)/shard_map/feed_last/pallas_call | solution.py:675
  286.8 13.2 %branch_back.1 = (f32[752,1280]{1,0:T(8,128)}, bf16[752,1280]{1,0:T(8,128)(2,1)}, bf16[640,768]{1,0:T(8,128)(2,1)}, bf16[640,768]{1,0:T(8,128)(2,1)}, f32[4,1280]{1,0:T(4,128)}) custom-call(bf16[752,1280]{1,0:T(8,128)(2,1)} %get-tuple-element.109.own_ref, bf16[752,1280]{1,0:T(8,128)(2,1)} %copy-done.25, f32[752,1280]{1,0:T(8,128)} %get-tuple-element.111.middle_ref, ...), custom_call_target="tpu_custom_call" | custom-call | flops 7392460800 | bytes 17326080 | tf_op jit(solution)/shard_map/branch_back/pallas_call | solution.py:772
  301.3 22.5 %side_grads.1 = bf16[1280,3840]{1,0:T(8,128)(2,1)} custom-call(bf16[752,1280]{1,0:T(8,128)(2,1)} %get-tuple-element.116.second_ref.so_ref, bf16[752,1280]{1,0:T(8,128)(2,1)} %collective-permute-done.8.second_ref.st_ref, bf16[752,2560]{1,0:T(8,128)(2,1)} %get-tuple-element.117.bo_ref, bf16[752,2560]{1,0:T(8,128)(2,1)} %get-tuple-element.118.bt_ref, ...), custom_call_target="tpu_custom_call" | custom-call | flops 36962304000 | bytes 11550720 | tf_op jit(solution)/shard_map/side_grads/pallas_call | solution.py:817
  324.8 30.6 %attend_back.2 = (bf16[752,960]{1,0:T(8,128)(2,1)}, bf16[752,960]{1,0:T(8,128)(2,1)}) custom-call(bf16[8,752,128]{2,1,0:T(8,128)(2,1)} %get-tuple-element.128.q_ref.qo_ref, bf16[8,752,128]{2,1,0:T(8,128)(2,1)} %get-tuple-element.94.q_ref.qt_ref, bf16[8,752,128]{2,1,0:T(8,128)(2,1)} %get-tuple-element.95.ko_ref, ...), custom_call_target="tpu_custom_call" | custom-call | flops 130292121600 | bytes 9240576 | tf_op jit(solution)/shard_map/attend_back/pallas_call | solution.py:542
  355.5 8.7 %head_grad.2 = bf16[1280,960]{1,0:T(8,128)(2,1)} custom-call(bf16[752,1280]{1,0:T(8,128)(2,1)} %get-tuple-element.90.lo_ref, bf16[752,1280]{1,0:T(8,128)(2,1)} %get-tuple-element.93.lt_ref, bf16[752,960]{1,0:T(8,128)(2,1)} %get-tuple-element.125.refs_0_, bf16[752,960]{1,0:T(8,128)(2,1)} %get-tuple-element.126.refs_1_.refs_0_), custom_call_target="tpu_custom_call" | custom-call | flops 73924608 | bytes 183910 | tf_op jit(solution)/shard_map/head_grad/pallas_call | solution.py:705
  364.2 2.7 dynamic-slice_bitcast_fusion
  367.6 2.6 collective-permute-done.12
  374.0 30.7 %attend_back.3 = (bf16[752,960]{1,0:T(8,128)(2,1)}, bf16[752,960]{1,0:T(8,128)(2,1)}) custom-call(bf16[8,752,128]{2,1,0:T(8,128)(2,1)} %get-tuple-element.128.q_ref.qo_ref, bf16[8,752,128]{2,1,0:T(8,128)(2,1)} %get-tuple-element.94.q_ref.qt_ref, bf16[8,752,128]{2,1,0:T(8,128)(2,1)} %get-tuple-element.95.ko_ref, ...), custom_call_target="tpu_custom_call" | custom-call | flops 325730304 | bytes 184811 | tf_op jit(solution)/shard_map/attend_back/pallas_call | solution.py:542
  405.0 6.5 %collective-permute-done.14 = bf16[752,1280]{1,0:T(8,128)(2,1)} collective-permute-done((bf16[752,1280]{1,0:T(8,128)(2,1)}, bf16[752,1280]{1,0:T(8,128)(2,1)}, u32[]{:S(2)}, u32[]{:S(2)}) %collective-permute-start.14) | collective-permute-done | bytes 1925152 | tf_op jit(solution)/shard_map/ppermute | solution.py:920
  411.5 10.1 %first_back.2 = (bf16[752,1280]{1,0:T(8,128)(2,1)}, f32[2,1280]{1,0:T(2,128)}, f32[1,1920]{1,0:T(1,128)}) custom-call(bf16[752,960]{1,0:T(8,128)(2,1)} %get-tuple-element.126.refs_1_.refs_0_, bf16[752,960]{1,0:T(8,128)(2,1)} %get-tuple-element.136.refs_1_, bf16[1280,3200]{1,0:T(8,128)(2,1)} %all-gather.3.cloned.1.call-done.weight_ref.wo_ref.wt_ref.refs_2_, ...), custom_call_target="tpu_custom_call" | custom-call | flops 73924608 | bytes 233062 | tf_op jit(solution)/shard_map/first_back/pallas_call | solution.py:872
  421.6 8.9 %head_grad.3 = bf16[1280,960]{1,0:T(8,128)(2,1)} custom-call(bf16[752,1280]{1,0:T(8,128)(2,1)} %get-tuple-element.90.lo_ref, bf16[752,1280]{1,0:T(8,128)(2,1)} %get-tuple-element.93.lt_ref, bf16[752,960]{1,0:T(8,128)(2,1)} %get-tuple-element.138.refs_0_.refs_1_, bf16[752,960]{1,0:T(8,128)(2,1)} %get-tuple-element.136.refs_1_), custom_call_target="tpu_custom_call" | custom-call | flops 73924608 | bytes 183910 | tf_op jit(solution)/shard_map/head_grad/pallas_call | solution.py:705
  430.6 10.4 %first_back.3 = (bf16[752,1280]{1,0:T(8,128)(2,1)}, f32[2,1280]{1,0:T(2,128)}, f32[1,1920]{1,0:T(1,128)}) custom-call(bf16[752,960]{1,0:T(8,128)(2,1)} %get-tuple-element.125.refs_0_, bf16[752,960]{1,0:T(8,128)(2,1)} %get-tuple-element.138.refs_0_.refs_1_, bf16[1280,3200]{1,0:T(8,128)(2,1)} %all-gather.3.cloned.1.call-done.weight_ref.wo_ref.wt_ref.refs_2_, ...), custom_call_target="tpu_custom_call" | custom-call | flops 73924608 | bytes 233062 | tf_op jit(solution)/shard_map/first_back/pallas_call | solution.py:872
  445.2 3.2 collective-permute-done.16
  452.4 2.0 collective-permute-start.15
  454.3 17.5 %collective-permute-done.17 = bf16[4,88,960]{2,1,0:T(8,128)(2,1)S(1)} collective-permute-done((bf16[4,88,960]{2,1,0:T(8,128)(2,1)S(1)}, bf16[4,88,960]{2,1,0:T(8,128)(2,1)S(1)}, u32[]{:S(2)}, u32[]{:S(2)}) %collective-permute-start.17) | collective-permute-done | bytes 675872 | tf_op jit(solution)/shard_map/ppermute | solution.py:956
  476.6 31.6 %collective-permute-done.18 = bf16[1,176,960]{2,1,0:T(8,128)(2,1)} collective-permute-done((bf16[1,176,960]{2,1,0:T(8,128)(2,1)}, bf16[1,176,960]{2,1,0:T(8,128)(2,1)}, u32[]{:S(2)}, u32[]{:S(2)}) %collective-permute-start.18) | collective-permute-done | bytes 337952 | tf_op jit(solution)/shard_map/ppermute | solution.py:956
  509.4 4.6 add_convert_fusion
  514.1 6.5 %frames_back.1 = bf16[752,1280]{1,0:T(8,128)(2,1)} custom-call(bf16[752,1280]{1,0:T(8,128)(2,1)} %bitcast.94, bf16[752,1280]{1,0:T(8,128)(2,1)} %get-tuple-element.152.own_ref, bf16[752,1280]{1,0:T(8,128)(2,1)} %collective-permute-done.19.far_ref, f32[752,1280]{1,0:T(8,128)} %get-tuple-element.154.mgrad_ref, f32[1,1280]{1,0:T(1,128)} %squeeze.80.gain_ref), custom_call_target="tpu_custom_call" | custom-call | flops 385024 | bytes 231014 | tf_op jit(solution)/shard_map/frames_back/pallas_call | solution.py:907
  527.0 2.1 collective-permute-start.21
  (186 shorter events, 68.0 us)
Async XLA Ops:
  7.2 82.9 %all-gather.3.cloned.1.call-start = ((), (), s32[]{:S(2)}) async-start(), calls=%async_computation.2 | async-start | bytes 8704000 | tf_op jit(solution)/shard_map/all_gather | solution.py:985
  7.2 6.9 %collective-permute-start.1 = (bf16[80,640]{1,0:T(8,128)(2,1)}, bf16[80,640]{1,0:T(8,128)(2,1)S(1)}, u32[]{:S(2)}, u32[]{:S(2)}) collective-permute-start(bf16[80,640]{1,0:T(8,128)(2,1)} %bitcast.119), channel_id=1, source_target_pairs={{0,1},{1,0},{2,3},{3,2},{4,5},{5,4},{6,7},{7,6},{8,9},{9,8},{10,11... | collective-permute-start | bytes 307208 | tf_op jit(solution)/shard_map/ppermute | solution.py:920
  15.0 193.1 %all-gather.5.cloned.1.call-start = ((), (), s32[]{:S(2)}) async-start(), calls=%async_computation.3 | async-start | bytes 13926400 | tf_op jit(solution)/shard_map/all_gather | solution.py:989
  17.2 503.5 %reduce-scatter.5.cloned.1.call-start = ((), (), s32[]{:S(2)}) async-start(), calls=%async_computation.5 | async-start | bytes 6963200 | tf_op jit(solution)/shard_map/reduce_scatter | solution.py:1033
  17.4 3.6 collective-permute-start
  21.0 42.4 %collective-permute-start.6 = (bf16[752,1280]{1,0:T(8,128)(2,1)S(1)}, bf16[752,1280]{1,0:T(8,128)(2,1)}, u32[]{:S(2)}, u32[]{:S(2)}) collective-permute-start(bf16[752,1280]{1,0:T(8,128)(2,1)S(1)} %bitcast.95), channel_id=1, source_target_pairs={{0,1},{1,0},{2,3},{3,2},{4,5},{5,4},{6,7},{7,6},{8,9},{9,8},{10,11... | collective-permute-start | bytes 5775368 | tf_op jit(solution)/shard_map/ppermute | solution.py:920
  22.0 1.2 collective-permute-start.2
  23.2 3.7 collective-permute-start.3
  26.9 4.0 collective-permute-start.4
  31.0 5.5 %collective-permute-start.5 = (bf16[16,480]{1,0:T(8,128)(2,1)S(1)}, bf16[16,480]{1,0:T(8,128)(2,1)S(1)}, u32[]{:S(2)}, u32[]{:S(2)}) collective-permute-start(bf16[16,480]{1,0:T(8,128)(2,1)S(1)} %maximum_select_fusion.1), channel_id=1, source_target_pairs={{0,16},{2,18},{4,20},{6,22},{8,24},{10,26},{12,28},{14,30},{16,0},... | collective-permute-start | bytes 46088 | tf_op jit(solution)/shard_map/ppermute | solution.py:933
  63.4 101.9 %collective-permute-start.9 = (bf16[752,1280]{1,0:T(8,128)(2,1)}, bf16[752,1280]{1,0:T(8,128)(2,1)S(1)}, u32[]{:S(2)}, u32[]{:S(2)}) collective-permute-start(bf16[752,1280]{1,0:T(8,128)(2,1)} %bitcast.122), channel_id=1, source_target_pairs={{0,1},{1,0},{2,3},{3,2},{4,5},{5,4},{6,7},{7,6},{8,9},{9,8},{10,11... | collective-permute-start | bytes 5775368 | tf_op jit(solution)/shard_map/ppermute | solution.py:920
  126.4 27.4 %collective-permute-start.7 = (bf16[640,768]{1,0:T(8,128)(2,1)}, bf16[640,768]{1,0:T(8,128)(2,1)S(1)}, u32[]{:S(2)}, u32[]{:S(2)}) collective-permute-start(bf16[640,768]{1,0:T(8,128)(2,1)} %bitcast.125), channel_id=1, source_target_pairs={{0,1},{1,0},{2,3},{3,2},{4,5},{5,4},{6,7},{7,6},{8,9},{9,8},{10,11... | collective-permute-start | bytes 2949128 | tf_op jit(solution)/shard_map/ppermute | solution.py:920
  164.0 44.1 %collective-permute-start.8 = (bf16[752,1280]{1,0:T(8,128)(2,1)}, bf16[752,1280]{1,0:T(8,128)(2,1)}, u32[]{:S(2)}, u32[]{:S(2)}) collective-permute-start(bf16[752,1280]{1,0:T(8,128)(2,1)} %get-tuple-element.116.second_ref.so_ref), channel_id=1, source_target_pairs={{0,1},{1,0},{2,3},{3,2},{4,5},{5,4},{6,7},{7,6},{8,9},{9,8},{10,11... | collective-permute-start | bytes 5775368 | tf_op jit(solution)/shard_map/ppermute | solution.py:920
  165.3 42.8 %copy-start.24 = (bf16[752,1280]{1,0:T(8,128)(2,1)}, bf16[752,1280]{1,0:T(8,128)(2,1)S(1)}, u32[]{:S(2)}) copy-start(bf16[752,1280]{1,0:T(8,128)(2,1)S(1)} %collective-permute-done.9.grad_ref.refs_0_) | copy-start | bytes 5775364
  240.6 44.9 %collective-permute-start.10 = (bf16[752,1280]{1,0:T(8,128)(2,1)}, bf16[752,1280]{1,0:T(8,128)(2,1)S(1)}, u32[]{:S(2)}, u32[]{:S(2)}) collective-permute-start(bf16[752,1280]{1,0:T(8,128)(2,1)} %get-tuple-element.110), channel_id=1, source_target_pairs={{0,1},{1,0},{2,3},{3,2},{4,5},{5,4},{6,7},{7,6},{8,9},{9,8},{10,11... | collective-permute-start | bytes 5775368 | tf_op jit(solution)/shard_map/ppermute | solution.py:920
  285.0 237.6 %reduce-scatter.3.cloned.1.call-start = ((), (), s32[]{:S(2)}) async-start(), calls=%async_computation.4 | async-start | bytes 10444800 | tf_op jit(solution)/shard_map/reduce_scatter | solution.py:1058
  300.0 23.9 %collective-permute-start.11 = (bf16[640,768]{1,0:T(8,128)(2,1)}, bf16[640,768]{1,0:T(8,128)(2,1)S(1)}, u32[]{:S(2)}, u32[]{:S(2)}) collective-permute-start(bf16[640,768]{1,0:T(8,128)(2,1)} %get-tuple-element.114), channel_id=1, source_target_pairs={{0,1},{1,0},{2,3},{3,2},{4,5},{5,4},{6,7},{7,6},{8,9},{9,8},{10,11... | collective-permute-start | bytes 2949128 | tf_op jit(solution)/shard_map/ppermute | solution.py:920
  366.8 3.4 collective-permute-start.12
  366.8 44.7 %collective-permute-start.14 = (bf16[752,1280]{1,0:T(8,128)(2,1)}, bf16[752,1280]{1,0:T(8,128)(2,1)}, u32[]{:S(2)}, u32[]{:S(2)}) collective-permute-start(bf16[752,1280]{1,0:T(8,128)(2,1)} %get-tuple-element.130), channel_id=1, source_target_pairs={{0,1},{1,0},{2,3},{3,2},{4,5},{5,4},{6,7},{7,6},{8,9},{9,8},{10,11... | collective-permute-start | bytes 5775368 | tf_op jit(solution)/shard_map/ppermute | solution.py:920
  373.1 31.6 %collective-permute-start.13 = (bf16[4,80,960]{2,1,0:T(8,128)(2,1)S(1)}, bf16[4,80,960]{2,1,0:T(8,128)(2,1)S(1)}, u32[]{:S(2)}, u32[]{:S(2)}) collective-permute-start(bf16[4,80,960]{2,1,0:T(8,128)(2,1)S(1)} %dynamic-slice_bitcast_fusion.2), channel_id=1, source_target_pairs={{0,4},{2,6},{4,0},{6,2},{8,12},{10,14},{12,8},{14,10},{16,20},{18,... | collective-permute-start | bytes 1843208 | tf_op jit(solution)/shard_map/ppermute | solution.py:956
  374.0 30.7 %copy-start.5 = (bf16[8,80,960]{2,1,0:T(8,128)(2,1)S(1)}, bf16[8,80,960]{2,1,0:T(8,128)(2,1)}, u32[]{:S(2)}) copy-start(bf16[8,80,960]{2,1,0:T(8,128)(2,1)} %copy-done.4) | copy-start | bytes 3686404
  445.2 3.3 collective-permute-start.16
  450.2 25.2 %copy-start.9 = (f32[32,40]{1,0:T(8,128)S(1)}, f32[32,40]{1,0:T(8,128)}, u32[]{:S(2)}) copy-start(f32[32,40]{1,0:T(8,128)} %get-tuple-element.161) | copy-start | bytes 15364
  450.2 21.6 %collective-permute-start.17 = (bf16[4,88,960]{2,1,0:T(8,128)(2,1)S(1)}, bf16[4,88,960]{2,1,0:T(8,128)(2,1)S(1)}, u32[]{:S(2)}, u32[]{:S(2)}) collective-permute-start(bf16[4,88,960]{2,1,0:T(8,128)(2,1)S(1)} %dynamic-slice_bitcast_fusion.1), channel_id=1, source_target_pairs={{0,4},{2,6},{4,0},{6,2},{8,12},{10,14},{12,8},{14,10},{16,20},{18,... | collective-permute-start | bytes 2027528 | tf_op jit(solution)/shard_map/ppermute | solution.py:956
  450.9 63.1 %collective-permute-start.19 = (bf16[752,1280]{1,0:T(8,128)(2,1)}, bf16[752,1280]{1,0:T(8,128)(2,1)}, u32[]{:S(2)}, u32[]{:S(2)}) collective-permute-start(bf16[752,1280]{1,0:T(8,128)(2,1)} %get-tuple-element.153), channel_id=1, source_target_pairs={{0,1},{1,0},{2,3},{3,2},{4,5},{5,4},{6,7},{7,6},{8,9},{9,8},{10,11... | collective-permute-start | bytes 5775368 | tf_op jit(solution)/shard_map/ppermute | solution.py:920
  452.4 23.2 %collective-permute-start.15 = (bf16[1,160,960]{2,1,0:T(8,128)(2,1)}, bf16[1,160,960]{2,1,0:T(8,128)(2,1)}, u32[]{:S(2)}, u32[]{:S(2)}) collective-permute-start(bf16[1,160,960]{2,1,0:T(8,128)(2,1)} %dynamic-slice_bitcast_fusion.4), channel_id=1, source_target_pairs={{0,16},{2,18},{4,20},{6,22},{8,24},{10,26},{12,28},{14,30},{16,0},... | collective-permute-start | bytes 921608 | tf_op jit(solution)/shard_map/ppermute | solution.py:956
  473.2 36.2 %copy-start.6 = (bf16[752,1280]{1,0:T(8,128)(2,1)S(1)}, bf16[752,1280]{1,0:T(8,128)(2,1)}, u32[]{:S(2)}) copy-start(bf16[752,1280]{1,0:T(8,128)(2,1)} %get-tuple-element.148) | copy-start | bytes 5775364
  474.0 34.2 %collective-permute-start.18 = (bf16[1,176,960]{2,1,0:T(8,128)(2,1)}, bf16[1,176,960]{2,1,0:T(8,128)(2,1)}, u32[]{:S(2)}, u32[]{:S(2)}) collective-permute-start(bf16[1,176,960]{2,1,0:T(8,128)(2,1)} %dynamic-slice_bitcast_fusion.3), channel_id=1, source_target_pairs={{0,16},{2,18},{4,20},{6,22},{8,24},{10,26},{12,28},{14,30},{16,0},... | collective-permute-start | bytes 1013768 | tf_op jit(solution)/shard_map/ppermute | solution.py:956
  509.3 11.2 %collective-permute-start.20 = (bf16[1,80,960]{2,1,0:T(8,128)(2,1)S(1)}, bf16[1,80,960]{2,1,0:T(8,128)(2,1)S(1)}, u32[]{:S(2)}, u32[]{:S(2)}) collective-permute-start(bf16[1,80,960]{2,1,0:T(8,128)(2,1)S(1)} %dynamic-slice_bitcast_fusion.6), channel_id=1, source_target_pairs={{0,8},{2,10},{4,12},{6,14},{8,0},{10,2},{12,4},{14,6},{16,24},{18,... | collective-permute-start | bytes 460808 | tf_op jit(solution)/shard_map/ppermute | solution.py:956
  525.5 4.8 collective-permute-start.22
  527.0 6.3 %collective-permute-start.21 = (bf16[1,88,960]{2,1,0:T(8,128)(2,1)S(1)}, bf16[1,88,960]{2,1,0:T(8,128)(2,1)S(1)}, u32[]{:S(2)}, u32[]{:S(2)}) collective-permute-start(bf16[1,88,960]{2,1,0:T(8,128)(2,1)S(1)} %dynamic-slice_bitcast_fusion.5), channel_id=1, source_target_pairs={{0,8},{2,10},{4,12},{6,14},{8,0},{10,2},{12,4},{14,6},{16,24},{18,... | collective-permute-start | bytes 506888 | tf_op jit(solution)/shard_map/ppermute | solution.py:956
  534.2 3.7 collective-permute-start.23
  (25 other events, 162.6 us)
Sparse Core Ops, SparseCore 0:
  15.1 74.9 all-gather.2
  93.0 102.2 all-gather.4
  285.2 85.7 reduce-scatter.4
  375.5 133.4 reduce-scatter.2
